TPU v7x, 32 devices: a whole 2x2x4 slice. The times are simulated.
32 devices in a mesh: dp: 8 (over z, y), fsdp: 4 (over x, core).
Axes of the slice: x: 2, y: 2, z: 4, core: 2. Of those that a mesh axis runs over, the one named last changes fastest.
Arguments:
- tokens: bfloat16 [32768, 512], P(('dp', 'fsdp')), may hold values from -6 to 6
- cotangent: bfloat16 [32768, 512], P(('dp', 'fsdp')), may hold values from -6 to 6
- group_id: int32 [32], P(('dp', 'fsdp')), may hold values from 0 to 3
- w_qkv: bfloat16 [512, 1536], P(('dp', 'fsdp')), may hold values from -0.25 to 0.25
- w_out: bfloat16 [512, 512], P(('dp', 'fsdp')), may hold values from -1 to 1
- w_ffn_in: bfloat16 [512, 2048], P(('dp', 'fsdp')), may hold values from -0.25 to 0.25
- w_ffn_out: bfloat16 [2048, 512], P(('dp', 'fsdp')), may hold values from -0.125 to 0.125
- gain_one: bfloat16 [512], P(('dp', 'fsdp')), may hold values from 0.5 to 1.5
- shift_one: bfloat16 [512], P(('dp', 'fsdp')), may hold values from -1.5 to 1.5
- gain_two: bfloat16 [512], P(('dp', 'fsdp')), may hold values from 0.5 to 1.5
- shift_two: bfloat16 [512], P(('dp', 'fsdp')), may hold values from -1.5 to 1.5
- bias_in: bfloat16 [2048], P(('dp', 'fsdp')), may hold values from -2.5 to 2.5
- bias_out: bfloat16 [512], P(('dp', 'fsdp')), may hold values from -1.5 to 1.5
- feature_matrix: bfloat16 [8, 256, 64], replicated, may hold values from -6 to 6
Outputs:
- activations: bfloat16 [32768, 512], P(('dp', 'fsdp'))
- input_grad: bfloat16 [32768, 512], P(('dp', 'fsdp'))
- grad_w_qkv: float32 [512, 1536], P(('dp', 'fsdp'))
- grad_w_out: float32 [512, 512], P(('dp', 'fsdp'))
- grad_w_ffn_in: float32 [512, 2048], P(('dp', 'fsdp'))
- grad_w_ffn_out: float32 [2048, 512], P(('dp', 'fsdp'))
- grad_gain_one: float32 [512], P(('dp', 'fsdp'))
- grad_shift_one: float32 [512], P(('dp', 'fsdp'))
- grad_gain_two: float32 [512], P(('dp', 'fsdp'))
- grad_shift_two: float32 [512], P(('dp', 'fsdp'))
- grad_bias_in: float32 [2048], P(('dp', 'fsdp'))
- grad_bias_out: float32 [512], P(('dp', 'fsdp'))
Inputs may be any that keep to these rules, and one draw needn't show every extreme that they name: `group_id`: group ids are numbered within each batch slice: sequences of different slices never share a group, whatever their ids.
All inputs are finite; a program needn't handle non-finite values.
Results may differ from a plain program's by a relative error of at most 0.019.
The roundings to bfloat16 on the way count: a program that leaves them out, or rounds other values in their place, can miss the bound.
Values may be sent and summed in bfloat16 or wider, within the bound.
A program may use at most 192 MiB of HBM per device.

v0:
```python
import math

import jax
import jax.numpy as jnp
from jax import lax
from jax.sharding import PartitionSpec as P

BLOCK = 512


EPSILON = 1e-05


def normed(values, gain_vec, shift_vec):
    average = jnp.mean(values, axis=-1, keepdims=True)
    centered = values - average
    spread = jnp.mean(centered * centered, axis=-1, keepdims=True)
    return centered * lax.rsqrt(spread + EPSILON) * gain_vec + shift_vec


def gelu_exact(values):
    return jax.nn.gelu(values, approximate=False)


def contract_rows(left_op, right_op):
    return lax.dot_general(
        left_op, right_op, (((0,), (0,)), ((), ())), preferred_element_type=jnp.float32
    )


def contract_cols(left_op, right_op):
    return lax.dot_general(
        left_op, right_op, (((1,), (1,)), ((), ())), preferred_element_type=jnp.float32
    )


def feature_map(scaled_values, random_features_matrix):
    output_scores = jnp.einsum(
        "lxn,xpn->lxp", scaled_values, random_features_matrix, preferred_element_type=jnp.float32
    )
    widened = scaled_values.astype(jnp.float32)
    square = jnp.sum(widened * widened, axis=-1, keepdims=True)
    return jnp.exp(output_scores - 0.5 * square) / math.sqrt(random_features_matrix.shape[1])


def feature_back(grad_feat, feats_full, scaled_values, random_features_matrix, factor):
    product = grad_feat * feats_full
    lowered_dot_result = product.astype(jnp.bfloat16)
    grad_scaled = jnp.einsum(
        "kbc,bcl->kbl",
        lowered_dot_result,
        random_features_matrix,
        preferred_element_type=jnp.float32,
    )
    grad_scaled = grad_scaled - scaled_values.astype(jnp.float32) * jnp.sum(
        product, axis=-1, keepdims=True
    )
    return grad_scaled * factor


def body(
    tokens,
    cotangent,
    group_id,
    w_qkv,
    w_out,
    w_ffn_in,
    w_ffn_out,
    gain_one,
    shift_one,
    gain_two,
    shift_two,
    bias_in,
    bias_out,
    feature_matrix,
):
    gathered = (
        lax.all_gather(w_qkv, ("dp", "fsdp"), axis=0, tiled=True),
        lax.all_gather(w_out, ("dp", "fsdp"), axis=0, tiled=True),
        lax.all_gather(w_ffn_in, ("dp", "fsdp"), axis=0, tiled=True),
        lax.all_gather(w_ffn_out, ("dp", "fsdp"), axis=0, tiled=True),
        lax.all_gather(gain_one, ("dp", "fsdp"), axis=0, tiled=True),
        lax.all_gather(shift_one, ("dp", "fsdp"), axis=0, tiled=True),
        lax.all_gather(gain_two, ("dp", "fsdp"), axis=0, tiled=True),
        lax.all_gather(shift_two, ("dp", "fsdp"), axis=0, tiled=True),
        lax.all_gather(bias_in, ("dp", "fsdp"), axis=0, tiled=True),
        lax.all_gather(bias_out, ("dp", "fsdp"), axis=0, tiled=True),
    )
    full_qkv, full_out, full_in, full_hid, full_g1, full_s1, full_g2, full_s2, full_b1, full_b2 = (
        gathered
    )
    own_seqs = group_id.shape[0]
    slice_seqs = lax.axis_size("dp") * own_seqs
    labels = jnp.arange(slice_seqs // 2, dtype=jnp.int32)
    onehot = (group_id[:, None] == labels[None, :]).astype(jnp.float32)
    counts = lax.psum(jnp.sum(onehot, axis=0), "dp")
    group_size = jnp.sum(onehot * counts[None, :], axis=-1)
    groups = jnp.sum((counts > 0.5).astype(jnp.float32))
    seq_weight = slice_seqs / (groups * group_size)
    seq_len = tokens.shape[0] // own_seqs
    width = full_out.shape[0]
    num_heads = feature_matrix.shape[0]
    head_size = width // num_heads
    num_feats = feature_matrix.shape[1]
    factor = head_size ** (-0.25)
    block_count = seq_len // BLOCK
    causal = jnp.tril(jnp.ones((BLOCK, BLOCK), jnp.float32))
    row_data = tokens.astype(jnp.float32)
    g1_full = full_g1.astype(jnp.float32)
    s1_full = full_s1.astype(jnp.float32)
    g2_full = full_g2.astype(jnp.float32)
    s2_full = full_s2.astype(jnp.float32)
    normal_one = normed(row_data, g1_full, s1_full).astype(jnp.bfloat16)
    projected_features = jnp.dot(normal_one, full_qkv, preferred_element_type=jnp.float32)
    query_rows = (
        (projected_features[:, :width] * factor)
        .astype(jnp.bfloat16)
        .reshape(-1, num_heads, head_size)
    )
    key_rows = (
        (projected_features[:, width : 2 * width] * factor)
        .astype(jnp.bfloat16)
        .reshape(-1, num_heads, head_size)
    )
    value_rows = (
        projected_features[:, 2 * width :].astype(jnp.bfloat16).reshape(-1, num_heads, head_size)
    )
    query_full = feature_map(query_rows, feature_matrix)
    key_full = feature_map(key_rows, feature_matrix)
    query_low = query_full.astype(jnp.bfloat16)
    key_low = key_full.astype(jnp.bfloat16)

    def blocked(array):
        return array.reshape(own_seqs, block_count, BLOCK, num_heads, array.shape[-1])

    query_blocks = blocked(query_low)
    key_blocks = blocked(key_low)
    value_blocks = blocked(value_rows)
    running = jnp.zeros((own_seqs, num_heads, num_feats, head_size), jnp.float32)
    summed = jnp.zeros((own_seqs, num_heads, num_feats), jnp.float32)
    kept_states = []
    kept_sums = []
    kept_outs = []
    kept_dens = []
    for position in range(block_count):
        query_block = query_blocks[:, position]
        key_block = key_blocks[:, position]
        value_block = value_blocks[:, position]
        scores = (
            jnp.einsum(
                "sihm,sjhm->shij", query_block, key_block, preferred_element_type=jnp.float32
            )
            * causal
        )
        numerator = jnp.einsum(
            "shij,sjhd->sihd",
            scores.astype(jnp.bfloat16),
            value_block,
            preferred_element_type=jnp.float32,
        )
        numerator = numerator + jnp.einsum(
            "sihm,shmd->sihd",
            query_block,
            running.astype(jnp.bfloat16),
            preferred_element_type=jnp.float32,
        )
        denominator = jnp.transpose(jnp.sum(scores, axis=-1), (0, 2, 1))
        denominator = denominator + jnp.sum(
            query_block.astype(jnp.float32) * summed[:, None], axis=-1
        )
        kept_states.append(running)
        kept_sums.append(summed)
        kept_dens.append(denominator)
        kept_outs.append(numerator / denominator[..., None])
        running = running + jnp.einsum(
            "sjhm,sjhd->shmd", key_block, value_block, preferred_element_type=jnp.float32
        )
        summed = summed + jnp.sum(key_block.astype(jnp.float32), axis=1)
    attended = jnp.stack(kept_outs, axis=1).reshape(-1, width).astype(jnp.bfloat16)
    middle = row_data + jnp.dot(attended, full_out, preferred_element_type=jnp.float32)
    normal_two = normed(middle, g2_full, s2_full).astype(jnp.bfloat16)
    hidden_pre = jnp.dot(normal_two, full_in, preferred_element_type=jnp.float32) + full_b1.astype(
        jnp.float32
    )
    hidden_full, gelu_pullback = jax.vjp(gelu_exact, hidden_pre)
    hidden_act = hidden_full.astype(jnp.bfloat16)
    result = (
        middle
        + jnp.dot(hidden_act, full_hid, preferred_element_type=jnp.float32)
        + full_b2.astype(jnp.float32)
    )
    activations = result.astype(jnp.bfloat16)
    regathered = (
        lax.all_gather(w_qkv, ("dp", "fsdp"), axis=0, tiled=True),
        lax.all_gather(w_out, ("dp", "fsdp"), axis=0, tiled=True),
        lax.all_gather(w_ffn_in, ("dp", "fsdp"), axis=0, tiled=True),
        lax.all_gather(w_ffn_out, ("dp", "fsdp"), axis=0, tiled=True),
        lax.all_gather(gain_one, ("dp", "fsdp"), axis=0, tiled=True),
        lax.all_gather(shift_one, ("dp", "fsdp"), axis=0, tiled=True),
        lax.all_gather(gain_two, ("dp", "fsdp"), axis=0, tiled=True),
        lax.all_gather(shift_two, ("dp", "fsdp"), axis=0, tiled=True),
        lax.all_gather(bias_in, ("dp", "fsdp"), axis=0, tiled=True),
        lax.all_gather(bias_out, ("dp", "fsdp"), axis=0, tiled=True),
    )
    back_qkv, back_out, back_in, back_hid, back_g1, back_s1, back_g2, back_s2, back_b1, back_b2 = (
        regathered
    )
    row_weight = jnp.repeat(seq_weight, seq_len)[:, None]
    grad_rows = cotangent.astype(jnp.float32) * row_weight
    grad_low = grad_rows.astype(jnp.bfloat16)
    grad_bias_out = jnp.sum(grad_rows, axis=0)
    grad_w_ffn_out = contract_rows(hidden_act, grad_low)
    grad_hidden = contract_cols(grad_low, back_hid)
    (grad_pre,) = gelu_pullback(grad_hidden)
    pre_low = grad_pre.astype(jnp.bfloat16)
    grad_w_ffn_in = contract_rows(normal_two, pre_low)
    grad_bias_in = jnp.sum(pre_low.astype(jnp.float32), axis=0)
    grad_normal_two = contract_cols(pre_low, back_in)
    _, norm_two_pullback = jax.vjp(
        normed, middle, back_g2.astype(jnp.float32), back_s2.astype(jnp.float32)
    )
    grad_mid_norm, grad_gain_two, grad_shift_two = norm_two_pullback(grad_normal_two)
    grad_middle = grad_rows + grad_mid_norm
    middle_low = grad_middle.astype(jnp.bfloat16)
    grad_w_out = contract_rows(attended, middle_low)
    grad_attended = contract_cols(middle_low, back_out).reshape(
        own_seqs, block_count, BLOCK, num_heads, head_size
    )
    grad_running = jnp.zeros((own_seqs, num_heads, num_feats, head_size), jnp.float32)
    grad_summed = jnp.zeros((own_seqs, num_heads, num_feats), jnp.float32)
    query_grads = [None] * block_count
    key_grads = [None] * block_count
    value_grads = [None] * block_count
    for position in reversed(range(block_count)):
        query_block = query_blocks[:, position]
        key_block = key_blocks[:, position]
        value_block = value_blocks[:, position]
        scores = (
            jnp.einsum(
                "sihm,sjhm->shij", query_block, key_block, preferred_element_type=jnp.float32
            )
            * causal
        )
        denominator = kept_dens[position]
        grad_block = grad_attended[:, position]
        grad_numer = (grad_block / denominator[..., None]).astype(jnp.bfloat16)
        grad_denom = -jnp.sum(grad_block * kept_outs[position], axis=-1) / denominator
        grad_scores = jnp.einsum(
            "sihd,sjhd->shij", grad_numer, value_block, preferred_element_type=jnp.float32
        )
        grad_scores = (
            (grad_scores + jnp.transpose(grad_denom, (0, 2, 1))[..., None]) * causal
        ).astype(jnp.bfloat16)
        state_low = kept_states[position].astype(jnp.bfloat16)
        grad_state_low = grad_running.astype(jnp.bfloat16)
        grad_query = jnp.einsum(
            "shij,sjhm->sihm", grad_scores, key_block, preferred_element_type=jnp.float32
        )
        grad_query = grad_query + jnp.einsum(
            "sihd,shmd->sihm", grad_numer, state_low, preferred_element_type=jnp.float32
        )
        grad_query = grad_query + grad_denom[..., None] * kept_sums[position][:, None]
        grad_key = jnp.einsum(
            "shij,sihm->sjhm", grad_scores, query_block, preferred_element_type=jnp.float32
        )
        grad_key = grad_key + jnp.einsum(
            "sjhd,shmd->sjhm", value_block, grad_state_low, preferred_element_type=jnp.float32
        )
        grad_key = grad_key + grad_summed[:, None]
        grad_value = jnp.einsum(
            "shij,sihd->sjhd",
            scores.astype(jnp.bfloat16),
            grad_numer,
            preferred_element_type=jnp.float32,
        )
        grad_value = grad_value + jnp.einsum(
            "sjhm,shmd->sjhd", key_block, grad_state_low, preferred_element_type=jnp.float32
        )
        grad_running = grad_running + jnp.einsum(
            "sihm,sihd->shmd", query_block, grad_numer, preferred_element_type=jnp.float32
        )
        grad_summed = grad_summed + jnp.sum(
            query_block.astype(jnp.float32) * grad_denom[..., None], axis=1
        )
        query_grads[position] = grad_query
        key_grads[position] = grad_key
        value_grads[position] = grad_value
    grad_query_feat = jnp.stack(query_grads, axis=1).reshape(-1, num_heads, num_feats)
    grad_key_feat = jnp.stack(key_grads, axis=1).reshape(-1, num_heads, num_feats)
    grad_value_rows = jnp.stack(value_grads, axis=1).reshape(-1, width)
    grad_query_rows = feature_back(
        grad_query_feat, query_full, query_rows, feature_matrix, factor
    ).reshape(-1, width)
    grad_key_rows = feature_back(grad_key_feat, key_full, key_rows, feature_matrix, factor).reshape(
        -1, width
    )
    grad_projected = jnp.concatenate(
        [grad_query_rows, grad_key_rows, grad_value_rows], axis=1
    ).astype(jnp.bfloat16)
    grad_w_qkv = contract_rows(normal_one, grad_projected)
    grad_normal_one = contract_cols(grad_projected, back_qkv)
    _, norm_one_pullback = jax.vjp(
        normed, row_data, back_g1.astype(jnp.float32), back_s1.astype(jnp.float32)
    )
    grad_row_norm, grad_gain_one, grad_shift_one = norm_one_pullback(grad_normal_one)
    input_grad = (grad_middle + grad_row_norm).astype(jnp.bfloat16)
    all_parts = (
        lax.psum_scatter(grad_w_qkv, ("dp", "fsdp"), scatter_dimension=0, tiled=True),
        lax.psum_scatter(grad_w_out, ("dp", "fsdp"), scatter_dimension=0, tiled=True),
        lax.psum_scatter(grad_w_ffn_in, ("dp", "fsdp"), scatter_dimension=0, tiled=True),
        lax.psum_scatter(grad_w_ffn_out, ("dp", "fsdp"), scatter_dimension=0, tiled=True),
        lax.psum_scatter(grad_gain_one, ("dp", "fsdp"), scatter_dimension=0, tiled=True),
        lax.psum_scatter(grad_shift_one, ("dp", "fsdp"), scatter_dimension=0, tiled=True),
        lax.psum_scatter(grad_gain_two, ("dp", "fsdp"), scatter_dimension=0, tiled=True),
        lax.psum_scatter(grad_shift_two, ("dp", "fsdp"), scatter_dimension=0, tiled=True),
        lax.psum_scatter(grad_bias_in, ("dp", "fsdp"), scatter_dimension=0, tiled=True),
        lax.psum_scatter(grad_bias_out, ("dp", "fsdp"), scatter_dimension=0, tiled=True),
    )
    (
        part_w_qkv,
        part_w_out,
        part_w_ffn_in,
        part_w_ffn_out,
        part_gain_one,
        part_shift_one,
        part_gain_two,
        part_shift_two,
        part_bias_in,
        part_bias_out,
    ) = all_parts
    return (
        activations,
        input_grad,
        part_w_qkv,
        part_w_out,
        part_w_ffn_in,
        part_w_ffn_out,
        part_gain_one,
        part_shift_one,
        part_gain_two,
        part_shift_two,
        part_bias_in,
        part_bias_out,
    )


def solution(mesh):
    return jax.shard_map(
        body,
        mesh=mesh,
        in_specs=(
            P(("dp", "fsdp"), None),
            P(("dp", "fsdp"), None),
            P(("dp", "fsdp")),
            P(("dp", "fsdp"), None),
            P(("dp", "fsdp"), None),
            P(("dp", "fsdp"), None),
            P(("dp", "fsdp"), None),
            P(("dp", "fsdp")),
            P(("dp", "fsdp")),
            P(("dp", "fsdp")),
            P(("dp", "fsdp")),
            P(("dp", "fsdp")),
            P(("dp", "fsdp")),
            P(),
        ),
        out_specs=(
            P(("dp", "fsdp"), None),
            P(("dp", "fsdp"), None),
            P(("dp", "fsdp"), None),
            P(("dp", "fsdp"), None),
            P(("dp", "fsdp"), None),
            P(("dp", "fsdp"), None),
            P(("dp", "fsdp")),
            P(("dp", "fsdp")),
            P(("dp", "fsdp")),
            P(("dp", "fsdp")),
            P(("dp", "fsdp")),
            P(("dp", "fsdp")),
        ),
        check_vma=False,
    )
```

profile of v0, /device:TPU:0, one launch (start us, length us, event | category | flops | bytes accessed | tf_op | source)
XLA Modules:
  0.0 793.1 jit_solution(2289666026672868952)
XLA Ops:
  10.3 23.1 %psum.7 = f32[4]{0:T(128)S(1)} all-reduce(f32[4]{0:T(128)S(1)} %compare_convert_fusion.1), channel_id=1, replica_groups=mesh['dp'=8,'fsdp'=4] {'dp'}, use_global_device_ids=true, to_apply=%region_11.12 | all-reduce | flops 4 | bytes 32 | tf_op jit(solution)/shard_map/psum | solution.py:96
  38.5 37.2 %all-reduce.13 = (bf16[512]{0:T(512)(128)(2,1)S(1)}, bf16[512]{0:T(512)(128)(2,1)S(1)}, bf16[512]{0:T(512)(128)(2,1)S(1)}, bf16[512]{0:T(512)(128)(2,1)S(1)}, bf...) all-reduce(bf16[512]{0:T(512)(128)(2,1)S(1)} %dynamic-update-slice., ...), channel_id=1, replica_groups=mesh['dp'=8,'fsdp'=4] {'dp','fsdp'}, use_global_device_ids=true, to_apply=%add.1 | all-reduce | flops 4608 | bytes 18432
  75.7 46.5 %all_gather.39 = bf16[512,512]{1,0:T(8,128)(2,1)} all-gather(bf16[16,512]{1,0:T(8,128)(2,1)} %param.18), channel_id=1, replica_groups=mesh['dp'=8,'fsdp'=4] {'dp','fsdp'}, dimensions={0}, use_global_device_ids=true | all-gather | bytes 540672 | tf_op jit(solution)/shard_map/all_gather | solution.py:79
  128.2 3.4 fusion.143
  136.6 4.1 fusion.13
  146.2 4.1 fusion.11
  154.4 4.5 fusion.54
  174.4 7.2 multiply_reduce_fusion.1
  190.9 25.0 %multiply_convert_fusion.2 = (bf16[1024,2048]{1,0:T(8,128)(2,1)}, f32[1024,2048]{1,0:T(8,128)}, f32[1024,2048]{1,0:T(8,128)}) fusion(f32[2048]{0:T(1024)S(1)} %convert_element_type.206, bf16[512,2048]{1,0:T(8,128)(2,1)} %all-gather.6.cloned.1.call-done, f32[1024,512]{0,1:T(8,128)} %copy-done.14, f32[512]{0:T(512)S(1)} %convert_element_type.204, ...), kind=kOutput, calls=%fused_computation.14 | convolution fusion | flops 2288517120 | bytes 25186304 | tf_op jit(solution)/shard_map/dot_general | solution.py:182
  215.9 9.5 %convert_reduce_fusion = (f32[2048]{0:T(1024)S(1)}, bf16[1024,2048]{1,0:T(8,128)(2,1)S(1)}) fusion(f32[1024,2048]{1,0:T(8,128)} %get-tuple-element.71, bf16[2048,512]{1,0:T(8,128)(2,1)} %all-gather.8.cloned.1.call-done, bf16[1024,512]{0,1:T(8,128)(2,1)S(1)} %copy-done.30, f32[]{:T(128)S(6)} %div.115, f32[1024,2048]{1,0:T(8,128)} %get-tuple-element.91, ...), kind=kOutput, calls=%fused_computation.10 | convolution fusion | flops 2184706048 | bytes 24133636 | tf_op jit(solution)/shard_map/dot_general | solution.py:32
  225.4 3.7 fusion.153
  240.8 4.2 reshape.434
  245.0 4.3 fusion.149
  255.5 3.5 fusion.58
  261.4 3.3 fusion.48
  264.7 3.4 fusion.76
  268.3 5.2 fusion.86
  275.2 4.8 fusion.87
  285.8 4.3 pad_maximum_fusion.1
  290.1 9.2 %copy.142 = f32[1,2,512,8,256]{4,2,1,3,0:T(8,128)} copy(f32[1,2,512,8,256]{2,4,3,1,0:T(8,128)} %pad_maximum_fusion.1) | data formatting | bytes 16777216 | tf_op jit(solution)/shard_map/stack | solution.py:289
  304.0 4.2 pad_maximum_fusion
  308.2 4.1 copy.137
  318.6 5.1 fusion.39
  332.0 3.6 fusion.84
  335.7 6.6 fusion.106
  343.9 6.6 fusion.145
  351.1 6.2 add_convert_fusion.2
  359.8 5.5 fusion.152
  371.2 37.2 %all-reduce.12 = (f32[512]{0:T(512)S(1)}, f32[512]{0:T(512)S(1)}, f32[512]{0:T(512)S(1)}, f32[512]{0:T(512)S(1)}, f32[2048]{0:T(1024)S(1)}, /*index=5*/f32[512]{0:T(512)S(1)}) all-reduce(f32[512]{0:T(512)S(1)} %get-tuple-element.50, f32[512]{0:T(512)S(1)} %get-tuple-element.92, ...), channel_id=6, replica_groups=mesh['dp'=8,'fsdp'=4] {'dp','fsdp'}, use_global_device_ids=true, to_apply=%region_28.29.clone | all-reduce | flops 4608 | bytes 36864
  414.2 89.4 %reduce-scatter.5.cloned.1.call-done = f32[16,1536]{1,0:T(8,128)} async-done(((f32[512,1536]{1,0:T(8,128)}), f32[16,1536]{1,0:T(8,128)}) %reduce-scatter.5.cloned.1.call-update) | async-done | bytes 98320 | tf_op jit(solution)/shard_map/reduce_scatter | solution.py:308
  503.5 142.6 %reduce-scatter.11.cloned.1.call-done = f32[64,512]{1,0:T(8,128)} async-done(((f32[2048,512]{1,0:T(8,128)}), f32[64,512]{1,0:T(8,128)}) %reduce-scatter.11.cloned.1.call-update) | async-done | bytes 131088 | tf_op jit(solution)/shard_map/reduce_scatter | solution.py:311
  646.1 140.0 %reduce-scatter.9.cloned.1.call-done = f32[16,2048]{1,0:T(8,128)} async-done(((f32[512,2048]{1,0:T(8,128)}), f32[16,2048]{1,0:T(8,128)}) %reduce-scatter.9.cloned.1.call-update) | async-done | bytes 131088 | tf_op jit(solution)/shard_map/reduce_scatter | solution.py:310
  (275 shorter events, 113.7 us)
Async XLA Ops:
  7.2 129.4 %copy-start = (bf16[8,256,64]{1,2,0:T(8,128)(2,1)S(1)}, bf16[8,256,64]{1,2,0:T(8,128)(2,1)}, u32[]{:S(2)}) copy-start(bf16[8,256,64]{1,2,0:T(8,128)(2,1)} %param.27) | copy-start | bytes 786436
  7.2 117.7 %copy-start.46 = (bf16[1024,512]{1,0:T(8,128)(2,1)S(1)}, bf16[1024,512]{1,0:T(8,128)(2,1)}, u32[]{:S(2)}) copy-start(bf16[1024,512]{1,0:T(8,128)(2,1)} %param.15) | copy-start | bytes 3145732
  7.2 121.0 %all-gather.4.cloned.1.call-start = ((), (), s32[]{:S(2)}) async-start(), calls=%async_computation.4 | async-start | bytes 1622016 | tf_op jit(solution)/shard_map/all_gather | solution.py:78
  7.9 182.9 %all-gather.6.cloned.1.call-start = ((), (), s32[]{:S(2)}) async-start(), calls=%async_computation.5 | async-start | bytes 2162688 | tf_op jit(solution)/shard_map/all_gather | solution.py:80
  8.7 207.1 %all-gather.8.cloned.1.call-start = ((), (), s32[]{:S(2)}) async-start(), calls=%async_computation.6 | async-start | bytes 2162688 | tf_op jit(solution)/shard_map/all_gather | solution.py:81
  9.4 404.7 %reduce-scatter.7.cloned.1.call-start = ((), (), s32[]{:S(2)}) async-start(), calls=%async_computation.8 | async-start | bytes 1081344 | tf_op jit(solution)/shard_map/reduce_scatter | solution.py:309
  75.7 56.0 %copy-start.63 = (f32[512]{0:T(512)}, f32[512]{0:T(512)S(1)}, u32[]{:S(2)}) copy-start(f32[512]{0:T(512)S(1)} %convert_element_type.187) | copy-start | bytes 6148
  75.7 56.0 %copy-start.61 = (f32[512]{0:T(512)}, f32[512]{0:T(512)S(1)}, u32[]{:S(2)}) copy-start(f32[512]{0:T(512)S(1)} %convert_element_type.186) | copy-start | bytes 6148
  123.8 64.6 %copy-start.12 = (bf16[1024,512]{0,1:T(8,128)(2,1)}, bf16[1024,512]{0,1:T(8,128)(2,1)S(1)}, u32[]{:S(2)}) copy-start(bf16[1024,512]{0,1:T(8,128)(2,1)S(1)} %copy.108) | copy-start | bytes 3145732
  124.0 7.7 copy-start.55
  124.9 6.8 copy-start.57
  166.0 15.6 %copy-start.34 = (bf16[1,1,512,8,64]{2,4,3,1,0:T(8,128)(2,1)}, bf16[1,1,512,8,64]{2,4,3,1,0:T(8,128)(2,1)S(1)}, u32[]{:S(2)}) copy-start(bf16[1,1,512,8,64]{2,4,3,1,0:T(8,128)(2,1)S(1)} %copy.176) | copy-start | bytes 1572868
  168.1 15.1 %copy-start.36 = (bf16[1,1,512,8,64]{2,4,3,1,0:T(8,128)(2,1)}, bf16[1,1,512,8,64]{2,4,3,1,0:T(8,128)(2,1)S(1)}, u32[]{:S(2)}) copy-start(bf16[1,1,512,8,64]{2,4,3,1,0:T(8,128)(2,1)S(1)} %copy.173) | copy-start | bytes 1572868
  168.1 6.2 copy-start.7
  170.4 11.2 %copy-start.48 = (bf16[8,256,64]{1,2,0:T(8,128)(2,1)}, bf16[8,256,64]{1,2,0:T(8,128)(2,1)S(1)}, u32[]{:S(2)}) copy-start(bf16[8,256,64]{1,2,0:T(8,128)(2,1)S(1)} %fusion.88) | copy-start | bytes 786436
  173.6 8.0 %slice-start = ((s8[8388608]{0:T(1024)(128)(4,1)}), s8[4194304]{0:T(1024)(128)(4,1)S(1)}, s32[]{:S(2)}) async-start(s8[8388608]{0:T(1024)(128)(4,1)} %bitcast.315), calls=%async_computation.11 | async-start | bytes 8388608
  174.3 7.3 slice-start.1
  190.8 25.0 %copy-start.30 = (bf16[1024,512]{0,1:T(8,128)(2,1)S(1)}, bf16[1024,512]{0,1:T(8,128)(2,1)}, u32[]{:S(2)}) copy-start(bf16[1024,512]{0,1:T(8,128)(2,1)} %copy.122) | copy-start | bytes 3145732
  215.8 9.6 %copy-start.66 = (bf16[512,2048]{1,0:T(8,128)(2,1)S(1)}, bf16[512,2048]{1,0:T(8,128)(2,1)}, u32[]{:S(2)}) copy-start(bf16[512,2048]{1,0:T(8,128)(2,1)} %all-gather.6.cloned.1.call-done) | copy-start | bytes 6291460
  240.8 8.6 %copy-start.27 = (f32[1,512,8,64]{1,3,2,0:T(8,128)S(1)}, f32[1,512,8,64]{1,3,2,0:T(8,128)}, u32[]{:S(2)}) copy-start(f32[1,512,8,64]{1,3,2,0:T(8,128)} %copy-done.26) | copy-start | bytes 3145732
  268.2 235.3 %reduce-scatter.5.cloned.1.call-start = ((), (), s32[]{:S(2)}) async-start(), calls=%async_computation.7 | async-start | bytes 3244032 | tf_op jit(solution)/shard_map/reduce_scatter | solution.py:308
  290.1 9.2 %copy-start.49 = (bf16[8,256,64]{1,2,0:T(8,128)(2,1)S(1)}, bf16[8,256,64]{1,2,0:T(8,128)(2,1)}, u32[]{:S(2)}) copy-start(bf16[8,256,64]{1,2,0:T(8,128)(2,1)} %copy-done.48) | copy-start | bytes 786436
  304.0 11.6 %slice-start.4 = ((s8[8388608]{0:T(1024)(128)(4,1)}), s8[4194304]{0:T(1024)(128)(4,1)S(1)}, s32[]{:S(2)}) async-start(s8[8388608]{0:T(1024)(128)(4,1)} %bitcast.337), calls=%async_computation.15 | async-start | bytes 8388608
  308.2 7.4 slice-start.5
  308.2 7.4 copy-start.54
  315.6 8.1 %slice-start.2 = ((s8[8388608]{0:T(1024)(128)(4,1)}), s8[4194304]{0:T(1024)(128)(4,1)S(1)}, s32[]{:S(2)}) async-start(s8[8388608]{0:T(1024)(128)(4,1)} %bitcast.335), calls=%async_computation.13 | async-start | bytes 8388608
  315.6 8.1 %slice-start.6 = ((s8[8388608]{0:T(1024)(128)(4,1)}), s8[4194304]{0:T(1024)(128)(4,1)S(1)}, s32[]{:S(2)}) async-start(s8[8388608]{0:T(1024)(128)(4,1)} %bitcast.339), calls=%async_computation.17 | async-start | bytes 8388608
  318.5 6.4 slice-start.7
  318.5 6.4 copy-start.52
  323.6 7.4 copy-start.44
  335.6 310.5 %reduce-scatter.11.cloned.1.call-start = ((), (), s32[]{:S(2)}) async-start(), calls=%async_computation.10 | async-start | bytes 4325376 | tf_op jit(solution)/shard_map/reduce_scatter | solution.py:311
  342.3 443.8 %reduce-scatter.9.cloned.1.call-start = ((), (), s32[]{:S(2)}) async-start(), calls=%async_computation.9 | async-start | bytes 4325376 | tf_op jit(solution)/shard_map/reduce_scatter | solution.py:310
  (51 other events, 164.4 us)
Sparse Core Ops, SparseCore 0:
  10.9 57.9 all-gather.3
  71.8 56.1 all-gather.5
  130.8 55.1 all-gather.7
  268.3 130.8 reduce-scatter.6
  406.0 97.4 reduce-scatter.4
  506.3 139.7 reduce-scatter.10
  649.0 136.9 reduce-scatter.8
where the time goes:
time: 797 us; the launch traced here: 793 us
  waiting for transfers between devices  374 us (47%)
  matrix products  146 us (18%)
  blocking collectives  144 us (18%)
  local copies, waits for them, and re-layouts  80.2 us (10%)
  other arithmetic  31.1 us (4%)
  between operations  17.5 us (2%)
    reduce_scatter x1, waiting for transfers between devices, body(): lax.psum_scatter(grad_w_ffn_out, ('dp', 'fsdp'), scatter_dimension=0, til...  143 us
    reduce_scatter x1, waiting for transfers between devices, body(): lax.psum_scatter(grad_w_ffn_in, ('dp', 'fsdp'), scatter_dimension=0, tile...  140 us
    reduce_scatter x1, waiting for transfers between devices, body(): lax.psum_scatter(grad_w_qkv, ('dp', 'fsdp'), scatter_dimension=0, tiled=T...  89.4 us
    unnamed x2, blocking collectives  74.4 us
    all_gather x1, blocking collectives, body(): lax.all_gather(w_out, ('dp', 'fsdp'), axis=0, tiled=True)  46.5 us
    unnamed x178, local copies, waits for them, and re-layouts  41.8 us
    dot_general x1, matrix products, body(): jnp.dot(normal_two, full_in, preferred_element_type=jnp.float32)  25 us
    psum x1, blocking collectives, body(): counts = lax.psum(jnp.sum(onehot, axis=0), 'dp')  23.1 us
  transfers between devices with their start and end apart: 7, of which 3 were waited for; matrix products, arithmetic and copies ran while one was open for 24% of the time, Pallas kernels for 0%

commit v1 on v0

v1 whole, which is shorter than its diff:
```python
import functools
import math

import jax
import jax.numpy as jnp
from jax import lax
from jax.experimental import pallas as pl
from jax.experimental.pallas import tpu as pltpu
from jax.sharding import PartitionSpec as P

BLOCK = 512
EPSILON = 1e-05
TILE = 256
LANES = 128
LOG2E = 1.4426950408889634
AXES = ("dp", "fsdp")
BF = jnp.bfloat16
F32 = jnp.float32


def dot(left, right):
    return lax.dot_general(left, right, (((1,), (0,)), ((), ())), preferred_element_type=F32)


def dot_bt(left, right):
    return lax.dot_general(left, right, (((1,), (1,)), ((), ())), preferred_element_type=F32)


def dot_at(left, right):
    return lax.dot_general(left, right, (((0,), (0,)), ((), ())), preferred_element_type=F32)


def lane_ids(rows, width=LANES):
    return lax.broadcasted_iota(jnp.int32, (rows, width), 1)


def tile_at(index, size=TILE):
    return pl.ds(pl.multiple_of(index * size, size), size)


def centred(values):
    mu = jnp.mean(values, axis=-1, keepdims=True)
    cen = values - mu
    inv = lax.rsqrt(jnp.mean(cen * cen, axis=-1, keepdims=True) + EPSILON)
    return cen * inv, inv


def norm_back(grad, unit, inv, gain):
    e = grad * gain
    return inv * (
        e
        - jnp.mean(e, axis=-1, keepdims=True)
        - unit * jnp.mean(e * unit, axis=-1, keepdims=True)
    )


def causal(values, offset):
    row = lax.broadcasted_iota(jnp.int32, values.shape, 0)
    col = lax.broadcasted_iota(jnp.int32, values.shape, 1)
    return jnp.where(col <= row + offset, values, 0.0).astype(BF)


def anticausal(values):
    row = lax.broadcasted_iota(jnp.int32, values.shape, 0)
    col = lax.broadcasted_iota(jnp.int32, values.shape, 1)
    return jnp.where(col >= row, values, 0.0).astype(BF)


def project_rows(i, x_ref, wq, prm_ref, h_ref, q_ref, k_ref, v_ref, factor):
    rows = tile_at(i)
    unit, _ = centred(x_ref[rows, :].astype(F32))
    h = (unit * prm_ref[0:1, :] + prm_ref[1:2, :]).astype(BF)
    h_ref[rows, :] = h
    width = h.shape[1]
    qkv = dot(h, wq)
    q_ref[rows, :] = (qkv[:, :width] * factor).astype(BF)
    k_ref[rows, :] = (qkv[:, width : 2 * width] * factor).astype(BF)
    v_ref[rows, :] = qkv[:, 2 * width :].astype(BF)


def attend_pair(p, q_ref, k_ref, v_ref, fx_ref, pq_ref, pk_ref, att_ref, attr_ref, den_ref):
    length = q_ref.shape[0]
    feats = fx_ref.shape[1]
    lanes = tile_at(p, LANES)
    shift = 0.5 * math.log2(feats)
    cols = [tile_at(2 * p + hh, feats) for hh in range(2)]
    for hh in range(2):
        fm = fx_ref[2 * p + hh][:, :LANES]
        for src, dst in ((q_ref, pq_ref), (k_ref, pk_ref)):
            for t in range(length // TILE):
                rows = slice(t * TILE, (t + 1) * TILE)
                part = src[rows, lanes]
                scores = dot_bt(part, fm)
                wide = jnp.where(lane_ids(TILE) // 64 == hh, part.astype(F32), 0.0)
                square = jnp.sum(wide * wide, axis=-1, keepdims=True)
                feat = jnp.exp2(scores * LOG2E - (square * (0.5 * LOG2E) + shift))
                dst[rows, cols[hh]] = feat.astype(BF)
    ones = jnp.ones((length, LANES), BF)
    vx = jnp.concatenate([v_ref[:, lanes], ones], axis=1)
    states = [None, None]
    low = [None, None]
    for b in range(length // BLOCK):
        base = b * BLOCK
        for i in range(BLOCK // TILE):
            rows = slice(base + i * TILE, base + (i + 1) * TILE)
            keys = slice(base, base + (i + 1) * TILE)
            got = []
            for hh in range(2):
                pq = pq_ref[rows, cols[hh]]
                weights = causal(dot_bt(pq, pk_ref[keys, cols[hh]]), i * TILE)
                both = dot(weights, vx[keys])
                if b:
                    both = both + dot(pq, low[hh])
                got.append(both)
            first = lane_ids(TILE) < 64
            num = jnp.where(first, got[0][:, :LANES], got[1][:, :LANES])
            den = jnp.where(first, got[0][:, LANES:], got[1][:, LANES:])
            att = num / den
            att_ref[rows, lanes] = att
            attr_ref[rows, lanes] = att.astype(BF)
            den_ref[rows, lanes] = den
        if base + BLOCK < length:
            block = slice(base, base + BLOCK)
            for hh in range(2):
                more = dot_at(pk_ref[block, cols[hh]], vx[block])
                states[hh] = more if b == 0 else states[hh] + more
                low[hh] = states[hh].astype(BF)


def forward_kernel(
    factor, x_ref, wq_ref, prm_ref, fx_ref,
    h_ref, q_ref, k_ref, v_ref, pq_ref, pk_ref, att_ref, attr_ref, den_ref,
):
    def rows(i, carry):
        project_rows(i, x_ref, wq_ref[...], prm_ref, h_ref, q_ref, k_ref, v_ref, factor)
        return carry

    lax.fori_loop(0, x_ref.shape[0] // TILE, rows, 0)

    def pair(p, carry):
        attend_pair(p, q_ref, k_ref, v_ref, fx_ref, pq_ref, pk_ref, att_ref, attr_ref, den_ref)
        return carry

    lax.fori_loop(0, x_ref.shape[1] // LANES, pair, 0)


def middle_kernel(
    x_ref, attr_ref, cot_ref, wo_ref, wi_ref, wf_ref, prm_ref, bin_ref, seq_ref,
    act_ref, dy_ref, datt_ref, gprm_ref, gbin_ref, gf_ref, gi_ref, go_ref,
    hid_ref, du_ref, h_ref, gr_ref, dor_ref,
):
    length, width = x_ref.shape
    hidden = wi_ref.shape[1]
    chunk = 512
    gprm_ref[...] = jnp.zeros_like(gprm_ref)
    gbin_ref[...] = jnp.zeros_like(gbin_ref)

    def rows(t, carry):
        rows = tile_at(t)
        y = x_ref[rows, :].astype(F32) + dot(attr_ref[rows, :], wo_ref[...])
        unit, inv = centred(y)
        gain = prm_ref[2:3, :]
        h = (unit * gain + prm_ref[3:4, :]).astype(BF)
        h_ref[rows, :] = h
        g = cot_ref[rows, :].astype(F32) * seq_ref[0:1, 0:1]
        gr = g.astype(BF)
        gr_ref[rows, :] = gr
        out = y + prm_ref[4:5, :]
        dh = jnp.zeros((TILE, width), F32)
        for c in range(hidden // chunk):
            cs = slice(c * chunk, (c + 1) * chunk)
            wi = wi_ref[:, cs]
            wf = wf_ref[cs, :]
            u = dot(h, wi) + bin_ref[0:1, cs]
            cdf = 0.5 + 0.5 * lax.erf(u * math.sqrt(0.5))
            slope = cdf + u * jnp.exp2(u * u * (-0.5 * LOG2E)) * (1.0 / math.sqrt(2.0 * math.pi))
            hid = (u * cdf).astype(BF)
            hid_ref[rows, cs] = hid
            out = out + dot(hid, wf)
            du = (dot_bt(gr, wf) * slope).astype(BF)
            du_ref[rows, cs] = du
            gbin_ref[0:1, cs] += jnp.sum(du.astype(F32), axis=0, keepdims=True)
            dh = dh + dot_bt(du, wi)
        act_ref[rows, :] = out.astype(BF)
        gprm_ref[2:3, :] += jnp.sum(dh * unit, axis=0, keepdims=True)
        gprm_ref[3:4, :] += jnp.sum(dh, axis=0, keepdims=True)
        gprm_ref[4:5, :] += jnp.sum(g, axis=0, keepdims=True)
        dy = g + norm_back(dh, unit, inv, gain)
        dy_ref[rows, :] = dy
        dor = dy.astype(BF)
        dor_ref[rows, :] = dor
        datt_ref[rows, :] = dot_bt(dor, wo_ref[...])
        return carry

    lax.fori_loop(0, length // TILE, rows, 0)

    def grad_f(c, carry):
        cs = tile_at(c)
        gf_ref[cs, :] = dot_at(hid_ref[:, cs], gr_ref[...]).astype(gf_ref.dtype)
        return carry

    lax.fori_loop(0, hidden // TILE, grad_f, 0)

    def grad_i(c, carry):
        cs = tile_at(c)
        gi_ref[cs, :] = dot_at(h_ref[:, cs], du_ref[...]).astype(gi_ref.dtype)
        go_ref[cs, :] = dot_at(attr_ref[:, cs], dor_ref[...]).astype(go_ref.dtype)
        return carry

    lax.fori_loop(0, width // TILE, grad_i, 0)


def back_pair(
    p, factor, q_ref, k_ref, v_ref, pq_ref, pk_ref, att_ref, den_ref, datt_ref, fx_ref,
    ht_ref, dqkv_ref, gq_ref, dn_ref, acc_ref,
):
    length = q_ref.shape[0]
    feats = fx_ref.shape[1]
    width = q_ref.shape[1]
    lanes = tile_at(p, LANES)
    blocks = length // BLOCK
    cols = [tile_at(2 * p + hh, feats) for hh in range(2)]
    v = v_ref[:, lanes]
    two = jnp.where(lane_ids(length) < 2, 1.0, 0.0).astype(BF)
    vx = jnp.concatenate([v, jnp.ones((length, LANES), BF)], axis=1)
    v2 = jnp.concatenate([v, two], axis=1)
    for t in range(length // TILE):
        rows = slice(t * TILE, (t + 1) * TILE)
        dn = datt_ref[rows, lanes] / den_ref[rows, lanes]
        prod = dn * att_ref[rows, lanes]
        lane = lane_ids(TILE)
        for hh in range(2):
            mine = lane // 64 == hh
            dden = -jnp.sum(jnp.where(mine, prod, 0.0), axis=-1, keepdims=True)
            high = dden.astype(BF).astype(F32)
            extra = jnp.where(lane == 0, high, jnp.where(lane == 1, dden - high, 0.0))
            dn_ref[hh, rows, :LANES] = jnp.where(mine, dn, 0.0).astype(BF)
            dn_ref[hh, rows, LANES:] = extra.astype(BF)
    for hh in range(2):
        mine = lane_ids(TILE) // 64 == hh
        fx = fx_ref[2 * p + hh]
        low = [None] * blocks
        total = None
        for b in range(blocks - 1):
            block = slice(b * BLOCK, (b + 1) * BLOCK)
            more = dot_at(pk_ref[block, cols[hh]], vx[block])
            total = more if total is None else total + more
            low[b + 1] = total.astype(BF)
        back = [None] * blocks
        total = None
        for b in range(blocks - 1, 0, -1):
            block = slice(b * BLOCK, (b + 1) * BLOCK)
            more = dot_at(pq_ref[block, cols[hh]], dn_ref[hh, block, :])
            total = more if total is None else total + more
            dz = total[:, LANES : LANES + 1] + total[:, LANES + 1 : LANES + 2]
            high = dz.astype(BF).astype(F32)
            lane = lane_ids(feats)
            extra = jnp.where(lane == 0, high, jnp.where(lane == 1, dz - high, 0.0))
            back[b - 1] = jnp.concatenate([total[:, :LANES], extra], axis=1).astype(BF)

        def finish(grad, feat, part, where, hh=hh, fx=fx, mine=mine):
            e = (grad * feat.astype(F32)).astype(BF)
            res = dot(e, fx)
            out = (res[:, :LANES] - part.astype(F32) * res[:, LANES:]) * factor
            rows, at = where
            if hh == 0:
                acc_ref[at, rows, :] = out
            else:
                both = jnp.where(mine, out, acc_ref[at, rows, :])
                start = pl.multiple_of(p * LANES + at * width, LANES)
                dqkv_ref[rows, pl.ds(start, LANES)] = both.astype(BF)

        for b in range(blocks):
            base = b * BLOCK
            for i in range(BLOCK // TILE):
                rows = slice(base + i * TILE, base + (i + 1) * TILE)
                keys = slice(base, base + (i + 1) * TILE)
                dn = dn_ref[hh, rows, :]
                da = causal(dot_bt(dn, v2[keys]), i * TILE)
                grad = dot(da, pk_ref[keys, cols[hh]])
                if b:
                    grad = grad + dot_bt(dn, low[b])
                finish(grad, pq_ref[rows, cols[hh]], q_ref[rows, lanes], (rows, 0))
                later = slice(base + i * TILE, base + BLOCK)
                pk = pk_ref[rows, cols[hh]]
                pql = pq_ref[later, cols[hh]]
                dnl = dn_ref[hh, later, :]
                dat = anticausal(dot_bt(v2[rows], dnl))
                grad = dot(dat, pql)
                at = anticausal(dot_bt(pk, pql))
                dv = dot(at, dnl[:, :LANES])
                if b < blocks - 1:
                    grad = grad + dot_bt(v2[rows], back[b])
                    dv = dv + dot(pk, back[b][:, :LANES])
                finish(grad, pk, k_ref[rows, lanes], (rows, 1))
                if hh == 0:
                    acc_ref[2, rows, :] = dv
                else:
                    both = acc_ref[2, rows, :] + dv
                    start = pl.multiple_of(p * LANES + 2 * width, LANES)
                    dqkv_ref[rows, pl.ds(start, LANES)] = both.astype(BF)
    for at in range(3):
        where = pl.ds(pl.multiple_of(p * LANES + at * width, LANES), LANES)
        gq_ref[:, where] = dot(ht_ref[...], dqkv_ref[:, where]).astype(gq_ref.dtype)


def input_rows(t, x_ref, wq, prm_ref, dqkv_ref, dy_ref, out_ref, gprm_ref):
    rows = tile_at(t)
    dh = dot_bt(dqkv_ref[rows, :], wq)
    unit, inv = centred(x_ref[rows, :].astype(F32))
    gprm_ref[0:1, :] += jnp.sum(dh * unit, axis=0, keepdims=True)
    gprm_ref[1:2, :] += jnp.sum(dh, axis=0, keepdims=True)
    out_ref[rows, :] = (dy_ref[rows, :] + norm_back(dh, unit, inv, prm_ref[0:1, :])).astype(BF)


def backward_kernel(
    factor, x_ref, h_ref, q_ref, k_ref, v_ref, pq_ref, pk_ref, att_ref, den_ref, datt_ref, dy_ref,
    wq_ref, fx_ref, prm_ref, gin_ref,
    out_ref, gq_ref, gprm_ref,
    ht_ref, dqkv_ref, dn_ref, acc_ref,
):
    gprm_ref[...] = gin_ref[...]
    for t in range(x_ref.shape[0] // TILE):
        rows = slice(t * TILE, (t + 1) * TILE)
        ht_ref[:, rows] = h_ref[rows, :].T

    def pair(p, carry):
        back_pair(
            p, factor, q_ref, k_ref, v_ref, pq_ref, pk_ref, att_ref, den_ref, datt_ref, fx_ref,
            ht_ref, dqkv_ref, gq_ref, dn_ref, acc_ref,
        )
        return carry

    lax.fori_loop(0, x_ref.shape[1] // LANES, pair, 0)

    def rows(t, carry):
        input_rows(t, x_ref, wq_ref[...], prm_ref, dqkv_ref, dy_ref, out_ref, gprm_ref)
        return carry

    lax.fori_loop(0, x_ref.shape[0] // TILE, rows, 0)


def call(kernel, outs, scratch, name):
    return pl.pallas_call(
        kernel,
        out_shape=[jax.ShapeDtypeStruct(s, d) for s, d in outs],
        scratch_shapes=[pltpu.VMEM(s, d) for s, d in scratch],
        compiler_params=pltpu.CompilerParams(vmem_limit_bytes=60 * 2**20),
        name=name,
    )


def body(
    tokens, cotangent, group_id, w_qkv, w_out, w_ffn_in, w_ffn_out,
    gain_one, shift_one, gain_two, shift_two, bias_in, bias_out, feature_matrix,
):
    gather = functools.partial(lax.all_gather, axis_name=AXES, axis=0, tiled=True)
    scatter = functools.partial(
        lax.psum_scatter, axis_name=AXES, scatter_dimension=0, tiled=True
    )
    length, width = tokens.shape
    heads, feats, head_size = feature_matrix.shape
    hidden = w_ffn_in.shape[1]
    factor = head_size ** (-0.25)
    wq, wo, wi, wf = gather(w_qkv), gather(w_out), gather(w_ffn_in), gather(w_ffn_out)
    prm = gather(jnp.stack([gain_one, shift_one, gain_two, shift_two, bias_out], axis=1))
    prm = jnp.pad(prm.T.astype(F32), ((0, 3), (0, 0)))
    full_bin = gather(bias_in).astype(F32)[None]

    slice_seqs = lax.axis_size("dp") * group_id.shape[0]
    labels = jnp.arange(slice_seqs // 2, dtype=jnp.int32)
    onehot = (group_id[:, None] == labels[None, :]).astype(F32)
    counts = lax.psum(jnp.sum(onehot, axis=0), "dp")
    group_size = jnp.sum(onehot * counts[None, :], axis=-1)
    groups = jnp.sum((counts > 0.5).astype(F32))
    seq_weight = jnp.broadcast_to((slice_seqs / (groups * group_size))[:, None], (1, LANES))

    fm = feature_matrix
    zero = jnp.zeros_like(fm)
    even = (jnp.arange(heads) % 2 == 0)[:, None, None]
    fx = jnp.concatenate(
        [jnp.where(even, fm, zero), jnp.where(even, zero, fm), jnp.ones((heads, feats, LANES), BF)],
        axis=-1,
    )
    big = (length, width)
    h1, q, k, v, pq, pk, att, attr, den = call(
        functools.partial(forward_kernel, factor),
        [(big, BF)] * 4 + [((length, heads * feats), BF)] * 2 + [(big, F32), (big, BF), (big, F32)],
        [],
        "forward",
    )(tokens, wq, prm, fx)
    act, dy, datt, gprm, gbin, gf, gi, go = call(
        middle_kernel,
        [
            (big, BF), (big, F32), (big, F32), ((8, width), F32), ((1, hidden), F32),
            ((hidden, width), BF), ((width, hidden), BF), ((width, width), BF),
        ],
        [((length, hidden), BF), ((length, hidden), BF), (big, BF), (big, BF), (big, BF)],
        "middle",
    )(tokens, attr, cotangent, wo, wi, wf, prm, full_bin, seq_weight)
    input_grad, gq, gprm = call(
        functools.partial(backward_kernel, factor),
        [(big, BF), ((width, 3 * width), BF), ((8, width), F32)],
        [
            ((width, length), BF), ((length, 3 * width), BF),
            ((2, length, 2 * LANES), BF), ((3, length, LANES), F32),
        ],
        "backward",
    )(tokens, h1, q, k, v, pq, pk, att, den, datt, dy, wq, fx, prm, gprm)
    small = scatter(gprm.T)
    part = [scatter(t).astype(F32) for t in (gq, go, gi, gf)]
    return (act, input_grad, *part, *(small[:, i] for i in range(4)), scatter(gbin[0]), small[:, 4])


def solution(mesh):
    rows, vec = P(AXES, None), P(AXES)
    return jax.shard_map(
        body,
        mesh=mesh,
        in_specs=(rows, rows, vec, *[rows] * 4, *[vec] * 6, P()),
        out_specs=(*[rows] * 6, *[vec] * 6),
        check_vma=False,
    )
```

time: 797 us -> 901 us (1.13)
  waiting for transfers between devices: 374 us -> 593 us
  matrix products: 146 us -> 0 us
  Pallas kernels: 0 us -> 90.5 us
  local copies, waits for them, and re-layouts: 80.2 us -> 9.49 us
  blocking collectives: 144 us -> 181 us
  other arithmetic: 31.1 us -> 9.24 us
    dot_general x38 -> x0, matrix products: 146 us -> none  [the longest x1 25 us: body(): jnp.dot(normal_two, full_in, preferred_element_type=jnp.float32)]
    reduce_scatter x4, waiting for transfers between devices: 372 us -> 495 us  [body(): part = [scatter(t).astype(F32) for t in (gq, go, gi, gf)]]
    unnamed x7 -> x9, waiting for transfers between devices: 2.12 us -> 95 us
    pallas_call x0 -> x3, Pallas kernels: none -> 90.5 us  [the longest x1 40.5 us: body(): call(functools.partial(backward_kernel, factor), [(big, BF), ((width, 3 *...]
    all_gather x1 -> x2, blocking collectives: 46.5 us -> 82.4 us  [the longest x1 44.3 us: body(): gather(w_out)]
    unnamed x178 -> x15, local copies, waits for them, and re-layouts: 41.8 us -> 7.25 us
    reduce_sum x18 -> x0, other arithmetic: 18.9 us -> none  [the longest x2 5.82 us: feature_back(): jnp.sum(product, axis=-1, keepdims=True)]
    another operation x5 -> x1, local copies, waits for them, and re-layouts: 17.8 us -> 0.75 us  [body(): jnp.stack([gain_one, shift_one, gain_two, shift_two, bias_out], axis=1)]
  transfers between devices with their start and end apart: 7 -> 8, of which waited for: 3 -> 6; matrix products, arithmetic and copies ran while one was open for 24% -> 2% of each run, Pallas kernels for 0% -> 2%
where the time goes in v1:
time: 901 us; the launch traced here: 900 us
  waiting for transfers between devices  593 us (66%)
  blocking collectives  181 us (20%)
  Pallas kernels  90.5 us (10%)
  between operations  16.2 us (2%)
  local copies, waits for them, and re-layouts  9.49 us (1%)
  other arithmetic  9.24 us (1%)
    reduce_scatter x4, waiting for transfers between devices, body(): part = [scatter(t).astype(F32) for t in (gq, go, gi, gf)]  495 us
    unnamed x9, waiting for transfers between devices  95 us
    unnamed x2, blocking collectives  75.7 us
    all_gather x1, blocking collectives, body(): gather(w_out)  44.3 us
    pallas_call x1, Pallas kernels, body(): call(functools.partial(backward_kernel, factor), [(big, BF), ((width, 3 *...  40.5 us
    all_gather x1, blocking collectives, body(): gather(jnp.stack([gain_one, shift_one, gain_two, shift_two, bias_out], ax...  38.1 us
    pallas_call x1, Pallas kernels, body(): call(middle_kernel, [(big, BF), (big, F32), (big, F32), ((8, width), F32)...  28.8 us
    psum x1, blocking collectives, body(): counts = lax.psum(jnp.sum(onehot, axis=0), 'dp')  23.1 us
  transfers between devices with their start and end apart: 8, of which 6 were waited for; matrix products, arithmetic and copies ran while one was open for 2% of the time, Pallas kernels for 2%

profile of v1, /device:TPU:0, one launch (start us, length us, event | category | flops | bytes accessed | tf_op | source)
XLA Modules:
  0.0 900.1 jit_solution(4998620124857030868)
XLA Ops:
  7.2 0.7 all-gather.5.cloned.1.call-update
  8.0 0.7 all-gather.7.cloned.1.call-update
  8.7 0.7 all-gather.9.cloned.1.call-update
  10.1 23.1 %psum.7 = f32[4]{0:T(128)S(1)} all-reduce(f32[4]{0:T(128)S(1)} %compare_convert_fusion.1), channel_id=1, replica_groups=mesh['dp'=8,'fsdp'=4] {'dp'}, use_global_device_ids=true, to_apply=%region_0.1 | all-reduce | flops 4 | bytes 32 | tf_op jit(solution)/shard_map/psum | solution.py:373
  33.2 1.2 copy.33
  34.5 0.7 stack.23
  35.2 38.1 %all-gather = bf16[32,16,5]{1,2,0:T(8,128)(2,1)S(1)} all-gather(bf16[1,16,5]{1,2,0:T(8,128)(2,1)S(1)} %bitcast.24), channel_id=1, replica_groups=mesh['dp'=8,'fsdp'=4] {'dp','fsdp'}, dimensions={0}, use_global_device_ids=true | all-gather | bytes 5280 | tf_op jit(solution)/shard_map/all_gather | solution.py:366
  73.5 0.9 dynamic-update-slice
  74.3 37.1 %all-reduce.1 = bf16[2048]{0:T(1024)(128)(2,1)S(1)} all-reduce(bf16[2048]{0:T(1024)(128)(2,1)S(1)} %dynamic-update-slice), channel_id=1, replica_groups=mesh['dp'=8,'fsdp'=4] {'dp','fsdp'}, use_global_device_ids=true, to_apply=%add.1 | all-reduce | flops 2048 | bytes 8192
  111.4 0.6 broadcast_in_dim.40
  112.0 0.6 fusion
  114.0 0.6 pad_convert_fusion.prm_ref
  114.7 1.5 maximum_maximum_fusion.fx_ref
  116.2 44.3 %all_gather.20.wo_ref = bf16[512,512]{1,0:T(8,128)(2,1)} all-gather(bf16[16,512]{1,0:T(8,128)(2,1)S(1)} %copy-done), channel_id=1, replica_groups=mesh['dp'=8,'fsdp'=4] {'dp','fsdp'}, dimensions={0}, use_global_device_ids=true | all-gather | bytes 540672 | tf_op jit(solution)/shard_map/all_gather | solution.py:365
  160.5 21.2 %forward.1 = (bf16[1024,512]{1,0:T(8,128)(2,1)}, bf16[1024,512]{1,0:T(8,128)(2,1)}, bf16[1024,512]{1,0:T(8,128)(2,1)}, bf16[1024,512]{1,0:T(8,128)(2,1)}, bf16[1...) custom-call(bf16[1024,512]{1,0:T(8,128)(2,1)} %x_ref.5, ...), custom_call_target="tpu_custom_call" | custom-call | tf_op jit(solution)/shard_map/forward/pallas_call | solution.py:386
  181.7 3.4 all-gather.9.cloned.1.call-done.wf_ref
  185.6 28.8 %middle.1 = (bf16[1024,512]{1,0:T(8,128)(2,1)}, f32[1024,512]{1,0:T(8,128)}, f32[1024,512]{1,0:T(8,128)}, f32[8,512]{1,0:T(8,128)}, f32[1,2048]{1,0:T(1,128)}, /...) custom-call(bf16[1024,512]{1,0:T(8,128)(2,1)} %x_ref.5, ...), custom_call_target="tpu_custom_call" | custom-call | tf_op jit(solution)/shard_map/middle/pallas_call | solution.py:392
  214.4 40.5 %backward.1 = (bf16[1024,512]{1,0:T(8,128)(2,1)}, bf16[512,1536]{1,0:T(8,128)(2,1)}, f32[8,512]{1,0:T(8,128)}) custom-call(bf16[1024,512]{1,0:T(8,128)(2,1)} %x_ref.5, bf16[1024,512]{1,0:T(8,128)(2,1)} %get-tuple-element.34.h_ref, bf16[1024,512]{1,0:T(8,128)(2,1)} %get-tuple-element.35.q_ref, bf16[1024,512]{1,0:T(8,128)(2,1)} %get-tuple-element.36.k_ref, ...), custom_call_target="tpu_custom_call" | custom-call | tf_op jit(solution)/shard_map/backward/pallas_call | solution.py:401
  254.9 1.5 copy.35
  257.7 0.7 reduce-scatter.12.cloned.1.call-update
  258.4 0.7 reduce-scatter.14.cloned.1.call-update
  259.1 38.7 %all-reduce.2 = f32[2048]{0:T(1024)S(1)} all-reduce(f32[2048]{0:T(1024)S(1)} %bitcast.25), channel_id=7, replica_groups=mesh['dp'=8,'fsdp'=4] {'dp','fsdp'}, use_global_device_ids=true, to_apply=%region_8.9.clone | all-reduce | flops 2048 | bytes 16384
  298.4 90.5 %reduce-scatter.16.cloned.1.call-done = f32[16,8]{1,0:T(8,128)} async-done(((f32[512,8]{1,0:T(8,128)}), f32[16,8]{1,0:T(8,128)}) %reduce-scatter.16.cloned.1.call-update) | async-done | bytes 528
  388.9 1.0 fusion.3
  392.8 127.9 %reduce-scatter.10.cloned.1.call-done = bf16[16,512]{1,0:T(8,128)(2,1)} async-done(((bf16[512,512]{1,0:T(8,128)(2,1)}), bf16[16,512]{1,0:T(8,128)(2,1)}) %reduce-scatter.10.cloned.1.call-update) | async-done | bytes 16400 | tf_op jit(solution)/shard_map/reduce_scatter | solution.py:411
  520.7 1.3 convert_element_type.32
  522.0 96.7 %reduce-scatter.8.cloned.1.call-done = bf16[16,1536]{1,0:T(8,128)(2,1)} async-done(((bf16[512,1536]{1,0:T(8,128)(2,1)}), bf16[16,1536]{1,0:T(8,128)(2,1)}) %reduce-scatter.8.cloned.1.call-update) | async-done | bytes 49168 | tf_op jit(solution)/shard_map/reduce_scatter | solution.py:411
  618.8 1.4 convert_element_type.31
  620.2 136.5 %reduce-scatter.12.cloned.1.call-done = bf16[16,2048]{1,0:T(8,128)(2,1)} async-done(((bf16[512,2048]{1,0:T(8,128)(2,1)}), bf16[16,2048]{1,0:T(8,128)(2,1)}) %reduce-scatter.12.cloned.1.call-update) | async-done | bytes 65552 | tf_op jit(solution)/shard_map/reduce_scatter | solution.py:411
  756.8 1.5 convert_element_type.33
  758.3 133.5 %reduce-scatter.14.cloned.1.call-done = bf16[64,512]{1,0:T(8,128)(2,1)} async-done(((bf16[2048,512]{1,0:T(8,128)(2,1)}), bf16[64,512]{1,0:T(8,128)(2,1)}) %reduce-scatter.14.cloned.1.call-update) | async-done | bytes 65552 | tf_op jit(solution)/shard_map/reduce_scatter | solution.py:411
  891.8 1.5 convert_element_type.34
  (32 shorter events, 5.7 us)
Async XLA Ops:
  7.2 153.3 %all-gather.5.cloned.1.call-start = ((), (), s32[]{:S(2)}) async-start(), calls=%async_computation.5 | async-start | bytes 1622016 | tf_op jit(solution)/shard_map/all_gather | solution.py:365
  7.9 173.8 %all-gather.7.cloned.1.call-start = ((), (), s32[]{:S(2)}) async-start(), calls=%async_computation.6 | async-start | bytes 2162688 | tf_op jit(solution)/shard_map/all_gather | solution.py:365
  8.7 176.5 %all-gather.9.cloned.1.call-start = ((), (), s32[]{:S(2)}) async-start(), calls=%async_computation.7 | async-start | bytes 2162688 | tf_op jit(solution)/shard_map/all_gather | solution.py:365
  9.4 379.5 %reduce-scatter.16.cloned.1.call-start = ((), (), s32[]{:S(2)}) async-start(), calls=%async_computation.12 | async-start | bytes 270336
  34.5 81.7 %copy-start = (bf16[16,512]{1,0:T(8,128)(2,1)S(1)}, bf16[16,512]{1,0:T(8,128)(2,1)}, u32[]{:S(2)}) copy-start(bf16[16,512]{1,0:T(8,128)(2,1)} %param.18) | copy-start | bytes 49156
  256.4 264.3 %reduce-scatter.10.cloned.1.call-start = ((), (), s32[]{:S(2)}) async-start(), calls=%async_computation.9 | async-start | bytes 540672 | tf_op jit(solution)/shard_map/reduce_scatter | solution.py:411
  257.0 361.7 %reduce-scatter.8.cloned.1.call-start = ((), (), s32[]{:S(2)}) async-start(), calls=%async_computation.8 | async-start | bytes 1622016 | tf_op jit(solution)/shard_map/reduce_scatter | solution.py:411
  257.6 499.2 %reduce-scatter.12.cloned.1.call-start = ((), (), s32[]{:S(2)}) async-start(), calls=%async_computation.10 | async-start | bytes 2162688 | tf_op jit(solution)/shard_map/reduce_scatter | solution.py:411
  257.7 1.5 copy-start.1
  258.4 633.4 %reduce-scatter.14.cloned.1.call-start = ((), (), s32[]{:S(2)}) async-start(), calls=%async_computation.11 | async-start | bytes 2162688 | tf_op jit(solution)/shard_map/reduce_scatter | solution.py:411
Sparse Core Ops, SparseCore 0:
  10.9 57.7 all-gather.4
  71.5 55.4 all-gather.6
  129.9 55.1 all-gather.8
  256.6 132.3 reduce-scatter.15
  391.1 129.5 reduce-scatter.9
  525.8 92.9 reduce-scatter.7
  621.0 135.6 reduce-scatter.11
  759.1 132.6 reduce-scatter.13

commit v2 on v1

--- a/solution.py
+++ b/solution.py
@@ -30,6 +30,12 @@
     return lax.dot_general(left, right, (((0,), (0,)), ((), ())), preferred_element_type=F32)
 
 
+def unit_rows(rows):
+    row = lax.broadcasted_iota(jnp.int32, (rows, LANES), 0)
+    col = lax.broadcasted_iota(jnp.int32, (rows, LANES), 1)
+    return jnp.where(row == col, 1.0, 0.0).astype(BF)
+
+
 def lane_ids(rows, width=LANES):
     return lax.broadcasted_iota(jnp.int32, (rows, width), 1)
 
@@ -64,6 +70,195 @@
     row = lax.broadcasted_iota(jnp.int32, values.shape, 0)
     col = lax.broadcasted_iota(jnp.int32, values.shape, 1)
     return jnp.where(col >= row, values, 0.0).astype(BF)
+
+
+MESH_ID = pl.DeviceIdType.MESH
+
+
+class Place:
+    def __init__(self, nz):
+        dp, fs = lax.axis_index("dp"), lax.axis_index("fsdp")
+        self.nz = nz
+        self.z, self.y = lax.div(dp, 2), lax.rem(dp, 2)
+        self.x, self.c = lax.div(fs, 2), lax.rem(fs, 2)
+
+    def device(self, z=None, y=None, x=None, c=None):
+        z, y = self.z if z is None else z, self.y if y is None else y
+        x, c = self.x if x is None else x, self.c if c is None else c
+        return {"dp": z * 2 + y, "fsdp": x * 2 + c}
+
+    def up(self, k):
+        return lax.rem(self.z + k, self.nz)
+
+    def down(self, k):
+        return lax.rem(self.z + self.nz - k, self.nz)
+
+    def peers(self):
+        yield self.device(c=1 - self.c)
+        yield self.device(x=1 - self.x)
+        yield self.device(y=1 - self.y)
+        for k in range(1, self.nz):
+            yield self.device(z=self.up(k))
+
+    def barrier(self):
+        sem = pltpu.get_barrier_semaphore()
+        for peer in self.peers():
+            pl.semaphore_signal(sem, inc=1, device_id=peer, device_id_type=MESH_ID)
+        pl.semaphore_wait(sem, 2 + self.nz)
+
+
+def remote(src, dst, send, recv, peer):
+    return pltpu.make_async_remote_copy(
+        src_ref=src, dst_ref=dst, send_sem=send, recv_sem=recv, device_id=peer,
+        device_id_type=MESH_ID,
+    )
+
+
+class Gather:
+    def __init__(self, place, shard, whole, view, sems, m, y_first):
+        self.place, self.shard, self.whole, self.view = place, shard, whole, view
+        self.send, self.recv, self.own = sems
+        self.m = m
+        self.y_first = y_first
+
+    def at(self, *index):
+        return self.whole.at[(*index, *self.view)]
+
+    def hops(self, stage):
+        p = self.place
+        every = slice(None)
+        if stage == 0:
+            src = self.shard.at[self.view]
+            for k in range(1, p.nz):
+                yield src, self.at(p.z, p.y, p.x, p.c), self.at(p.down(k), p.y, p.x, p.c), p.device(z=p.up(k))
+        elif stage == 3:
+            mine = self.at(every, every, every, p.c)
+            yield mine, mine, self.at(every, every, every, 1 - p.c), p.device(c=1 - p.c)
+        elif self.y_first:
+            if stage == 1:
+                mine = self.at(every, p.y, p.x, p.c)
+                yield mine, mine, self.at(every, 1 - p.y, p.x, p.c), p.device(y=1 - p.y)
+            else:
+                mine = self.at(every, every, p.x, p.c)
+                yield mine, mine, self.at(every, every, 1 - p.x, p.c), p.device(x=1 - p.x)
+        else:
+            if stage == 1:
+                mine = self.at(every, p.y, p.x, p.c)
+                yield mine, mine, self.at(every, p.y, 1 - p.x, p.c), p.device(x=1 - p.x)
+            else:
+                mine = self.at(every, p.y, every, p.c)
+                yield mine, mine, self.at(every, 1 - p.y, every, p.c), p.device(y=1 - p.y)
+
+    def copies(self, stage, arriving):
+        for k, (src, dst, land, peer) in enumerate(self.hops(stage)):
+            yield remote(
+                src, land if arriving else dst, self.send.at[self.m, stage, k],
+                self.recv.at[self.m, stage, k], peer,
+            )
+
+    def local(self):
+        p = self.place
+        return pltpu.make_async_copy(
+            self.shard.at[self.view], self.at(p.z, p.y, p.x, p.c), self.own.at[self.m]
+        )
+
+    def start(self):
+        for copy in self.copies(0, False):
+            copy.start()
+        self.local().start()
+
+    def arrive(self, stage):
+        for copy in self.copies(stage, True):
+            copy.wait_recv()
+
+    def step(self, stage):
+        self.arrive(stage - 1)
+        if stage == 1:
+            self.local().wait()
+        for copy in self.copies(stage, False):
+            copy.start()
+
+    def drain(self):
+        for stage in range(4):
+            for copy in self.copies(stage, False):
+                copy.wait_send()
+
+
+class Reduce:
+    def __init__(self, place, source, bufs, sems, load, write):
+        self.place, self.source = place, source
+        self.l0, self.r0, self.l1, self.r1, self.l2, self.r2, self.r3 = bufs
+        self.send, self.recv, self.own = sems
+        self.load, self.write = load, write
+
+    def hops(self, stage, c):
+        p = self.place
+        every = slice(None)
+        if stage == 0:
+            yield self.source.at[c, every, every, every, 1 - p.c], self.r0.at[c], self.r0.at[c], p.device(c=1 - p.c)
+        elif stage == 1:
+            yield self.l0.at[c, every, every, 1 - p.x], self.r1.at[c], self.r1.at[c], p.device(x=1 - p.x)
+        elif stage == 2:
+            yield self.l1.at[c, every, 1 - p.y], self.r2.at[c], self.r2.at[c], p.device(y=1 - p.y)
+        else:
+            for k in range(1, p.nz):
+                yield self.l2.at[c, p.up(k)], self.r3.at[c, k - 1], self.r3.at[c, k - 1], p.device(z=p.up(k))
+
+    def copies(self, stage, c):
+        for k, (src, dst, _, peer) in enumerate(self.hops(stage, c)):
+            yield remote(src, dst, self.send.at[c, stage, k], self.recv.at[c, stage, k], peer)
+
+    def local(self, c):
+        p = self.place
+        every = slice(None)
+        return pltpu.make_async_copy(
+            self.source.at[c, every, every, every, p.c], self.l0.at[c], self.own.at[c]
+        )
+
+    def begin(self, stage, c):
+        for copy in self.copies(stage, c):
+            copy.start()
+
+    def step(self, stage, c):
+        p = self.place
+        if stage == 0:
+            self.begin(0, c)
+            if self.load:
+                self.local(c).start()
+            return
+        for copy in self.copies(stage - 1, c):
+            copy.wait_recv()
+        if stage == 1:
+            if self.load:
+                self.local(c).wait()
+                mine = self.l0[c]
+            else:
+                mine = self.source[c, :, :, :, p.c]
+            self.l0[c] = (mine.astype(F32) + self.r0[c].astype(F32)).astype(BF)
+        elif stage == 2:
+            self.l1[c] = (self.l0[c, :, :, p.x].astype(F32) + self.r1[c].astype(F32)).astype(BF)
+        elif stage == 3:
+            self.l2[c] = (self.l1[c, :, p.y].astype(F32) + self.r2[c].astype(F32)).astype(BF)
+        else:
+            total = self.l2[c, p.z].astype(F32)
+            for k in range(p.nz - 1):
+                total = total + self.r3[c, k].astype(F32)
+            self.write(c, total)
+            return
+        self.begin(stage, c)
+
+    def drain(self, c):
+        for stage in range(4):
+            for copy in self.copies(stage, c):
+                copy.wait_send()
+
+    @staticmethod
+    def shapes(n, nz, rows, cols):
+        return [
+            ((n, nz, 2, 2, rows, cols), BF), ((n, nz, 2, 2, rows, cols), BF),
+            ((n, nz, 2, rows, cols), BF), ((n, nz, 2, rows, cols), BF),
+            ((n, nz, rows, cols), BF), ((n, nz, rows, cols), BF), ((n, nz - 1, rows, cols), BF),
+        ]
 
 
 def project_rows(i, x_ref, wq, prm_ref, h_ref, q_ref, k_ref, v_ref, factor):
@@ -145,15 +340,15 @@
 
 
 def middle_kernel(
-    x_ref, attr_ref, cot_ref, wo_ref, wi_ref, wf_ref, prm_ref, bin_ref, seq_ref,
-    act_ref, dy_ref, datt_ref, gprm_ref, gbin_ref, gf_ref, gi_ref, go_ref,
-    hid_ref, du_ref, h_ref, gr_ref, dor_ref,
+    x_ref, attr_ref, cot_ref, wo_ref, wi_ref, wf_ref, prm_ref, seq_ref,
+    act_ref, dy_ref, datt_ref, gprm_ref, g_ref,
+    hid_ref, du_ref, h_ref, gr_ref, dor_ref, bin_ref,
 ):
     length, width = x_ref.shape
     hidden = wi_ref.shape[1]
-    chunk = 512
+    chunk = width
     gprm_ref[...] = jnp.zeros_like(gprm_ref)
-    gbin_ref[...] = jnp.zeros_like(gbin_ref)
+    bin_ref[...] = dot_bt(unit_rows(8), wf_ref[:, width:])
 
     def rows(t, carry):
         rows = tile_at(t)
@@ -170,7 +365,7 @@
         for c in range(hidden // chunk):
             cs = slice(c * chunk, (c + 1) * chunk)
             wi = wi_ref[:, cs]
-            wf = wf_ref[cs, :]
+            wf = wf_ref[cs, :width]
             u = dot(h, wi) + bin_ref[0:1, cs]
             cdf = 0.5 + 0.5 * lax.erf(u * math.sqrt(0.5))
             slope = cdf + u * jnp.exp2(u * u * (-0.5 * LOG2E)) * (1.0 / math.sqrt(2.0 * math.pi))
@@ -179,7 +374,7 @@
             out = out + dot(hid, wf)
             du = (dot_bt(gr, wf) * slope).astype(BF)
             du_ref[rows, cs] = du
-            gbin_ref[0:1, cs] += jnp.sum(du.astype(F32), axis=0, keepdims=True)
+            gprm_ref[5 + c : 6 + c, :] += jnp.sum(du.astype(F32), axis=0, keepdims=True)
             dh = dh + dot_bt(du, wi)
         act_ref[rows, :] = out.astype(BF)
         gprm_ref[2:3, :] += jnp.sum(dh * unit, axis=0, keepdims=True)
@@ -195,16 +390,22 @@
     lax.fori_loop(0, length // TILE, rows, 0)
 
     def grad_f(c, carry):
-        cs = tile_at(c)
-        gf_ref[cs, :] = dot_at(hid_ref[:, cs], gr_ref[...]).astype(gf_ref.dtype)
+        grad = dot_at(hid_ref[:, tile_at(c)], gr_ref[...]).astype(BF)
+        grad = grad.reshape(4, 4, 16, width)
+        for q in range(4):
+            g_ref[q, c] = grad[:, q]
         return carry
 
     lax.fori_loop(0, hidden // TILE, grad_f, 0)
 
     def grad_i(c, carry):
         cs = tile_at(c)
-        gi_ref[cs, :] = dot_at(h_ref[:, cs], du_ref[...]).astype(gi_ref.dtype)
-        go_ref[cs, :] = dot_at(attr_ref[:, cs], dor_ref[...]).astype(go_ref.dtype)
+        at = pl.ds(c * 4, 4)
+        grad = dot_at(h_ref[:, cs], du_ref[...]).astype(BF)
+        for k in range(hidden // chunk):
+            g_ref[4 + k, at] = grad[:, k * chunk : (k + 1) * chunk].reshape(4, 4, 16, width)
+        grad = dot_at(attr_ref[:, cs], dor_ref[...]).astype(BF)
+        g_ref[4 + hidden // chunk, at] = grad.reshape(4, 4, 16, width)
         return carry
 
     lax.fori_loop(0, width // TILE, grad_i, 0)
@@ -212,7 +413,7 @@
 
 def back_pair(
     p, factor, q_ref, k_ref, v_ref, pq_ref, pk_ref, att_ref, den_ref, datt_ref, fx_ref,
-    ht_ref, dqkv_ref, gq_ref, dn_ref, acc_ref,
+    ht_ref, dqkv_ref, dn_ref, acc_ref, tick, store,
 ):
     length = q_ref.shape[0]
     feats = fx_ref.shape[1]
@@ -299,9 +500,10 @@
                     both = acc_ref[2, rows, :] + dv
                     start = pl.multiple_of(p * LANES + 2 * width, LANES)
                     dqkv_ref[rows, pl.ds(start, LANES)] = both.astype(BF)
+                tick((hh * blocks + b) * (BLOCK // TILE) + i)
     for at in range(3):
         where = pl.ds(pl.multiple_of(p * LANES + at * width, LANES), LANES)
-        gq_ref[:, where] = dot(ht_ref[...], dqkv_ref[:, where]).astype(gq_ref.dtype)
+        store(at, where, dot(ht_ref[...], dqkv_ref[:, where]).astype(BF))
 
 
 def input_rows(t, x_ref, wq, prm_ref, dqkv_ref, dy_ref, out_ref, gprm_ref):
@@ -313,6 +515,12 @@
     out_ref[rows, :] = (dy_ref[rows, :] + norm_back(dh, unit, inv, prm_ref[0:1, :])).astype(BF)
 
 
+def flip_rows(h_ref, ht_ref):
+    for t in range(h_ref.shape[0] // TILE):
+        rows = slice(t * TILE, (t + 1) * TILE)
+        ht_ref[:, rows] = h_ref[rows, :].T
+
+
 def backward_kernel(
     factor, x_ref, h_ref, q_ref, k_ref, v_ref, pq_ref, pk_ref, att_ref, den_ref, datt_ref, dy_ref,
     wq_ref, fx_ref, prm_ref, gin_ref,
@@ -320,14 +528,15 @@
     ht_ref, dqkv_ref, dn_ref, acc_ref,
 ):
     gprm_ref[...] = gin_ref[...]
-    for t in range(x_ref.shape[0] // TILE):
-        rows = slice(t * TILE, (t + 1) * TILE)
-        ht_ref[:, rows] = h_ref[rows, :].T
+    flip_rows(h_ref, ht_ref)
+
+    def store(at, where, value):
+        gq_ref[:, where] = value
 
     def pair(p, carry):
         back_pair(
             p, factor, q_ref, k_ref, v_ref, pq_ref, pk_ref, att_ref, den_ref, datt_ref, fx_ref,
-            ht_ref, dqkv_ref, gq_ref, dn_ref, acc_ref,
+            ht_ref, dqkv_ref, dn_ref, acc_ref, lambda j: None, store,
         )
         return carry
 
@@ -340,17 +549,267 @@
     lax.fori_loop(0, x_ref.shape[0] // TILE, rows, 0)
 
 
-def call(kernel, outs, scratch, name):
+def gather_forward_kernel(
+    nz, factor, x_ref, wqs_ref, wos_ref, wis_ref, wfs_ref, fx_ref,
+    h_ref, q_ref, k_ref, v_ref, pq_ref, pk_ref, att_ref, attr_ref, den_ref, prm_ref, seq_ref,
+    wq_ref, wo_ref, wi_ref, wf_ref,
+    send, recv, own,
+):
+    length, width = x_ref.shape
+    place = Place(nz)
+    every = slice(None)
+    sems = (send, recv, own)
+    cut = width * 3 // 2
+    half = wis_ref.shape[1] // 2
+    low, high = slice(0, 32), slice(32, 64)
+    q0 = Gather(place, wqs_ref, wq_ref, (every, slice(0, cut)), sems, 0, True)
+    q1 = Gather(place, wqs_ref, wq_ref, (every, slice(cut, wqs_ref.shape[1])), sems, 1, False)
+    o = Gather(place, wos_ref, wo_ref, (every, every), sems, 2, True)
+    i0 = Gather(place, wis_ref, wi_ref, (every, slice(0, half)), sems, 3, True)
+    i1 = Gather(place, wis_ref, wi_ref, (every, slice(half, 2 * half)), sems, 4, False)
+    f0 = Gather(place, wfs_ref, wf_ref, (low, every), sems, 5, True)
+    f1 = Gather(place, wfs_ref, wf_ref, (high, every), sems, 6, False)
+    first, rest = (q0, q1), (o, i0, i1, f0, f1)
+    place.barrier()
+    for g in (*first, *rest):
+        g.start()
+    for stage in (1, 2, 3):
+        for g in first:
+            g.step(stage)
+    for g in rest:
+        g.step(1)
+    for g in first:
+        g.arrive(3)
+
+    wqx = wq_ref[...].reshape(width, wqs_ref.shape[1])
+    small = wqx[:, 3 * width :]
+    prm_ref[...] = dot_bt(unit_rows(8), small)
+    nf = 4
+    me = lax.axis_index("dp") * nf + lax.axis_index("fsdp")
+    row = lax.broadcasted_iota(jnp.int32, small.shape, 0)
+    lane = lane_ids(width).astype(F32)
+    peer = lax.div(row, 16)
+    ids = small[:, 5:6].astype(F32)
+    hit = (lane == ids) & (lax.rem(row, 16) == 0)
+    counts = jnp.sum(
+        jnp.where(hit & (lax.rem(peer, nf) == lax.axis_index("fsdp")), 1.0, 0.0),
+        axis=0, keepdims=True,
+    )
+    mine = jnp.sum(jnp.where(hit & (peer == me), 1.0, 0.0), axis=0, keepdims=True)
+    size = jnp.sum(counts * mine, axis=1, keepdims=True)
+    groups = jnp.sum(jnp.where(counts > 0.5, 1.0, 0.0), axis=1, keepdims=True)
+    members = lax.axis_size("dp")
+    seq_ref[...] = jnp.broadcast_to(members / (groups * size), seq_ref.shape)
+
+    def rows(i, carry):
+        wq = wq_ref[..., : 3 * width].reshape(width, 3 * width)
+        project_rows(i, x_ref, wq, prm_ref, h_ref, q_ref, k_ref, v_ref, factor)
+        return carry
+
+    lax.fori_loop(0, length // TILE, rows, 0)
+    for g in rest:
+        g.step(2)
+
+    def pair(p, carry):
+        attend_pair(p, q_ref, k_ref, v_ref, fx_ref, pq_ref, pk_ref, att_ref, attr_ref, den_ref)
+        return carry
+
+    pairs = width // LANES
+    lax.fori_loop(0, pairs - 2, pair, 0)
+    for g in (o, i0, i1):
+        g.step(3)
+    lax.fori_loop(pairs - 2, pairs, pair, 0)
+    for g in (f0, f1):
+        g.step(3)
+    for g in rest:
+        g.arrive(3)
+    for g in (*first, *rest):
+        g.drain()
+
+
+def reduce_backward_kernel(
+    nz, factor, x_ref, h_ref, q_ref, k_ref, v_ref, pq_ref, pk_ref, att_ref, den_ref, datt_ref,
+    dy_ref, wq_ref, fx_ref, prm_ref, gin_ref, g_ref,
+    out_ref, parts_ref, partq_ref, total_ref,
+    ht_ref, dqkv_ref, dn_ref, acc_ref, gq_ref, sum_ref, got_ref, *rest,
+):
+    place = Place(nz)
+    bufs, bufs_q = rest[:7], rest[7:14]
+    sems, sems_q, (send, recv) = rest[14:17], rest[17:20], rest[20:]
+    width = x_ref.shape[1]
+    chunks = g_ref.shape[0]
+    pairs = width // LANES
+
+    def write(c, value):
+        parts_ref[c] = value
+
+    def write_q(c, value):
+        for at in range(3):
+            where = pl.ds(pl.multiple_of(c * LANES + at * width, LANES), LANES)
+            partq_ref[:, where] = value[:, at * LANES : (at + 1) * LANES]
+
+    big = Reduce(place, g_ref, bufs, sems, True, write)
+    own = Reduce(place, gq_ref, bufs_q, sems_q, False, write_q)
+
+    place.barrier()
+
+    def begin(c, carry):
+        big.step(0, c)
+        return carry
+
+    lax.fori_loop(0, chunks, begin, 0)
+    sum_ref[0] = gin_ref[...]
+    flip_rows(h_ref, ht_ref)
+
+    def pair(p, carry):
+        def advance(ring, stage, c, count):
+            @pl.when((c >= 0) & (c < count))
+            def _():
+                ring.step(stage, c)
+
+        def tick(j):
+            if j % 2:
+                advance(big, 2, 4 * p + (j - 7) // 2, chunks)
+            else:
+                advance(big, 1, 4 * p + j // 2 - 1, chunks)
+                advance(big, 3, 4 * p + j // 2 - 5, chunks)
+                advance(big, 4, 4 * p + j // 2 - 7, chunks)
+            if j == 1:
+                advance(own, 1, p - 1, pairs)
+                advance(own, 3, p - 2, pairs)
+            if j == 5:
+                advance(own, 2, p - 1, pairs)
+                advance(own, 4, p - 2, pairs)
+
+        def store(at, where, value):
+            shape = (nz, 2, 2, 2, 16, LANES)
+            gq_ref[p, ..., at * LANES : (at + 1) * LANES] = value.reshape(shape)
+
+        back_pair(
+            p, factor, q_ref, k_ref, v_ref, pq_ref, pk_ref, att_ref, den_ref, datt_ref, fx_ref,
+            ht_ref, dqkv_ref, dn_ref, acc_ref, tick, store,
+        )
+        own.step(0, p)
+        return carry
+
+    lax.fori_loop(0, pairs, pair, 0)
+    last = pairs - 1
+    small = sum_ref.at[0]
+
+    def rows(t, carry):
+        wq = wq_ref[:, : 3 * width]
+        input_rows(t, x_ref, wq, prm_ref, dqkv_ref, dy_ref, out_ref, small)
+        return carry
+
+    tiles = x_ref.shape[0] // TILE
+    lax.fori_loop(0, 1, rows, 0)
+    own.step(1, last)
+    own.step(3, last - 1)
+    lax.fori_loop(1, tiles - 1, rows, 0)
+    own.step(2, last)
+    own.step(4, last - 1)
+    lax.fori_loop(tiles - 1, tiles, rows, 0)
+
+    def exchange(stage):
+        if stage < 3:
+            at = [(0, place.device(c=1 - place.c)), (1, place.device(x=1 - place.x)),
+                  (2, place.device(y=1 - place.y))][stage]
+            hops = [at]
+        else:
+            hops = [(2 + k, place.device(z=place.up(k))) for k in range(1, nz)]
+        for slot, peer in hops:
+            yield slot, remote(
+                sum_ref.at[stage], got_ref.at[slot], send.at[slot], recv.at[slot], peer
+            )
+
+    def combine(stage):
+        value = sum_ref[stage]
+        for slot, copy in exchange(stage):
+            copy.wait_recv()
+            value = value + got_ref[slot]
+        return value
+
+    for _, copy in exchange(0):
+        copy.start()
+    own.step(3, last)
+    for stage in range(3):
+        sum_ref[stage + 1] = combine(stage)
+        for _, copy in exchange(stage + 1):
+            copy.start()
+        if stage == 1:
+            own.step(4, last)
+    total_ref[...] = combine(3)
+    for stage in range(4):
+        for _, copy in exchange(stage):
+            copy.wait_send()
+
+    def drain(c, carry):
+        big.drain(c)
+        return carry
+
+    lax.fori_loop(0, chunks, drain, 0)
+
+    def drain_q(c, carry):
+        own.drain(c)
+        return carry
+
+    lax.fori_loop(0, pairs, drain_q, 0)
+
+
+ANY = pl.BlockSpec(memory_space=pl.ANY)
+VM = pl.BlockSpec(memory_space=pltpu.VMEM)
+
+
+def call(kernel, outs, scratch, name, ins=None, out_specs=None, collective=None):
+    extra = {} if ins is None else {"in_specs": ins, "out_specs": out_specs}
+    params = {} if collective is None else {"collective_id": collective, "has_side_effects": True}
     return pl.pallas_call(
         kernel,
         out_shape=[jax.ShapeDtypeStruct(s, d) for s, d in outs],
-        scratch_shapes=[pltpu.VMEM(s, d) for s, d in scratch],
-        compiler_params=pltpu.CompilerParams(vmem_limit_bytes=60 * 2**20),
+        scratch_shapes=[pltpu.SemaphoreType.DMA(s) if d is None else pltpu.VMEM(s, d) for s, d in scratch],
+        compiler_params=pltpu.CompilerParams(vmem_limit_bytes=60 * 2**20, **params),
         name=name,
+        **extra,
     )
 
 
-def body(
+def padded_features(fm):
+    heads, feats, _ = fm.shape
+    zero = jnp.zeros_like(fm)
+    even = (jnp.arange(heads) % 2 == 0)[:, None, None]
+    return jnp.concatenate(
+        [jnp.where(even, fm, zero), jnp.where(even, zero, fm), jnp.ones((heads, feats, LANES), BF)],
+        axis=-1,
+    )
+
+
+def middle(tokens, attr, cotangent, wo, wi, wf, prm, seq_weight):
+    length, width = tokens.shape
+    hidden = wi.shape[1]
+    big, deep = (length, width), (length, hidden)
+    chunks = 5 + hidden // width
+    return call(
+        middle_kernel,
+        [(big, BF), (big, F32), (big, F32), ((16, width), F32), ((chunks, width // 64, 4, 16, width), BF)],
+        [(deep, BF), (deep, BF), (big, BF), (big, BF), (big, BF), ((8, hidden), F32)],
+        "middle",
+    )(tokens, attr, cotangent, wo, wi, wf, prm, seq_weight)
+
+
+def forward_outs(length, width, heads, feats):
+    big = (length, width)
+    deep = (length, heads * feats)
+    return [(big, BF)] * 4 + [(deep, BF)] * 2 + [(big, F32), (big, BF), (big, F32)]
+
+
+def backward_scratch(length, width):
+    return [
+        ((width, length), BF), ((length, 3 * width), BF),
+        ((2, length, 2 * LANES), BF), ((3, length, LANES), F32),
+    ]
+
+
+def plain_body(
     tokens, cotangent, group_id, w_qkv, w_out, w_ffn_in, w_ffn_out,
     gain_one, shift_one, gain_two, shift_two, bias_in, bias_out, feature_matrix,
 ):
@@ -365,7 +824,7 @@
     wq, wo, wi, wf = gather(w_qkv), gather(w_out), gather(w_ffn_in), gather(w_ffn_out)
     prm = gather(jnp.stack([gain_one, shift_one, gain_two, shift_two, bias_out], axis=1))
     prm = jnp.pad(prm.T.astype(F32), ((0, 3), (0, 0)))
-    full_bin = gather(bias_in).astype(F32)[None]
+    wf = jnp.concatenate([wf, jnp.pad(gather(bias_in)[:, None], ((0, 0), (0, LANES - 1)))], axis=1)
 
     slice_seqs = lax.axis_size("dp") * group_id.shape[0]
     labels = jnp.arange(slice_seqs // 2, dtype=jnp.int32)
@@ -373,47 +832,104 @@
     counts = lax.psum(jnp.sum(onehot, axis=0), "dp")
     group_size = jnp.sum(onehot * counts[None, :], axis=-1)
     groups = jnp.sum((counts > 0.5).astype(F32))
-    seq_weight = jnp.broadcast_to((slice_seqs / (groups * group_size))[:, None], (1, LANES))
-
-    fm = feature_matrix
-    zero = jnp.zeros_like(fm)
-    even = (jnp.arange(heads) % 2 == 0)[:, None, None]
-    fx = jnp.concatenate(
-        [jnp.where(even, fm, zero), jnp.where(even, zero, fm), jnp.ones((heads, feats, LANES), BF)],
-        axis=-1,
-    )
-    big = (length, width)
+    seq_weight = jnp.broadcast_to((slice_seqs / (groups * group_size))[:, None], (8, LANES))
+
+    fx = padded_features(feature_matrix)
     h1, q, k, v, pq, pk, att, attr, den = call(
         functools.partial(forward_kernel, factor),
-        [(big, BF)] * 4 + [((length, heads * feats), BF)] * 2 + [(big, F32), (big, BF), (big, F32)],
-        [],
-        "forward",
+        forward_outs(length, width, heads, feats), [], "forward",
     )(tokens, wq, prm, fx)
-    act, dy, datt, gprm, gbin, gf, gi, go = call(
-        middle_kernel,
-        [
-            (big, BF), (big, F32), (big, F32), ((8, width), F32), ((1, hidden), F32),
-            ((hidden, width), BF), ((width, hidden), BF), ((width, width), BF),
-        ],
-        [((length, hidden), BF), ((length, hidden), BF), (big, BF), (big, BF), (big, BF)],
-        "middle",
-    )(tokens, attr, cotangent, wo, wi, wf, prm, full_bin, seq_weight)
+    act, dy, datt, gprm, grads = middle(tokens, attr, cotangent, wo, wi, wf, prm, seq_weight)
     input_grad, gq, gprm = call(
         functools.partial(backward_kernel, factor),
-        [(big, BF), ((width, 3 * width), BF), ((8, width), F32)],
+        [((length, width), BF), ((width, 3 * width), BF), ((16, width), F32)],
+        backward_scratch(length, width), "backward",
+    )(tokens, h1, q, k, v, pq, pk, att, den, datt, dy, wq, fx, prm, gprm)
+    grads = grads.reshape(-1, width // 16, 16, width)
+    gf = grads[:4].transpose(1, 0, 2, 3).reshape(hidden, width)
+    gi = grads[4:-1].transpose(1, 2, 0, 3).reshape(width, hidden)
+    go = grads[-1].reshape(width, width)
+    small = scatter(gprm[:8].T)
+    gbin = scatter(gprm[5 : 5 + hidden // width].reshape(hidden))
+    part = [scatter(t).astype(F32) for t in (gq, go, gi, gf)]
+    return (act, input_grad, *part, *(small[:, i] for i in range(4)), gbin, small[:, 4])
+
+
+def ring_body(
+    tokens, cotangent, group_id, w_qkv, w_out, w_ffn_in, w_ffn_out,
+    gain_one, shift_one, gain_two, shift_two, bias_in, bias_out, feature_matrix,
+):
+    length, width = tokens.shape
+    heads, feats, head_size = feature_matrix.shape
+    hidden = w_ffn_in.shape[1]
+    factor = head_size ** (-0.25)
+    nz = lax.axis_size("dp") // 2
+    ids = jnp.broadcast_to(group_id.astype(BF), gain_one.shape)
+    small = jnp.stack([gain_one, shift_one, gain_two, shift_two, bias_out, ids], axis=1)
+    wqs = jnp.concatenate([w_qkv, jnp.pad(small, ((0, 0), (0, LANES - 6)))], axis=1)
+    wfs = jnp.concatenate([w_ffn_out, jnp.pad(bias_in[:, None], ((0, 0), (0, LANES - 1)))], axis=1)
+    fx = padded_features(feature_matrix)
+    wide = 3 * width + LANES
+    grid = (nz, 2, 2, 2)
+    h1, q, k, v, pq, pk, att, attr, den, prm, seq, wq, wo, wi, wf = call(
+        functools.partial(gather_forward_kernel, nz, factor),
         [
-            ((width, length), BF), ((length, 3 * width), BF),
-            ((2, length, 2 * LANES), BF), ((3, length, LANES), F32),
+            *forward_outs(length, width, heads, feats), ((8, width), F32), ((8, LANES), F32),
+            ((*grid, 16, wide), BF), ((*grid, 16, width), BF), ((*grid, 16, hidden), BF),
+            ((*grid, 64, width + LANES), BF),
         ],
-        "backward",
-    )(tokens, h1, q, k, v, pq, pk, att, den, datt, dy, wq, fx, prm, gprm)
-    small = scatter(gprm.T)
-    part = [scatter(t).astype(F32) for t in (gq, go, gi, gf)]
-    return (act, input_grad, *part, *(small[:, i] for i in range(4)), scatter(gbin[0]), small[:, 4])
+        [((7, 4, nz - 1), None), ((7, 4, nz - 1), None), ((7,), None)],
+        "gather_forward",
+        [VM, ANY, ANY, ANY, ANY, VM],
+        [VM] * 12 + [ANY] * 3,
+        0,
+    )(tokens, wqs, w_out, w_ffn_in, wfs, fx)
+    wq = wq.reshape(width, wide)
+    act, dy, datt, gprm, grads = middle(
+        tokens, attr, cotangent, wo.reshape(width, width), wi.reshape(width, hidden),
+        wf.reshape(hidden, width + LANES), prm, seq,
+    )
+    chunks = grads.shape[0]
+    pairs = width // LANES
+    input_grad, parts, gq, total = call(
+        functools.partial(reduce_backward_kernel, nz, factor),
+        [
+            ((length, width), BF), ((chunks, 16, width), F32), ((16, 3 * width), F32),
+            ((16, width), F32),
+        ],
+        [
+            *backward_scratch(length, width),
+            ((pairs, *grid, 16, 3 * LANES), BF),
+            ((4, 16, width), F32), ((2 + nz, 16, width), F32),
+            *Reduce.shapes(chunks, nz, 16, width),
+            *Reduce.shapes(pairs, nz, 16, 3 * LANES),
+            ((chunks, 4, nz - 1), None), ((chunks, 4, nz - 1), None), ((chunks,), None),
+            ((pairs, 4, nz - 1), None), ((pairs, 4, nz - 1), None), ((pairs,), None),
+            ((2 + nz,), None), ((2 + nz,), None),
+        ],
+        "reduce_backward",
+        [VM] * 15 + [ANY],
+        [VM] * 4,
+        1,
+    )(tokens, h1, q, k, v, pq, pk, att, den, datt, dy, wq, fx, prm, gprm, grads.reshape(chunks, *grid, 16, width))
+    gf = parts[:4].reshape(64, width)
+    gi = parts[4:-1].transpose(1, 0, 2).reshape(16, hidden)
+    go = parts[-1]
+    me = lax.axis_index("dp") * lax.axis_size("fsdp") + lax.axis_index("fsdp")
+    vec = [lax.dynamic_slice(total[i], (me * 16,), (16,)) for i in range(5)]
+    gbin = lax.dynamic_slice(total[5 : 5 + hidden // width].reshape(hidden), (me * 64,), (64,))
+    return (act, input_grad, gq, go, gi, gf, *vec[:4], gbin, vec[4])
 
 
 def solution(mesh):
     rows, vec = P(AXES, None), P(AXES)
+    devices = mesh.shape["dp"] * mesh.shape["fsdp"]
+
+    def body(*args):
+        width = args[0].shape[1]
+        ring = mesh.shape["fsdp"] == 4 and mesh.shape["dp"] % 2 == 0 and width == 16 * devices
+        return (ring_body if ring else plain_body)(*args)
+
     return jax.shard_map(
         body,
         mesh=mesh,

time: 901 us -> 186 us (0.21)
  waiting for transfers between devices: 593 us -> 0 us
  blocking collectives: 181 us -> 0 us
  Pallas kernels: 90.5 us -> 168 us
  between operations: 16.2 us -> 1.46 us
    reduce_scatter x4 -> x0, waiting for transfers between devices: 495 us -> none  [body(): part = [scatter(t).astype(F32) for t in (gq, go, gi, gf)]]
    unnamed x9 -> x0, waiting for transfers between devices: 95 us -> none
    all_gather x2 -> x0, blocking collectives: 82.4 us -> none  [the longest x1 44.3 us: body(): gather(w_out)]
    pallas_call x3, Pallas kernels: 90.5 us -> 168 us  [the longest x1 80 us: ring_body(): call(functools.partial(reduce_backward_kernel, nz, factor), [((length, wi...]
    unnamed x2 -> x0, blocking collectives: 75.7 us -> none
    psum x1 -> x0, blocking collectives: 23.1 us -> none  [body(): counts = lax.psum(jnp.sum(onehot, axis=0), 'dp')]
  transfers between devices with their start and end apart: 8 -> 0, of which waited for: 6 -> 0; matrix products, arithmetic and copies ran while one was open for 2% -> 0% of each run, Pallas kernels for 2% -> 0%
where the time goes in v2:
time: 186 us; the launch traced here: 185 us
  Pallas kernels  168 us (90%)
  local copies, waits for them, and re-layouts  12.6 us (7%)
  other arithmetic  2.89 us (2%)
    pallas_call x1, Pallas kernels, ring_body(): call(functools.partial(reduce_backward_kernel, nz, factor), [((length, wi...  80 us
    pallas_call x1, Pallas kernels, ring_body(): call(functools.partial(gather_forward_kernel, nz, factor), [*forward_outs...  58.9 us
    pallas_call x1, Pallas kernels, middle(): call(middle_kernel, [(big, BF), (big, F32), (big, F32), ((16, width), F32...  29.5 us
    unnamed x23, local copies, waits for them, and re-layouts  4.98 us

profile of v2, /device:TPU:0, one launch (start us, length us, event | category | flops | bytes accessed | tf_op | source)
XLA Modules:
  0.0 185.3 jit_solution(11456860139126378892)
XLA Ops:
  0.7 1.3 copy.40
  1.9 0.0 copy-start.4
  1.9 0.0 copy-start.5
  2.0 0.0 copy-start.6
  2.0 0.0 copy-start.7
  2.0 0.0 copy-start.8
  2.0 0.0 copy-start.2
  2.0 0.1 broadcast_select_fusion.1
  2.2 1.5 maximum_maximum_fusion.fx_ref
  3.6 0.1 copy.39
  3.8 0.6 fusion.2.wfs_ref
  5.1 0.1 copy.34
  5.2 0.1 copy.35
  5.3 0.1 copy.36
  5.4 0.1 copy.37
  5.5 0.1 copy.38
  5.6 0.1 stack.23
  5.7 0.6 fusion.3.wqs_ref
  6.3 58.9 %gather_forward.1 = (bf16[1024,512]{1,0:T(8,128)(2,1)}, bf16[1024,512]{1,0:T(8,128)(2,1)}, bf16[1024,512]{1,0:T(8,128)(2,1)}, bf16[1024,512]{1,0:T(8,128)(2,1)},...) custom-call(bf16[1024,512]{1,0:T(8,128)(2,1)} %x_ref.5, ...), custom_call_target="tpu_custom_call" | custom-call | tf_op jit(solution)/shard_map/gather_forward/pallas_call | solution.py:874
  65.2 29.5 %middle.1 = (bf16[1024,512]{1,0:T(8,128)(2,1)}, f32[1024,512]{1,0:T(8,128)}, f32[1024,512]{1,0:T(8,128)}, f32[16,512]{1,0:T(8,128)}, bf16[9,8,4,16,512]{4,3,2,1,0:T(8,128)(2,1)}) custom-call(bf16[1024,512]{1,0:T(8,128)(2,1)} %x_ref.5, bf16[1024,512]{1,0:T(8,128)(2,1)} %get-tuple-element.36.attr_ref, bf16[1024,512]{1,0:T(8,128)(2,1)} %cot_ref.1, ...), custom_call_target="tpu_custom_call" | custom-call | tf_op jit(solution)/shard_map/middle/pallas_call | solution.py:791
  94.6 80.0 %reduce_backward.1 = (bf16[1024,512]{1,0:T(8,128)(2,1)}, f32[9,16,512]{2,1,0:T(8,128)}, f32[16,1536]{1,0:T(8,128)}, f32[16,512]{1,0:T(8,128)}) custom-call(bf16[1024,512]{1,0:T(8,128)(2,1)} %x_ref.5, bf16[1024,512]{1,0:T(8,128)(2,1)} %get-tuple-element.43.h_ref, bf16[1024,512]{1,0:T(8,128)(2,1)} %get-tuple-element.44.q_ref, ...), custom_call_target="tpu_custom_call" | custom-call | tf_op jit(solution)/shard_map/reduce_backward/pallas_call | solution.py:894
  174.6 0.9 fusion.11
  175.6 0.6 fusion.6
  176.2 0.6 fusion.4
  176.7 1.6 fusion.10
  178.4 0.7 copy.43
  179.0 0.8 slice_bitcast_fusion.2
  179.8 0.6 dynamic_slice.36
  180.4 1.4 slice_bitcast_fusion.1
  181.8 0.6 fusion.8
  182.4 2.3 %copy.48 = bf16[1024,512]{1,0:T(8,128)(2,1)} copy(bf16[1024,512]{1,0:T(8,128)(2,1)} %get-tuple-element.86) | data formatting | bytes 2097152
  184.6 0.6 copy.49
  (17 shorter events, 0.1 us)
Async XLA Ops:
  0.6 3.0 %copy-start.3 = (bf16[64]{0:T(256)(128)(2,1)S(1)}, bf16[64]{0:T(256)(128)(2,1)}, u32[]{:S(2)}) copy-start(bf16[64]{0:T(256)(128)(2,1)} %param.25) | copy-start | bytes 388
  0.7 3.1 %copy-start.1 = (bf16[64,512]{1,0:T(8,128)(2,1)S(1)}, bf16[64,512]{1,0:T(8,128)(2,1)}, u32[]{:S(2)}) copy-start(bf16[64,512]{1,0:T(8,128)(2,1)} %param.20) | copy-start | bytes 196612
  1.9 3.2 %copy-start.4 = (bf16[16]{0:T(256)(128)(2,1)S(1)}, bf16[16]{0:T(256)(128)(2,1)}, u32[]{:S(2)}) copy-start(bf16[16]{0:T(256)(128)(2,1)} %param.21) | copy-start | bytes 100
  1.9 3.2 %copy-start.5 = (bf16[16]{0:T(256)(128)(2,1)S(1)}, bf16[16]{0:T(256)(128)(2,1)}, u32[]{:S(2)}) copy-start(bf16[16]{0:T(256)(128)(2,1)} %param.22) | copy-start | bytes 100
  2.0 3.3 %copy-start.6 = (bf16[16]{0:T(256)(128)(2,1)S(1)}, bf16[16]{0:T(256)(128)(2,1)}, u32[]{:S(2)}) copy-start(bf16[16]{0:T(256)(128)(2,1)} %param.23) | copy-start | bytes 100
  2.0 3.4 %copy-start.7 = (bf16[16]{0:T(256)(128)(2,1)S(1)}, bf16[16]{0:T(256)(128)(2,1)}, u32[]{:S(2)}) copy-start(bf16[16]{0:T(256)(128)(2,1)} %param.24) | copy-start | bytes 100
  2.0 3.5 %copy-start.8 = (bf16[16]{0:T(256)(128)(2,1)S(1)}, bf16[16]{0:T(256)(128)(2,1)}, u32[]{:S(2)}) copy-start(bf16[16]{0:T(256)(128)(2,1)} %param.26) | copy-start | bytes 100
  2.0 3.7 %copy-start.2 = (bf16[16,1536]{1,0:T(8,128)(2,1)S(1)}, bf16[16,1536]{1,0:T(8,128)(2,1)}, u32[]{:S(2)}) copy-start(bf16[16,1536]{1,0:T(8,128)(2,1)} %param.17) | copy-start | bytes 147460
  174.6 10.0 %copy-start = (f32[16,1536]{1,0:T(8,128)S(1)}, f32[16,1536]{1,0:T(8,128)}, u32[]{:S(2)}) copy-start(f32[16,1536]{1,0:T(8,128)} %get-tuple-element.87) | copy-start | bytes 294916

commit v3 on v2

--- a/solution.py
+++ b/solution.py
@@ -191,21 +191,27 @@
         self.send, self.recv, self.own = sems
         self.load, self.write = load, write
 
-    def hops(self, stage, c):
+    def hops(self, stage, c, x_first):
         p = self.place
         every = slice(None)
         if stage == 0:
-            yield self.source.at[c, every, every, every, 1 - p.c], self.r0.at[c], self.r0.at[c], p.device(c=1 - p.c)
+            yield self.source.at[c, every, every, every, 1 - p.c], self.r0.at[c], p.device(c=1 - p.c)
         elif stage == 1:
-            yield self.l0.at[c, every, every, 1 - p.x], self.r1.at[c], self.r1.at[c], p.device(x=1 - p.x)
+            if x_first:
+                yield self.l0.at[c, every, every, 1 - p.x], self.r1.at[c], p.device(x=1 - p.x)
+            else:
+                yield self.l0.at[c, every, 1 - p.y], self.r1.at[c], p.device(y=1 - p.y)
         elif stage == 2:
-            yield self.l1.at[c, every, 1 - p.y], self.r2.at[c], self.r2.at[c], p.device(y=1 - p.y)
+            if x_first:
+                yield self.l1.at[c, every, 1 - p.y], self.r2.at[c], p.device(y=1 - p.y)
+            else:
+                yield self.l1.at[c, every, 1 - p.x], self.r2.at[c], p.device(x=1 - p.x)
         else:
             for k in range(1, p.nz):
-                yield self.l2.at[c, p.up(k)], self.r3.at[c, k - 1], self.r3.at[c, k - 1], p.device(z=p.up(k))
-
-    def copies(self, stage, c):
-        for k, (src, dst, _, peer) in enumerate(self.hops(stage, c)):
+                yield self.l2.at[c, p.up(k)], self.r3.at[c, k - 1], p.device(z=p.up(k))
+
+    def copies(self, stage, c, x_first):
+        for k, (src, dst, peer) in enumerate(self.hops(stage, c, x_first)):
             yield remote(src, dst, self.send.at[c, stage, k], self.recv.at[c, stage, k], peer)
 
     def local(self, c):
@@ -215,18 +221,18 @@
             self.source.at[c, every, every, every, p.c], self.l0.at[c], self.own.at[c]
         )
 
-    def begin(self, stage, c):
-        for copy in self.copies(stage, c):
+    def begin(self, stage, c, x_first):
+        for copy in self.copies(stage, c, x_first):
             copy.start()
 
-    def step(self, stage, c):
+    def step(self, stage, c, x_first=False):
         p = self.place
         if stage == 0:
-            self.begin(0, c)
+            self.begin(0, c, x_first)
             if self.load:
                 self.local(c).start()
             return
-        for copy in self.copies(stage - 1, c):
+        for copy in self.copies(stage - 1, c, x_first):
             copy.wait_recv()
         if stage == 1:
             if self.load:
@@ -236,20 +242,22 @@
                 mine = self.source[c, :, :, :, p.c]
             self.l0[c] = (mine.astype(F32) + self.r0[c].astype(F32)).astype(BF)
         elif stage == 2:
-            self.l1[c] = (self.l0[c, :, :, p.x].astype(F32) + self.r1[c].astype(F32)).astype(BF)
+            mine = self.l0[c, :, :, p.x] if x_first else self.l0[c, :, p.y]
+            self.l1[c] = (mine.astype(F32) + self.r1[c].astype(F32)).astype(BF)
         elif stage == 3:
-            self.l2[c] = (self.l1[c, :, p.y].astype(F32) + self.r2[c].astype(F32)).astype(BF)
+            mine = self.l1[c, :, p.y] if x_first else self.l1[c, :, p.x]
+            self.l2[c] = (mine.astype(F32) + self.r2[c].astype(F32)).astype(BF)
         else:
             total = self.l2[c, p.z].astype(F32)
             for k in range(p.nz - 1):
                 total = total + self.r3[c, k].astype(F32)
             self.write(c, total)
             return
-        self.begin(stage, c)
-
-    def drain(self, c):
+        self.begin(stage, c, x_first)
+
+    def drain(self, c, x_first=False):
         for stage in range(4):
-            for copy in self.copies(stage, c):
+            for copy in self.copies(stage, c, x_first):
                 copy.wait_send()
 
     @staticmethod
@@ -339,76 +347,89 @@
     lax.fori_loop(0, x_ref.shape[1] // LANES, pair, 0)
 
 
+def ffn_rows(
+    t, x_ref, attr_ref, cot_ref, wo, wi, wf, prm_ref, bin_ref, seq_ref,
+    act_ref, dy_ref, datt_ref, gprm_ref, hid_ref, du_ref, h_ref, gr_ref, dor_ref, bin_row=0,
+):
+    width = x_ref.shape[1]
+    chunk = width
+    rows = tile_at(t)
+    y = x_ref[rows, :].astype(F32) + dot(attr_ref[rows, :], wo())
+    unit, inv = centred(y)
+    gain = prm_ref[2:3, :]
+    h = (unit * gain + prm_ref[3:4, :]).astype(BF)
+    h_ref[rows, :] = h
+    g = cot_ref[rows, :].astype(F32) * seq_ref[0:1, 0:1]
+    gr = g.astype(BF)
+    gr_ref[rows, :] = gr
+    out = y + prm_ref[4:5, :]
+    dh = jnp.zeros((TILE, width), F32)
+    for c in range(hid_ref.shape[1] // chunk):
+        cs = slice(c * chunk, (c + 1) * chunk)
+        u = dot(h, wi(cs)) + bin_ref[bin_row : bin_row + 1, cs]
+        cdf = 0.5 + 0.5 * lax.erf(u * math.sqrt(0.5))
+        slope = cdf + u * jnp.exp2(u * u * (-0.5 * LOG2E)) * (1.0 / math.sqrt(2.0 * math.pi))
+        hid = (u * cdf).astype(BF)
+        hid_ref[rows, cs] = hid
+        out = out + dot(hid, wf(c))
+        du = (dot_bt(gr, wf(c)) * slope).astype(BF)
+        du_ref[rows, cs] = du
+        gprm_ref[5 + c : 6 + c, :] += jnp.sum(du.astype(F32), axis=0, keepdims=True)
+        dh = dh + dot_bt(du, wi(cs))
+    act_ref[rows, :] = out.astype(BF)
+    gprm_ref[2:3, :] += jnp.sum(dh * unit, axis=0, keepdims=True)
+    gprm_ref[3:4, :] += jnp.sum(dh, axis=0, keepdims=True)
+    gprm_ref[4:5, :] += jnp.sum(g, axis=0, keepdims=True)
+    dy = g + norm_back(dh, unit, inv, gain)
+    dy_ref[rows, :] = dy
+    dor = dy.astype(BF)
+    dor_ref[rows, :] = dor
+    datt_ref[rows, :] = dot_bt(dor, wo())
+
+
+def grads_out(c, hid_ref, gr_ref, g_ref):
+    width = gr_ref.shape[1]
+    grad = dot_at(hid_ref[:, tile_at(c)], gr_ref[...]).astype(BF)
+    grad = grad.reshape(4, 4, 16, width)
+    for q in range(4):
+        g_ref[q, c] = grad[:, q]
+
+
+def grads_in(c, h_ref, du_ref, attr_ref, dor_ref, g_ref):
+    width = h_ref.shape[1]
+    count = du_ref.shape[1] // width
+    cs = tile_at(c)
+    at = pl.ds(c * 4, 4)
+    grad = dot_at(h_ref[:, cs], du_ref[...]).astype(BF)
+    for k in range(count):
+        g_ref[4 + k, at] = grad[:, k * width : (k + 1) * width].reshape(4, 4, 16, width)
+    grad = dot_at(attr_ref[:, cs], dor_ref[...]).astype(BF)
+    g_ref[4 + count, at] = grad.reshape(4, 4, 16, width)
+
+
+def loop(start, stop, step):
+    def run(i, carry):
+        step(i)
+        return carry
+
+    lax.fori_loop(start, stop, run, 0)
+
+
 def middle_kernel(
     x_ref, attr_ref, cot_ref, wo_ref, wi_ref, wf_ref, prm_ref, seq_ref,
     act_ref, dy_ref, datt_ref, gprm_ref, g_ref,
     hid_ref, du_ref, h_ref, gr_ref, dor_ref, bin_ref,
 ):
     length, width = x_ref.shape
-    hidden = wi_ref.shape[1]
-    chunk = width
     gprm_ref[...] = jnp.zeros_like(gprm_ref)
     bin_ref[...] = dot_bt(unit_rows(8), wf_ref[:, width:])
-
-    def rows(t, carry):
-        rows = tile_at(t)
-        y = x_ref[rows, :].astype(F32) + dot(attr_ref[rows, :], wo_ref[...])
-        unit, inv = centred(y)
-        gain = prm_ref[2:3, :]
-        h = (unit * gain + prm_ref[3:4, :]).astype(BF)
-        h_ref[rows, :] = h
-        g = cot_ref[rows, :].astype(F32) * seq_ref[0:1, 0:1]
-        gr = g.astype(BF)
-        gr_ref[rows, :] = gr
-        out = y + prm_ref[4:5, :]
-        dh = jnp.zeros((TILE, width), F32)
-        for c in range(hidden // chunk):
-            cs = slice(c * chunk, (c + 1) * chunk)
-            wi = wi_ref[:, cs]
-            wf = wf_ref[cs, :width]
-            u = dot(h, wi) + bin_ref[0:1, cs]
-            cdf = 0.5 + 0.5 * lax.erf(u * math.sqrt(0.5))
-            slope = cdf + u * jnp.exp2(u * u * (-0.5 * LOG2E)) * (1.0 / math.sqrt(2.0 * math.pi))
-            hid = (u * cdf).astype(BF)
-            hid_ref[rows, cs] = hid
-            out = out + dot(hid, wf)
-            du = (dot_bt(gr, wf) * slope).astype(BF)
-            du_ref[rows, cs] = du
-            gprm_ref[5 + c : 6 + c, :] += jnp.sum(du.astype(F32), axis=0, keepdims=True)
-            dh = dh + dot_bt(du, wi)
-        act_ref[rows, :] = out.astype(BF)
-        gprm_ref[2:3, :] += jnp.sum(dh * unit, axis=0, keepdims=True)
-        gprm_ref[3:4, :] += jnp.sum(dh, axis=0, keepdims=True)
-        gprm_ref[4:5, :] += jnp.sum(g, axis=0, keepdims=True)
-        dy = g + norm_back(dh, unit, inv, gain)
-        dy_ref[rows, :] = dy
-        dor = dy.astype(BF)
-        dor_ref[rows, :] = dor
-        datt_ref[rows, :] = dot_bt(dor, wo_ref[...])
-        return carry
-
-    lax.fori_loop(0, length // TILE, rows, 0)
-
-    def grad_f(c, carry):
-        grad = dot_at(hid_ref[:, tile_at(c)], gr_ref[...]).astype(BF)
-        grad = grad.reshape(4, 4, 16, width)
-        for q in range(4):
-            g_ref[q, c] = grad[:, q]
-        return carry
-
-    lax.fori_loop(0, hidden // TILE, grad_f, 0)
-
-    def grad_i(c, carry):
-        cs = tile_at(c)
-        at = pl.ds(c * 4, 4)
-        grad = dot_at(h_ref[:, cs], du_ref[...]).astype(BF)
-        for k in range(hidden // chunk):
-            g_ref[4 + k, at] = grad[:, k * chunk : (k + 1) * chunk].reshape(4, 4, 16, width)
-        grad = dot_at(attr_ref[:, cs], dor_ref[...]).astype(BF)
-        g_ref[4 + hidden // chunk, at] = grad.reshape(4, 4, 16, width)
-        return carry
-
-    lax.fori_loop(0, width // TILE, grad_i, 0)
+    loop(0, length // TILE, lambda t: ffn_rows(
+        t, x_ref, attr_ref, cot_ref, lambda: wo_ref[...], lambda cs: wi_ref[:, cs],
+        lambda c: wf_ref[c * width : (c + 1) * width, :width], prm_ref, bin_ref, seq_ref,
+        act_ref, dy_ref, datt_ref, gprm_ref, hid_ref, du_ref, h_ref, gr_ref, dor_ref,
+    ))
+    loop(0, hid_ref.shape[1] // TILE, lambda c: grads_out(c, hid_ref, gr_ref, g_ref))
+    loop(0, width // TILE, lambda c: grads_in(c, h_ref, du_ref, attr_ref, dor_ref, g_ref))
 
 
 def back_pair(
@@ -549,45 +570,11 @@
     lax.fori_loop(0, x_ref.shape[0] // TILE, rows, 0)
 
 
-def gather_forward_kernel(
-    nz, factor, x_ref, wqs_ref, wos_ref, wis_ref, wfs_ref, fx_ref,
-    h_ref, q_ref, k_ref, v_ref, pq_ref, pk_ref, att_ref, attr_ref, den_ref, prm_ref, seq_ref,
-    wq_ref, wo_ref, wi_ref, wf_ref,
-    send, recv, own,
-):
-    length, width = x_ref.shape
-    place = Place(nz)
-    every = slice(None)
-    sems = (send, recv, own)
-    cut = width * 3 // 2
-    half = wis_ref.shape[1] // 2
-    low, high = slice(0, 32), slice(32, 64)
-    q0 = Gather(place, wqs_ref, wq_ref, (every, slice(0, cut)), sems, 0, True)
-    q1 = Gather(place, wqs_ref, wq_ref, (every, slice(cut, wqs_ref.shape[1])), sems, 1, False)
-    o = Gather(place, wos_ref, wo_ref, (every, every), sems, 2, True)
-    i0 = Gather(place, wis_ref, wi_ref, (every, slice(0, half)), sems, 3, True)
-    i1 = Gather(place, wis_ref, wi_ref, (every, slice(half, 2 * half)), sems, 4, False)
-    f0 = Gather(place, wfs_ref, wf_ref, (low, every), sems, 5, True)
-    f1 = Gather(place, wfs_ref, wf_ref, (high, every), sems, 6, False)
-    first, rest = (q0, q1), (o, i0, i1, f0, f1)
-    place.barrier()
-    for g in (*first, *rest):
-        g.start()
-    for stage in (1, 2, 3):
-        for g in first:
-            g.step(stage)
-    for g in rest:
-        g.step(1)
-    for g in first:
-        g.arrive(3)
-
-    wqx = wq_ref[...].reshape(width, wqs_ref.shape[1])
-    small = wqx[:, 3 * width :]
-    prm_ref[...] = dot_bt(unit_rows(8), small)
+def sequence_weight(small, seq_ref):
     nf = 4
     me = lax.axis_index("dp") * nf + lax.axis_index("fsdp")
     row = lax.broadcasted_iota(jnp.int32, small.shape, 0)
-    lane = lane_ids(width).astype(F32)
+    lane = lane_ids(small.shape[0]).astype(F32)
     peer = lax.div(row, 16)
     ids = small[:, 5:6].astype(F32)
     hit = (lane == ids) & (lax.rem(row, 16) == 0)
@@ -601,36 +588,154 @@
     members = lax.axis_size("dp")
     seq_ref[...] = jnp.broadcast_to(members / (groups * size), seq_ref.shape)
 
-    def rows(i, carry):
-        wq = wq_ref[..., : 3 * width].reshape(width, 3 * width)
+
+def gather_forward_kernel(
+    nz, factor, x_ref, cot_in, wqs_ref, wos_ref, wis_ref, wfs_ref, fm_ref, id_ref,
+    g1_ref, s1_ref, g2_ref, s2_ref, bo_ref, bi_ref,
+    h_out, q_out, k_out, v_out, pq_out, pk_out, att_out, den_out, wq_out,
+    act_out, dy_out, datt_out, g_out, fx_out, prm_ref, gprm_ref,
+    h_ref, q_ref, k_ref, v_ref, pq_ref, pk_ref, att_ref, attr_ref, den_ref,
+    wq_ref, wo_ref, wi_ref, wf_ref, sp_ref, bp_ref, cot_ref, fx_ref, vec_ref, col_ref,
+    act_ref, dy_ref, datt_ref, g_ref, hid_ref, du_ref, h2_ref, gr_ref, dor_ref, bin_ref, seq_ref,
+    send, recv, own, one_sem, pair_sem, tile_sem, grad_sem,
+):
+    length, width = x_ref.shape
+    place = Place(nz)
+    every = slice(None)
+    sems = (send, recv, own)
+    cut = width * 3 // 2
+    half = wis_ref.shape[1] // 2
+    low, high = slice(0, 32), slice(32, 64)
+    q0 = Gather(place, wqs_ref, wq_ref, (every, slice(0, cut)), sems, 0, True)
+    q1 = Gather(place, wqs_ref, wq_ref, (every, slice(cut, 2 * cut)), sems, 1, False)
+    o = Gather(place, wos_ref, wo_ref, (every, every), sems, 2, True)
+    i0 = Gather(place, wis_ref, wi_ref, (every, slice(0, half)), sems, 3, True)
+    i1 = Gather(place, wis_ref, wi_ref, (every, slice(half, 2 * half)), sems, 4, False)
+    f0 = Gather(place, wfs_ref, wf_ref, (low, every), sems, 5, True)
+    f1 = Gather(place, wfs_ref, wf_ref, (high, every), sems, 6, False)
+    sp = Gather(place, col_ref, sp_ref, (slice(0, 16), every), sems, 7, True)
+    bp = Gather(place, col_ref, bp_ref, (slice(0, 64), every), sems, 8, False)
+    first, rest = (sp, q0, q1), (o, bp, i0, i1, f0, f1)
+
+    singles = [
+        pltpu.make_async_copy(src, dst, one_sem.at[n])
+        for n, (src, dst) in enumerate((
+            (cot_in, cot_ref), (wq_ref, wq_out), (h_ref, h_out), (q_ref, q_out),
+            (k_ref, k_out), (v_ref, v_out), (fx_ref, fx_out),
+        ))
+    ]
+
+    def pair_out(p):
+        moves = ((pq_ref, pq_out, 4), (pk_ref, pk_out, 4), (att_ref, att_out, 1), (den_ref, den_out, 1))
+        for n, (src, dst, many) in enumerate(moves):
+            cols = tile_at(p, many * LANES)
+            yield pltpu.make_async_copy(src.at[:, cols], dst.at[:, cols], pair_sem.at[p, n])
+
+    def tile_out(t):
+        rows = tile_at(t)
+        for n, (src, dst) in enumerate(((act_ref, act_out), (dy_ref, dy_out), (datt_ref, datt_out))):
+            yield pltpu.make_async_copy(src.at[rows], dst.at[rows], tile_sem.at[t, n])
+
+    def grad_out(c):
+        return pltpu.make_async_copy(g_ref.at[c], g_out.at[c], grad_sem.at[c])
+
+    vec_ref[...] = jnp.zeros_like(vec_ref)
+    for n, ref in enumerate((g1_ref, s1_ref, g2_ref, s2_ref, bo_ref)):
+        vec_ref[n : n + 1, : ref.shape[1]] = ref[...].astype(F32)
+    vec_ref[5:6, :] = jnp.full((1, LANES), id_ref[0], jnp.int32).astype(F32)
+    vec_ref[6:7, : bi_ref.shape[1]] = bi_ref[...].astype(F32)
+    col_ref[...] = dot_at(vec_ref[...].astype(BF), unit_rows(16)).astype(BF)
+    place.barrier()
+    for g in (*first, *rest):
+        g.start()
+    singles[0].start()
+    head_size, feats = fm_ref.shape[1:]
+    for n in range(fm_ref.shape[0]):
+        row = lax.broadcasted_iota(jnp.int32, (head_size, LANES), 0)
+        place_at = jnp.where(lane_ids(head_size) == row + (n % 2) * head_size, 1.0, 0.0).astype(BF)
+        fx_ref[n, :, :LANES] = dot_at(fm_ref[n], place_at).astype(BF)
+        fx_ref[n, :, LANES:] = jnp.ones((feats, LANES), BF)
+    singles[6].start()
+    for stage in (1, 2, 3):
+        for g in first:
+            g.step(stage)
+    for g in rest:
+        g.step(1)
+    for g in first:
+        g.arrive(3)
+    singles[1].start()
+    small = sp_ref[...].reshape(width, LANES)
+    prm_ref[...] = dot_bt(unit_rows(8), small)
+    sequence_weight(small, seq_ref)
+
+    def rows(i):
+        wq = wq_ref[...].reshape(width, 3 * width)
         project_rows(i, x_ref, wq, prm_ref, h_ref, q_ref, k_ref, v_ref, factor)
-        return carry
-
-    lax.fori_loop(0, length // TILE, rows, 0)
+
+    loop(0, length // TILE, rows)
+    for copy in singles[2:6]:
+        copy.start()
     for g in rest:
         g.step(2)
 
-    def pair(p, carry):
+    def pair(p):
         attend_pair(p, q_ref, k_ref, v_ref, fx_ref, pq_ref, pk_ref, att_ref, attr_ref, den_ref)
-        return carry
+        for copy in pair_out(p):
+            copy.start()
 
     pairs = width // LANES
-    lax.fori_loop(0, pairs - 2, pair, 0)
-    for g in (o, i0, i1):
+    loop(0, pairs - 1, pair)
+    for g in (o, bp, i0, i1):
         g.step(3)
-    lax.fori_loop(pairs - 2, pairs, pair, 0)
+    loop(pairs - 1, pairs, pair)
     for g in (f0, f1):
         g.step(3)
     for g in rest:
         g.arrive(3)
+    singles[0].wait()
+
+    gprm_ref[...] = jnp.zeros_like(gprm_ref)
+    hidden = hid_ref.shape[1]
+    bin_ref[...] = dot_bt(unit_rows(8), bp_ref[...].reshape(hidden, LANES))
+
+    def ffn(t):
+        ffn_rows(
+            t, x_ref, attr_ref, cot_ref, lambda: wo_ref[...].reshape(width, width),
+            lambda cs: wi_ref[..., cs].reshape(width, width),
+            lambda c: wf_ref[c].reshape(width, width), prm_ref, bin_ref, seq_ref,
+            act_ref, dy_ref, datt_ref, gprm_ref, hid_ref, du_ref, h2_ref, gr_ref, dor_ref, 6,
+        )
+        for copy in tile_out(t):
+            copy.start()
+
+    loop(0, length // TILE, ffn)
+    loop(0, hidden // TILE, lambda c: grads_out(c, hid_ref, gr_ref, g_ref))
+    for c in range(4):
+        grad_out(c).start()
+    loop(0, width // TILE, lambda c: grads_in(c, h2_ref, du_ref, attr_ref, dor_ref, g_ref))
+    chunks = g_ref.shape[0]
+    for c in range(4, chunks):
+        grad_out(c).start()
+    for copy in singles[1:]:
+        copy.wait()
+    for p in range(pairs):
+        for copy in pair_out(p):
+            copy.wait()
+    for t in range(length // TILE):
+        for copy in tile_out(t):
+            copy.wait()
+    for c in range(chunks):
+        grad_out(c).wait()
     for g in (*first, *rest):
         g.drain()
 
 
 def reduce_backward_kernel(
-    nz, factor, x_ref, h_ref, q_ref, k_ref, v_ref, pq_ref, pk_ref, att_ref, den_ref, datt_ref,
-    dy_ref, wq_ref, fx_ref, prm_ref, gin_ref, g_ref,
-    out_ref, parts_ref, partq_ref, total_ref,
+    nz, factor, x_in, h_in, q_in, k_in, v_in, pq_in, pk_in, att_in, den_in, datt_in,
+    dy_in, wq_in, fx_ref, prm_ref, gin_ref, g_ref,
+    out_ref, gf_ref, gi_ref, go_ref, partq_ref, small_ref,
+    x_ref, h_ref, q_ref, k_ref, v_ref, pq_ref, pk_ref, att_ref, den_ref, datt_ref, dy_ref, wq_ref,
+    pair_sem, full_sem,
     ht_ref, dqkv_ref, dn_ref, acc_ref, gq_ref, sum_ref, got_ref, *rest,
 ):
     place = Place(nz)
@@ -639,9 +744,20 @@
     width = x_ref.shape[1]
     chunks = g_ref.shape[0]
     pairs = width // LANES
+    wide = gi_ref.shape[1] // width
 
     def write(c, value):
-        parts_ref[c] = value
+        @pl.when(c < 4)
+        def _():
+            gf_ref[c] = value
+
+        @pl.when((c >= 4) & (c < 4 + wide))
+        def _():
+            gi_ref[:, pl.ds(pl.multiple_of((c - 4) * width, width), width)] = value
+
+        @pl.when(c == 4 + wide)
+        def _():
+            go_ref[...] = value
 
     def write_q(c, value):
         for at in range(3):
@@ -651,6 +767,25 @@
     big = Reduce(place, g_ref, bufs, sems, True, write)
     own = Reduce(place, gq_ref, bufs_q, sems_q, False, write_q)
 
+    full = [
+        pltpu.make_async_copy(src, dst, full_sem.at[n])
+        for n, (src, dst) in enumerate(
+            ((h_in, h_ref), (wq_in, wq_ref), (x_in, x_ref), (dy_in, dy_ref))
+        )
+    ]
+    by_pair = (
+        (pk_in, pk_ref, 4), (v_in, v_ref, 1), (datt_in, datt_ref, 1), (den_in, den_ref, 1),
+        (att_in, att_ref, 1), (pq_in, pq_ref, 4), (q_in, q_ref, 1), (k_in, k_ref, 1),
+    )
+
+    def load(p):
+        for n, (src, dst, many) in enumerate(by_pair):
+            cols = tile_at(p, many * LANES)
+            yield pltpu.make_async_copy(src.at[:, cols], dst.at[:, cols], pair_sem.at[p, n])
+
+    for copy in load(0):
+        copy.start()
+    full[0].start()
     place.barrier()
 
     def begin(c, carry):
@@ -658,33 +793,48 @@
         return carry
 
     lax.fori_loop(0, chunks, begin, 0)
+
+    def fetch(p, carry):
+        for copy in load(p):
+            copy.start()
+        return carry
+
+    lax.fori_loop(1, pairs, fetch, 0)
+    for copy in full[1:]:
+        copy.start()
     sum_ref[0] = gin_ref[...]
+    full[0].wait()
     flip_rows(h_ref, ht_ref)
 
     def pair(p, carry):
-        def advance(ring, stage, c, count):
+        def advance(ring, stage, c, count, x_first):
             @pl.when((c >= 0) & (c < count))
             def _():
-                ring.step(stage, c)
+                ring.step(stage, c, x_first)
+
+        def advance_big(stage, c0):
+            advance(big, stage, 4 * p + c0, chunks, c0 % 2 == 0)
 
         def tick(j):
             if j % 2:
-                advance(big, 2, 4 * p + (j - 7) // 2, chunks)
+                advance_big(2, (j - 7) // 2)
             else:
-                advance(big, 1, 4 * p + j // 2 - 1, chunks)
-                advance(big, 3, 4 * p + j // 2 - 5, chunks)
-                advance(big, 4, 4 * p + j // 2 - 7, chunks)
+                advance_big(1, j // 2 - 1)
+                advance_big(3, j // 2 - 5)
+                advance_big(4, j // 2 - 7)
             if j == 1:
-                advance(own, 1, p - 1, pairs)
-                advance(own, 3, p - 2, pairs)
+                advance(own, 1, p - 1, pairs, False)
+                advance(own, 3, p - 2, pairs, False)
             if j == 5:
-                advance(own, 2, p - 1, pairs)
-                advance(own, 4, p - 2, pairs)
+                advance(own, 2, p - 1, pairs, False)
+                advance(own, 4, p - 2, pairs, False)
 
         def store(at, where, value):
             shape = (nz, 2, 2, 2, 16, LANES)
             gq_ref[p, ..., at * LANES : (at + 1) * LANES] = value.reshape(shape)
 
+        for copy in load(p):
+            copy.wait()
         back_pair(
             p, factor, q_ref, k_ref, v_ref, pq_ref, pk_ref, att_ref, den_ref, datt_ref, fx_ref,
             ht_ref, dqkv_ref, dn_ref, acc_ref, tick, store,
@@ -693,28 +843,25 @@
         return carry
 
     lax.fori_loop(0, pairs, pair, 0)
+    for copy in full[1:]:
+        copy.wait()
     last = pairs - 1
     small = sum_ref.at[0]
 
     def rows(t, carry):
-        wq = wq_ref[:, : 3 * width]
+        wq = wq_ref[...]
         input_rows(t, x_ref, wq, prm_ref, dqkv_ref, dy_ref, out_ref, small)
         return carry
 
     tiles = x_ref.shape[0] // TILE
-    lax.fori_loop(0, 1, rows, 0)
-    own.step(1, last)
-    own.step(3, last - 1)
-    lax.fori_loop(1, tiles - 1, rows, 0)
-    own.step(2, last)
-    own.step(4, last - 1)
-    lax.fori_loop(tiles - 1, tiles, rows, 0)
 
     def exchange(stage):
         if stage < 3:
-            at = [(0, place.device(c=1 - place.c)), (1, place.device(x=1 - place.x)),
-                  (2, place.device(y=1 - place.y))][stage]
-            hops = [at]
+            hops = [
+                [(0, place.device(c=1 - place.c))],
+                [(1, place.device(x=1 - place.x))],
+                [(2, place.device(y=1 - place.y))],
+            ][stage]
         else:
             hops = [(2 + k, place.device(z=place.up(k))) for k in range(1, nz)]
         for slot, peer in hops:
@@ -722,6 +869,10 @@
                 sum_ref.at[stage], got_ref.at[slot], send.at[slot], recv.at[slot], peer
             )
 
+    def launch(stage):
+        for _, copy in exchange(stage):
+            copy.start()
+
     def combine(stage):
         value = sum_ref[stage]
         for slot, copy in exchange(stage):
@@ -729,31 +880,82 @@
             value = value + got_ref[slot]
         return value
 
-    for _, copy in exchange(0):
-        copy.start()
+    own.step(3, last - 1)
+    lax.fori_loop(0, tiles // 2, rows, 0)
+    own.step(1, last)
+    lax.fori_loop(tiles // 2, tiles, rows, 0)
+    launch(0)
+    own.step(4, last - 1)
+    own.step(2, last)
+    sum_ref[1] = combine(0)
+    launch(1)
     own.step(3, last)
-    for stage in range(3):
-        sum_ref[stage + 1] = combine(stage)
-        for _, copy in exchange(stage + 1):
-            copy.start()
-        if stage == 1:
-            own.step(4, last)
-    total_ref[...] = combine(3)
+    sum_ref[2] = combine(1)
+    launch(2)
+    own.step(4, last)
+    sum_ref[3] = combine(2)
+    launch(3)
+    small_ref[...] = combine(3)
     for stage in range(4):
         for _, copy in exchange(stage):
             copy.wait_send()
-
-    def drain(c, carry):
-        big.drain(c)
-        return carry
-
-    lax.fori_loop(0, chunks, drain, 0)
+    for c in range(chunks):
+        big.drain(c, c % 2 == 0)
 
     def drain_q(c, carry):
         own.drain(c)
         return carry
 
     lax.fori_loop(0, pairs, drain_q, 0)
+
+
+def finish_kernel(
+    act_in, grad_in, gq_in, gf_in, gi_in, go_in, small_in,
+    act_ref, grad_ref, gq_ref, go_ref, gi_ref, gf_ref,
+    g1_ref, s1_ref, g2_ref, s2_ref, bi_ref, bo_ref,
+    hold_ref, in_sem, out_sem,
+):
+    moves = []
+    for n, (src, dst) in enumerate(((act_in, act_ref), (grad_in, grad_ref))):
+        for t in range(src.shape[0] // TILE):
+            rows = pl.ds(t * TILE, TILE)
+            hold = hold_ref.at[n, rows]
+            moves.append((
+                pltpu.make_async_copy(src.at[rows], hold, in_sem.at[n, t]),
+                pltpu.make_async_copy(hold, dst.at[rows], out_sem.at[n, t]),
+            ))
+    for come, _ in moves:
+        come.start()
+    gq_ref[...] = gq_in[...]
+    go_ref[...] = go_in[...]
+    gi_ref[...] = gi_in[...]
+    gf_ref[...] = gf_in[...].reshape(gf_ref.shape)
+    width = small_in.shape[1]
+    me = lax.axis_index("dp") * 4 + lax.axis_index("fsdp")
+    row = lax.broadcasted_iota(jnp.int32, (width, LANES), 0)
+    lane = lane_ids(width)
+
+    def cut(value, start):
+        pick = jnp.where(row == lane + start, 1.0, 0.0)
+        return lax.dot_general(
+            value, pick, (((1,), (0,)), ((), ())), precision=lax.Precision.HIGHEST,
+            preferred_element_type=F32,
+        )
+
+    for come, go in moves:
+        come.wait()
+        go.start()
+    small = small_in[...]
+    part = cut(small, me * 16)
+    for n, ref in enumerate((g1_ref, s1_ref, g2_ref, s2_ref, bo_ref)):
+        ref[...] = part[n : n + 1, : ref.shape[1]]
+    each = width // 64
+    part = cut(small, lax.rem(me, each) * 64)
+    which = lax.broadcasted_iota(jnp.int32, part.shape, 0)
+    mine = jnp.where(which == 5 + lax.div(me, each), part, 0.0)
+    bi_ref[...] = jnp.sum(mine, axis=0, keepdims=True)[:, : bi_ref.shape[1]]
+    for _, go in moves:
+        go.wait()
 
 
 ANY = pl.BlockSpec(memory_space=pl.ANY)
@@ -864,40 +1066,47 @@
     hidden = w_ffn_in.shape[1]
     factor = head_size ** (-0.25)
     nz = lax.axis_size("dp") // 2
-    ids = jnp.broadcast_to(group_id.astype(BF), gain_one.shape)
-    small = jnp.stack([gain_one, shift_one, gain_two, shift_two, bias_out, ids], axis=1)
-    wqs = jnp.concatenate([w_qkv, jnp.pad(small, ((0, 0), (0, LANES - 6)))], axis=1)
-    wfs = jnp.concatenate([w_ffn_out, jnp.pad(bias_in[:, None], ((0, 0), (0, LANES - 1)))], axis=1)
-    fx = padded_features(feature_matrix)
-    wide = 3 * width + LANES
     grid = (nz, 2, 2, 2)
-    h1, q, k, v, pq, pk, att, attr, den, prm, seq, wq, wo, wi, wf = call(
+    wide = 3 * width
+    pairs = width // LANES
+    chunks = 5 + hidden // width
+    big, deep, tall = (length, width), (length, heads * feats), (length, hidden)
+    blocks = (chunks, width // 64, 4, 16, width)
+    kept = [*[(big, BF)] * 4, *[(deep, BF)] * 2]
+    h1, q, k, v, pq, pk, att, den, wq, act, dy, datt, grads, fx, prm, gprm = call(
         functools.partial(gather_forward_kernel, nz, factor),
         [
-            *forward_outs(length, width, heads, feats), ((8, width), F32), ((8, LANES), F32),
+            *kept, (big, F32), (big, F32), ((*grid, 16, wide), BF), (big, BF), (big, F32),
+            (big, F32), (blocks, BF), ((heads, feats, 2 * LANES), BF), ((8, width), F32), ((16, width), F32),
+        ],
+        [
+            *kept, (big, F32), (big, BF), (big, F32),
             ((*grid, 16, wide), BF), ((*grid, 16, width), BF), ((*grid, 16, hidden), BF),
-            ((*grid, 64, width + LANES), BF),
+            ((*grid, 64, width), BF), ((*grid, 16, LANES), BF), ((*grid, 64, LANES), BF), (big, BF),
+            ((heads, feats, 2 * LANES), BF), ((16, LANES), F32), ((LANES, LANES), BF),
+            (big, BF), (big, F32), (big, F32), (blocks, BF), (tall, BF), (tall, BF),
+            (big, BF), (big, BF), (big, BF), ((8, hidden), F32), ((8, LANES), F32),
+            ((9, 4, nz - 1), None), ((9, 4, nz - 1), None), ((9,), None), ((7,), None),
+            ((pairs, 4), None), ((length // TILE, 3), None), ((chunks,), None),
         ],
-        [((7, 4, nz - 1), None), ((7, 4, nz - 1), None), ((7,), None)],
         "gather_forward",
-        [VM, ANY, ANY, ANY, ANY, VM],
-        [VM] * 12 + [ANY] * 3,
+        [VM, *[ANY] * 5, VM, pl.BlockSpec(memory_space=pltpu.SMEM), *[VM] * 6],
+        [*[ANY] * 14, VM, VM],
         0,
-    )(tokens, wqs, w_out, w_ffn_in, wfs, fx)
+    )(
+        tokens, cotangent, w_qkv, w_out, w_ffn_in, w_ffn_out, feature_matrix.swapaxes(1, 2),
+        group_id, *(t[None] for t in (gain_one, shift_one, gain_two, shift_two, bias_out, bias_in)),
+    )
     wq = wq.reshape(width, wide)
-    act, dy, datt, gprm, grads = middle(
-        tokens, attr, cotangent, wo.reshape(width, width), wi.reshape(width, hidden),
-        wf.reshape(hidden, width + LANES), prm, seq,
-    )
-    chunks = grads.shape[0]
-    pairs = width // LANES
-    input_grad, parts, gq, total = call(
+    input_grad, gf, gi, go, gq, total = call(
         functools.partial(reduce_backward_kernel, nz, factor),
         [
-            ((length, width), BF), ((chunks, 16, width), F32), ((16, 3 * width), F32),
-            ((16, width), F32),
+            (big, BF), ((4, 16, width), F32), ((16, hidden), F32), ((16, width), F32),
+            ((16, 3 * width), F32), ((16, width), F32),
         ],
         [
+            *[(big, BF)] * 5, *[(deep, BF)] * 2, *[(big, F32)] * 4, ((width, wide), BF),
+            ((pairs, 8), None), ((4,), None),
             *backward_scratch(length, width),
             ((pairs, *grid, 16, 3 * LANES), BF),
             ((4, 16, width), F32), ((2 + nz, 16, width), F32),
@@ -908,17 +1117,22 @@
             ((2 + nz,), None), ((2 + nz,), None),
         ],
         "reduce_backward",
-        [VM] * 15 + [ANY],
-        [VM] * 4,
+        [ANY] * 12 + [VM] * 3 + [ANY],
+        [VM] * 6,
         1,
     )(tokens, h1, q, k, v, pq, pk, att, den, datt, dy, wq, fx, prm, gprm, grads.reshape(chunks, *grid, 16, width))
-    gf = parts[:4].reshape(64, width)
-    gi = parts[4:-1].transpose(1, 0, 2).reshape(16, hidden)
-    go = parts[-1]
-    me = lax.axis_index("dp") * lax.axis_size("fsdp") + lax.axis_index("fsdp")
-    vec = [lax.dynamic_slice(total[i], (me * 16,), (16,)) for i in range(5)]
-    gbin = lax.dynamic_slice(total[5 : 5 + hidden // width].reshape(hidden), (me * 64,), (64,))
-    return (act, input_grad, gq, go, gi, gf, *vec[:4], gbin, vec[4])
+    act, input_grad, gq, go, gi, gf, *vecs = call(
+        finish_kernel,
+        [
+            (big, BF), (big, BF), ((16, wide), F32), ((16, width), F32), ((16, hidden), F32),
+            ((64, width), F32), *[((1, 16), F32)] * 4, ((1, 64), F32), ((1, 16), F32),
+        ],
+        [((2, length, width), BF), ((2, length // TILE), None), ((2, length // TILE), None)],
+        "finish",
+        [ANY, ANY, *[VM] * 5],
+        [ANY, ANY, *[VM] * 10],
+    )(act, input_grad, gq, gf, gi, go, total)
+    return (act, input_grad, gq, go, gi, gf, *(t[0] for t in vecs))
 
 
 def solution(mesh):

time: 186 us -> 152 us (0.82)
  Pallas kernels: 168 us -> 151 us
  local copies, waits for them, and re-layouts: 12.6 us -> 0 us
  other arithmetic: 2.89 us -> 0 us
    pallas_call x3, Pallas kernels: 168 us -> 151 us  [the longest x1 76.1 us: ring_body(): call(functools.partial(gather_forward_kernel, nz, factor), [*kept, (big,...]
    unnamed x23 -> x0, local copies, waits for them, and re-layouts: 4.98 us -> none
    concatenate x3 -> x0, other arithmetic: 2.74 us -> none  [the longest x1 1.46 us: padded_features(): jnp.concatenate([jnp.where(even, fm, zero), jnp.where(even, zero, fm), jn...]
    slice x2 -> x0, local copies, waits for them, and re-layouts: 2.55 us -> none  [the longest x1 1.64 us: ring_body(): gf = parts[:4].reshape(64, width)]
    dynamic_slice x4 -> x0, local copies, waits for them, and re-layouts: 2.34 us -> none  [the longest x3 1.75 us: ring_body(): vec = [lax.dynamic_slice(total[i], (me * 16,), (16,)) for i in range(5)]]
where the time goes in v3:
time: 152 us
  Pallas kernels  151 us (99%)
    pallas_call x1, Pallas kernels, ring_body(): call(functools.partial(gather_forward_kernel, nz, factor), [*kept, (big,...  76.1 us
    pallas_call x1, Pallas kernels, ring_body(): call(functools.partial(reduce_backward_kernel, nz, factor), [(big, BF), (...  70.2 us
    pallas_call x1, Pallas kernels, ring_body(): call(finish_kernel, [(big, BF), (big, BF), ((16, wide), F32), ((16, width...  4.22 us

profile of v3, /device:TPU:0, one launch (start us, length us, event | category | flops | bytes accessed | tf_op | source)
XLA Modules:
  0.0 152.1 jit_solution(7913869712374274016)
XLA Ops:
  1.3 76.1 %gather_forward.1 = (bf16[1024,512]{1,0:T(8,128)(2,1)}, bf16[1024,512]{1,0:T(8,128)(2,1)}, bf16[1024,512]{1,0:T(8,128)(2,1)}, bf16[1024,512]{1,0:T(8,128)(2,1)},...) custom-call(bf16[1024,512]{1,0:T(8,128)(2,1)} %x_in.1, ...), custom_call_target="tpu_custom_call" | custom-call | tf_op jit(solution)/shard_map/gather_forward/pallas_call | solution.py:1076
  77.4 70.2 %reduce_backward.1 = (bf16[1024,512]{1,0:T(8,128)(2,1)}, f32[4,16,512]{2,1,0:T(8,128)}, f32[16,2048]{1,0:T(8,128)}, f32[16,512]{1,0:T(8,128)}, f32[16,1536]{1,0:T(8,128)}, /*index=5*/f32[16,512]{1,0:T(8,128)}) custom-call(bf16[1024,512]{1,0:T(8,128)(2,1)} %x_in.1, bf16[1024,512]{1,0:T(8,128)(2,1)} %get-tuple-element.47.h_in, ...), custom_call_target="tpu_custom_call" | custom-call | tf_op jit(solution)/shard_map/reduce_backward/pallas_call | solution.py:1101
  147.7 4.2 %finish.1 = (bf16[1024,512]{1,0:T(8,128)(2,1)}, bf16[1024,512]{1,0:T(8,128)(2,1)}, f32[16,1536]{1,0:T(8,128)}, f32[16,512]{1,0:T(8,128)}, f32[16,2048]{1,0:T(8,1...) custom-call(bf16[1024,512]{1,0:T(8,128)(2,1)} %get-tuple-element.46., ...), custom_call_target="tpu_custom_call" | custom-call | tf_op jit(solution)/shard_map/finish/pallas_call | solution.py:1124

commit v4 on v3

v4 whole, which is shorter than its diff:
```python
import functools
import math

import jax
import jax.numpy as jnp
from jax import lax
from jax.experimental import pallas as pl
from jax.experimental.pallas import tpu as pltpu
from jax.sharding import PartitionSpec as P

BLOCK = 512
EPSILON = 1e-05
TILE = 256
FEAT_TILE = 1024
FFN_TILE = 512
LANES = 128
LOG2E = 1.4426950408889634
AXES = ("dp", "fsdp")
BF = jnp.bfloat16
F32 = jnp.float32


def dot(left, right):
    return lax.dot_general(left, right, (((1,), (0,)), ((), ())), preferred_element_type=F32)


def dot_bt(left, right):
    return lax.dot_general(left, right, (((1,), (1,)), ((), ())), preferred_element_type=F32)


def dot_at(left, right):
    return lax.dot_general(left, right, (((0,), (0,)), ((), ())), preferred_element_type=F32)


def unit_rows(rows):
    row = lax.broadcasted_iota(jnp.int32, (rows, LANES), 0)
    col = lax.broadcasted_iota(jnp.int32, (rows, LANES), 1)
    return jnp.where(row == col, 1.0, 0.0).astype(BF)


def lane_ids(rows, width=LANES):
    return lax.broadcasted_iota(jnp.int32, (rows, width), 1)


def tile_at(index, size=TILE):
    return pl.ds(pl.multiple_of(index * size, size), size)


def centred(values):
    mu = jnp.mean(values, axis=-1, keepdims=True)
    cen = values - mu
    inv = lax.rsqrt(jnp.mean(cen * cen, axis=-1, keepdims=True) + EPSILON)
    return cen * inv, inv


def norm_back(grad, unit, inv, gain):
    e = grad * gain
    return inv * (
        e
        - jnp.mean(e, axis=-1, keepdims=True)
        - unit * jnp.mean(e * unit, axis=-1, keepdims=True)
    )


def causal(values, offset):
    row = lax.broadcasted_iota(jnp.int32, values.shape, 0)
    col = lax.broadcasted_iota(jnp.int32, values.shape, 1)
    return jnp.where(col <= row + offset, values, 0.0).astype(BF)


def anticausal(values):
    row = lax.broadcasted_iota(jnp.int32, values.shape, 0)
    col = lax.broadcasted_iota(jnp.int32, values.shape, 1)
    return jnp.where(col >= row, values, 0.0).astype(BF)


MESH_ID = pl.DeviceIdType.MESH


SUMS = {
    "grad0": ((4, 0),),
    "chunk1": ((4, 1),),
    "grad1": ((5, 0),),
    "chunk2": ((5, 1), (4, 2)),
    "grad2": ((6, 0),),
    "chunk3": ((6, 1), (5, 2), (4, 3)),
    "grad3": ((7, 0), (0, 0), (1, 0), (2, 0), (3, 0)),
    "final": ((7, 1), (0, 1), (6, 2), (5, 3), (4, 4)),
    "grad_o": ((8, 0),),
    "b0:1": ((1, 1),),
    "b0:2": ((7, 2), (6, 3)),
    "b0:3": ((2, 1),),
    "b0:4": ((0, 2), (5, 4)),
    "b0:5": ((3, 1),),
    "b0:7": ((8, 1), (1, 2), (7, 3)),
    "b1:1": ((2, 2), (6, 4)),
    "b1:2": ((0, 3),),
    "b1:3": ((3, 2), (1, 3)),
    "b1:5": ((8, 2), (7, 4)),
    "b1:6": ((2, 3), (0, 4)),
    "b1:7": ((3, 3),),
    "b2:0": ((1, 4), (8, 3)),
    "b2:3": ((2, 4),),
    "b2:4": ((3, 4),),
    "b2:5": ((8, 4),),
}
OWN_SUMS = {
    "b1:2": ((0, 1),),
    "b2:1": ((0, 2),),
    "b2:2": ((1, 1),),
    "b2:6": ((0, 3),),
    "b3:1": ((1, 2),),
    "b3:2": ((2, 1),),
    "b3:4": ((0, 4),),
    "b3:6": ((1, 3),),
}
PLAN = {
    "start": (("s", 1), ("q0", 1), ("q1", 1), ("q2", 1), ("s", 2), ("q3", 1), ("q0", 2), ("o", 1), ("q1", 2), ("i0", 1), ("q2", 2), ("s", 3), ("q3", 2), ("o", 2), ("q0", 3), ("i0", 2), ("q1", 3),),
    "0:0": (("f0", 1), ("f1", 1), ("i1", 1), ("f2", 1),),
    "0:1": (("q2", 3), ("f3", 1),),
    "0:4": (("i2", 1),),
    "0:8": (("q3", 3),),
    "0:9": (("i3", 1),),
    "1:3": (("i0", 3),),
    "1:6": (("o", 3),),
    "1:8": (("f1", 2),),
    "1:11": (("f0", 2),),
    "2:0": (("f3", 2),),
    "2:4": (("i1", 2),),
    "2:5": (("i2", 2),),
    "2:8": (("f2", 2),),
    "2:10": (("i3", 2),),
    "3:7": (("f1", 3),),
    "3:9": (("f0", 3),),
    "chunk0": (("i1", 3), ("i2", 3), ("f3", 3),),
    "grad0": (("f2", 3),),
    "chunk1": (("i3", 3),),
}
Y_FIRST = {"s", "q0", "q2", "q3", "o", "i2", "i3", "f1", "f3"}


class Place:
    def __init__(self, nz):
        dp, fs = lax.axis_index("dp"), lax.axis_index("fsdp")
        self.nz = nz
        self.z, self.y = lax.div(dp, 2), lax.rem(dp, 2)
        self.x, self.c = lax.div(fs, 2), lax.rem(fs, 2)

    def device(self, z=None, y=None, x=None, c=None):
        z, y = self.z if z is None else z, self.y if y is None else y
        x, c = self.x if x is None else x, self.c if c is None else c
        return {"dp": z * 2 + y, "fsdp": x * 2 + c}

    def up(self, k):
        return lax.rem(self.z + k, self.nz)

    def down(self, k):
        return lax.rem(self.z + self.nz - k, self.nz)

    def peers(self):
        yield self.device(c=1 - self.c)
        yield self.device(x=1 - self.x)
        yield self.device(y=1 - self.y)
        yield self.device(x=1 - self.x, c=1 - self.c)
        for k in range(1, self.nz):
            yield self.device(z=self.up(k))
            yield self.device(z=self.up(k), y=1 - self.y)

    def near(self):
        yield self.device(c=1 - self.c)
        yield self.device(x=1 - self.x)
        yield self.device(x=1 - self.x, c=1 - self.c)

    def far(self):
        yield self.device(y=1 - self.y)
        for k in range(1, self.nz):
            yield self.device(z=self.up(k))
            yield self.device(z=self.up(k), y=1 - self.y)

    def barrier(self):
        sem = pltpu.get_barrier_semaphore()
        for peer in self.peers():
            pl.semaphore_signal(sem, inc=1, device_id=peer, device_id_type=MESH_ID)
        pl.semaphore_wait(sem, 2 + 2 * self.nz)


def remote(src, dst, send, recv, peer):
    return pltpu.make_async_remote_copy(
        src_ref=src, dst_ref=dst, send_sem=send, recv_sem=recv, device_id=peer,
        device_id_type=MESH_ID,
    )


class Gather:
    def __init__(self, place, shard, whole, view, sems, m, y_first, plane=None, base=None):
        self.place, self.shard, self.whole, self.view = place, shard, whole, view
        self.send, self.recv, self.own = sems
        self.m = m
        self.y_first = y_first
        self.plane, self.base = plane, base

    def at(self, *index):
        return self.whole.at[(*index, *self.view)]

    def hops(self, stage):
        p = self.place
        every = slice(None)
        zs = every if self.plane is None else self.plane
        if stage == 0:
            src = self.shard.at[self.view]
            for k in range(1, p.nz):
                yield src, self.at(p.z, p.y, p.x, p.c), self.at(p.down(k), p.y, p.x, p.c), p.device(z=p.up(k))
        elif stage == 3:
            mine = self.at(zs, every, every, p.c)
            yield mine, mine, self.at(zs, every, every, 1 - p.c), p.device(c=1 - p.c)
        elif stage == 1:
            mine = self.at(zs, p.y, p.x, p.c)
            if self.y_first:
                yield mine, mine, self.at(zs, 1 - p.y, p.x, p.c), p.device(y=1 - p.y)
            else:
                yield mine, mine, self.at(zs, p.y, 1 - p.x, p.c), p.device(x=1 - p.x)
        elif self.y_first:
            mine = self.at(zs, every, p.x, p.c)
            yield mine, mine, self.at(zs, every, 1 - p.x, p.c), p.device(x=1 - p.x)
        else:
            mine = self.at(zs, p.y, every, p.c)
            yield mine, mine, self.at(zs, 1 - p.y, every, p.c), p.device(y=1 - p.y)

    def copies(self, stage, arriving):
        for k, (src, dst, land, peer) in enumerate(self.hops(stage)):
            yield remote(
                src, land if arriving else dst, self.send.at[self.m, stage, k],
                self.recv.at[self.m, stage, k], peer,
            )

    def local(self):
        p = self.place
        return pltpu.make_async_copy(
            self.shard.at[self.view], self.at(p.z, p.y, p.x, p.c), self.own.at[self.m]
        )

    def start(self):
        for copy in self.copies(0, False):
            copy.start()
        self.local().start()

    def arrive(self, stage):
        for copy in self.copies(stage, True):
            copy.wait_recv()

    def enter(self):
        if self.plane is None:
            self.arrive(0)
            self.local().wait()
            return
        p = self.place
        hop = lax.rem(p.z + p.nz - self.plane, p.nz)

        @pl.when(hop == 0)
        def _():
            self.base.local().wait()

        @pl.when(hop != 0)
        def _():
            k = jnp.maximum(hop, 1) - 1
            remote(
                self.shard.at[self.view], self.at(self.plane, p.y, p.x, p.c),
                self.send.at[self.base.m, 0, k], self.recv.at[self.base.m, 0, k],
                p.device(z=p.up(1)),
            ).wait_recv()

    def step(self, stage):
        if stage == 1:
            self.enter()
        else:
            self.arrive(stage - 1)
        for copy in self.copies(stage, False):
            copy.start()

    def drain(self, stages=range(4)):
        for stage in stages:
            for copy in self.copies(stage, False):
                copy.wait_send()


class Reduce:
    def __init__(self, place, source, bufs, sems, write):
        self.place, self.source = place, source
        self.r0, self.r1, self.r2, self.r3 = bufs
        self.send, self.recv = sems
        self.write = write

    def hops(self, stage, c, x_first):
        p = self.place
        every = slice(None)
        if stage == 0:
            yield self.source.at[c, every, every, every, 1 - p.c], self.r0.at[c], p.device(c=1 - p.c)
        elif stage == 1:
            if x_first:
                yield self.r0.at[c, every, every, 1 - p.x], self.r1.at[c], p.device(x=1 - p.x)
            else:
                yield self.r0.at[c, every, 1 - p.y], self.r1.at[c], p.device(y=1 - p.y)
        elif stage == 2:
            if x_first:
                yield self.r1.at[c, every, 1 - p.y], self.r2.at[c], p.device(y=1 - p.y)
            else:
                yield self.r1.at[c, every, 1 - p.x], self.r2.at[c], p.device(x=1 - p.x)
        else:
            for k in range(1, p.nz):
                yield self.r2.at[c, p.up(k)], self.r3.at[c, k - 1], p.device(z=p.up(k))

    def copies(self, stage, c, x_first):
        for k, (src, dst, peer) in enumerate(self.hops(stage, c, x_first)):
            yield remote(src, dst, self.send.at[c, stage, k], self.recv.at[c, stage, k], peer)

    def step(self, stage, c, x_first=False):
        p = self.place
        if stage:
            for copy in self.copies(stage - 1, c, x_first):
                copy.wait_recv()
        if stage == 1:
            mine = self.source[c, :, :, :, p.c]
            self.r0[c] = mine + self.r0[c]
        elif stage == 2:
            mine = self.r0[c, :, :, p.x] if x_first else self.r0[c, :, p.y]
            self.r1[c] = mine + self.r1[c]
        elif stage == 3:
            mine = self.r1[c, :, p.y] if x_first else self.r1[c, :, p.x]
            self.r2[c] = mine + self.r2[c]
        elif stage == 4:
            total = self.r2[c, p.z].astype(F32)
            for k in range(p.nz - 1):
                total = total + self.r3[c, k].astype(F32)
            self.write(c, total)
            return
        for copy in self.copies(stage, c, x_first):
            copy.start()

    def drain(self, c, x_first=False):
        for stage in range(4):
            for copy in self.copies(stage, c, x_first):
                copy.wait_send()

    @staticmethod
    def shapes(n, nz, rows, cols):
        return [
            ((n, nz, 2, 2, rows, cols), BF), ((n, nz, 2, rows, cols), BF),
            ((n, nz, rows, cols), BF), ((n, nz - 1, rows, cols), BF),
        ]


def project_rows(i, x_ref, wq, prm_ref, h_ref, q_ref, k_ref, v_ref, factor):
    rows = tile_at(i)
    unit, _ = centred(x_ref[rows, :].astype(F32))
    h = (unit * prm_ref[0:1, :] + prm_ref[1:2, :]).astype(BF)
    h_ref[rows, :] = h
    width = h.shape[1]
    qkv = dot(h, wq)
    q_ref[rows, :] = (qkv[:, :width] * factor).astype(BF)
    k_ref[rows, :] = (qkv[:, width : 2 * width] * factor).astype(BF)
    v_ref[rows, :] = qkv[:, 2 * width :].astype(BF)


def attend_pair(
    p, q_ref, k_ref, v_ref, fx_ref, pq_ref, pk_ref, attr_ref, den_ref, low_ref,
    site=lambda j: None,
):
    length = q_ref.shape[0]
    feats = fx_ref.shape[1]
    lanes = tile_at(p, LANES)
    shift = 0.5 * math.log2(feats)
    cols = [tile_at(2 * p + hh, feats) for hh in range(2)]
    step = FEAT_TILE
    for hh in range(2):
        fm = fx_ref[2 * p + hh][:, :LANES]
        for src, dst in ((q_ref, pq_ref), (k_ref, pk_ref)):
            for t in range(length // step):
                rows = slice(t * step, (t + 1) * step)
                part = src[rows, lanes]
                scores = dot_bt(part, fm)
                wide = jnp.where(lane_ids(step) // 64 == hh, part.astype(F32), 0.0)
                square = jnp.sum(wide * wide, axis=-1, keepdims=True)
                feat = jnp.exp2(scores * LOG2E - (square * (0.5 * LOG2E) + shift))
                dst[rows, cols[hh]] = feat.astype(BF)
            site(2 * hh + int(src is k_ref))
    ones = jnp.ones((length, LANES), BF)
    vx = jnp.concatenate([v_ref[:, lanes], ones], axis=1)
    states = [None, None]
    for b in range(length // BLOCK):
        base = b * BLOCK
        for i in range(BLOCK // TILE):
            rows = slice(base + i * TILE, base + (i + 1) * TILE)
            keys = slice(base, base + (i + 1) * TILE)
            got = []
            for hh in range(2):
                pq = pq_ref[rows, cols[hh]]
                weights = causal(dot_bt(pq, pk_ref[keys, cols[hh]]), i * TILE)
                both = dot(weights, vx[keys])
                if b:
                    both = both + dot(pq, low_ref[2 * p + hh, b - 1])
                got.append(both)
            first = lane_ids(TILE) < 64
            num = jnp.where(first, got[0][:, :LANES], got[1][:, :LANES])
            den = jnp.where(first, got[0][:, LANES:], got[1][:, LANES:])
            attr_ref[rows, lanes] = (num / den).astype(BF)
            den_ref[rows, lanes] = den
            site(4 + b * (BLOCK // TILE) + i)
        if base + BLOCK < length:
            block = slice(base, base + BLOCK)
            for hh in range(2):
                more = dot_at(pk_ref[block, cols[hh]], vx[block])
                states[hh] = more if b == 0 else states[hh] + more
                low_ref[2 * p + hh, b] = states[hh].astype(BF)


def forward_kernel(
    factor, x_ref, wq_ref, prm_ref, fx_ref,
    h_ref, q_ref, k_ref, v_ref, pq_ref, pk_ref, attr_ref, den_ref, low_ref,
):
    def rows(i, carry):
        project_rows(i, x_ref, wq_ref[...], prm_ref, h_ref, q_ref, k_ref, v_ref, factor)
        return carry

    lax.fori_loop(0, x_ref.shape[0] // TILE, rows, 0)

    def pair(p, carry):
        attend_pair(
            p, q_ref, k_ref, v_ref, fx_ref, pq_ref, pk_ref, attr_ref, den_ref, low_ref
        )
        return carry

    lax.fori_loop(0, x_ref.shape[1] // LANES, pair, 0)


def ffn_rows(
    t, x_ref, attr_ref, cot_ref, wo, wi, wf, prm_ref, bin_ref, seq_ref,
    act_ref, dy_ref, datt_ref, gprm_ref, hid_ref, du_ref, h_ref, gr_ref, dor_ref, bin_row=0,
):
    width = x_ref.shape[1]
    chunk = width
    rows = tile_at(t, FFN_TILE)
    y = x_ref[rows, :].astype(F32) + dot(attr_ref[rows, :], wo())
    unit, inv = centred(y)
    gain = prm_ref[2:3, :]
    h = (unit * gain + prm_ref[3:4, :]).astype(BF)
    h_ref[rows, :] = h
    g = cot_ref[rows, :].astype(F32) * seq_ref[0:1, 0:1]
    gr = g.astype(BF)
    gr_ref[rows, :] = gr
    out = y + prm_ref[4:5, :]
    dh = jnp.zeros((FFN_TILE, width), F32)
    for c in range(hid_ref.shape[1] // chunk):
        cs = slice(c * chunk, (c + 1) * chunk)
        u = dot(h, wi(cs)) + bin_ref[bin_row : bin_row + 1, cs]
        cdf = 0.5 + 0.5 * lax.erf(u * math.sqrt(0.5))
        slope = cdf + u * jnp.exp2(u * u * (-0.5 * LOG2E)) * (1.0 / math.sqrt(2.0 * math.pi))
        hid = (u * cdf).astype(BF)
        hid_ref[rows, cs] = hid
        out = out + dot(hid, wf(c))
        du = (dot_bt(gr, wf(c)) * slope).astype(BF)
        du_ref[rows, cs] = du
        gprm_ref[5 + c : 6 + c, :] += jnp.sum(du.astype(F32), axis=0, keepdims=True)
        dh = dh + dot_bt(du, wi(cs))
    act_ref[rows, :] = out.astype(BF)
    gprm_ref[2:3, :] += jnp.sum(dh * unit, axis=0, keepdims=True)
    gprm_ref[3:4, :] += jnp.sum(dh, axis=0, keepdims=True)
    gprm_ref[4:5, :] += jnp.sum(g, axis=0, keepdims=True)
    dy = g + norm_back(dh, unit, inv, gain)
    dy_ref[rows, :] = dy
    dor = dy.astype(BF)
    dor_ref[rows, :] = dor
    datt_ref[rows, :] = dot_bt(dor, wo())


def ffn_norm(t, x_ref, attr_ref, cot_ref, wo, prm_ref, seq_ref, y_ref, h_ref, gr_ref):
    rows = tile_at(t, FFN_TILE)
    y = x_ref[rows, :].astype(F32) + dot(attr_ref[rows, :], wo)
    y_ref[rows, :] = y
    unit, _ = centred(y)
    h_ref[rows, :] = (unit * prm_ref[2:3, :] + prm_ref[3:4, :]).astype(BF)
    gr_ref[rows, :] = (cot_ref[rows, :].astype(F32) * seq_ref[0:1, 0:1]).astype(BF)


def ffn_chunk(t, c, wi, wf, bias, h_ref, gr_ref, hid_ref, du_ref, gprm_ref):
    rows = tile_at(t, FFN_TILE)
    width = h_ref.shape[1]
    cs = slice(c * width, (c + 1) * width)
    u = dot(h_ref[rows, :], wi) + bias
    cdf = 0.5 + 0.5 * lax.erf(u * math.sqrt(0.5))
    slope = cdf + u * jnp.exp2(u * u * (-0.5 * LOG2E)) * (1.0 / math.sqrt(2.0 * math.pi))
    hid_ref[rows, cs] = (u * cdf).astype(BF)
    du = (dot_bt(gr_ref[rows, :], wf) * slope).astype(BF)
    du_ref[rows, cs] = du
    gprm_ref[5 + c : 6 + c, :] += jnp.sum(du.astype(F32), axis=0, keepdims=True)


def ffn_final(
    t, cot_ref, wo, wi, wf, prm_ref, seq_ref, y_ref, hid_ref, du_ref,
    act_ref, dy_ref, dor_ref, datt_ref, gprm_ref,
):
    rows = tile_at(t, FFN_TILE)
    y = y_ref[rows, :]
    act_ref[rows, :] = (y + dot(hid_ref[rows, :], wf) + prm_ref[4:5, :]).astype(BF)
    dh = dot_bt(du_ref[rows, :], wi)
    unit, inv = centred(y)
    g = cot_ref[rows, :].astype(F32) * seq_ref[0:1, 0:1]
    gprm_ref[2:3, :] += jnp.sum(dh * unit, axis=0, keepdims=True)
    gprm_ref[3:4, :] += jnp.sum(dh, axis=0, keepdims=True)
    gprm_ref[4:5, :] += jnp.sum(g, axis=0, keepdims=True)
    dy = g + norm_back(dh, unit, inv, prm_ref[2:3, :])
    dy_ref[rows, :] = dy
    dor = dy.astype(BF)
    dor_ref[rows, :] = dor
    datt_ref[rows, :] = dot_bt(dor, wo)


def put_rows(g_ref, chunk, c, value):
    if len(g_ref.shape) == 5:
        g_ref[chunk, c] = value
    else:
        g_ref[chunk, lax.div(c, 2), lax.rem(c, 2)] = value.reshape(2, 2, *value.shape[1:])


def grads_out(c, hid_ref, gr_ref, g_ref):
    width = gr_ref.shape[1]
    grad = dot_at(hid_ref[:, tile_at(c)], gr_ref[...]).astype(BF)
    grad = grad.reshape(4, 4, 16, width)
    for q in range(4):
        put_rows(g_ref, q, c, grad[:, q])


def grads_in(c, h_ref, du_ref, attr_ref, dor_ref, g_ref):
    width = h_ref.shape[1]
    count = du_ref.shape[1] // width
    cs = tile_at(c)
    at = pl.ds(c * 4, 4)
    grad = dot_at(h_ref[:, cs], du_ref[...]).astype(BF)
    for k in range(count):
        g_ref[4 + k, at] = grad[:, k * width : (k + 1) * width].reshape(4, 4, 16, width)
    grad = dot_at(attr_ref[:, cs], dor_ref[...]).astype(BF)
    g_ref[4 + count, at] = grad.reshape(4, 4, 16, width)


def loop(start, stop, step):
    def run(i, carry):
        step(i)
        return carry

    lax.fori_loop(start, stop, run, 0)


def middle_kernel(
    x_ref, attr_ref, cot_ref, wo_ref, wi_ref, wf_ref, prm_ref, seq_ref,
    act_ref, dy_ref, datt_ref, gprm_ref, g_ref,
    hid_ref, du_ref, h_ref, gr_ref, dor_ref, bin_ref,
):
    length, width = x_ref.shape
    gprm_ref[...] = jnp.zeros_like(gprm_ref)
    bin_ref[...] = dot_bt(unit_rows(8), wf_ref[:, width:])
    loop(0, length // FFN_TILE, lambda t: ffn_rows(
        t, x_ref, attr_ref, cot_ref, lambda: wo_ref[...], lambda cs: wi_ref[:, cs],
        lambda c: wf_ref[c * width : (c + 1) * width, :width], prm_ref, bin_ref, seq_ref,
        act_ref, dy_ref, datt_ref, gprm_ref, hid_ref, du_ref, h_ref, gr_ref, dor_ref,
    ))
    loop(0, hid_ref.shape[1] // TILE, lambda c: grads_out(c, hid_ref, gr_ref, g_ref))
    loop(0, width // TILE, lambda c: grads_in(c, h_ref, du_ref, attr_ref, dor_ref, g_ref))


def back_pair(
    p, factor, q_ref, k_ref, v_ref, pq_ref, pk_ref, att_ref, den_ref, datt_ref, fx_ref, low_ref,
    ht_ref, dqkv_ref, dn_ref, e_ref, da_ref, tick, store,
):
    length = q_ref.shape[0]
    feats = fx_ref.shape[1]
    lanes = tile_at(p, LANES)
    blocks = length // BLOCK
    cols = [tile_at(2 * p + hh, feats) for hh in range(2)]
    two = jnp.where(lane_ids(length) < 2, 1.0, 0.0).astype(BF)
    v2 = jnp.concatenate([v_ref[:, lanes], two], axis=1)
    for t in range(length // TILE):
        rows = slice(t * TILE, (t + 1) * TILE)
        dn = datt_ref[rows, lanes] / den_ref[rows, lanes]
        prod = dn * att_ref[rows, lanes].astype(F32)
        lane = lane_ids(TILE)
        for hh in range(2):
            mine = lane // 64 == hh
            dden = -jnp.sum(jnp.where(mine, prod, 0.0), axis=-1, keepdims=True)
            high = dden.astype(BF).astype(F32)
            extra = jnp.where(lane == 0, high, jnp.where(lane == 1, dden - high, 0.0))
            dn_ref[hh, rows, :LANES] = jnp.where(mine, dn, 0.0).astype(BF)
            dn_ref[hh, rows, LANES:] = extra.astype(BF)
    for hh in range(2):
        fx = fx_ref[2 * p + hh]
        back = [None] * blocks
        total = None
        for b in range(blocks - 1, 0, -1):
            block = slice(b * BLOCK, (b + 1) * BLOCK)
            more = dot_at(pq_ref[block, cols[hh]], dn_ref[hh, block, :])
            total = more if total is None else total + more
            dz = total[:, LANES : LANES + 1] + total[:, LANES + 1 : LANES + 2]
            high = dz.astype(BF).astype(F32)
            lane = lane_ids(feats)
            extra = jnp.where(lane == 0, high, jnp.where(lane == 1, dz - high, 0.0))
            back[b - 1] = jnp.concatenate([total[:, :LANES], extra], axis=1).astype(BF)

        def put(value, rows, at, hh=hh):
            where = pl.ds(pl.multiple_of((3 * p + at) * LANES, LANES), LANES)
            if hh:
                mine = lane_ids(value.shape[0]) >= 64
                value = jnp.where(mine, value, dqkv_ref[rows, where].astype(F32))
            dqkv_ref[rows, where] = value.astype(BF)

        for b in range(blocks):
            base = b * BLOCK
            for i in range(BLOCK // TILE):
                rows = slice(base + i * TILE, base + (i + 1) * TILE)
                keys = slice(base, base + (i + 1) * TILE)
                dn = dn_ref[hh, rows, :]
                da = causal(dot_bt(dn, v2[keys]), i * TILE)
                da_ref[i * TILE : (i + 1) * TILE, : (i + 1) * TILE] = da
                grad = dot(da, pk_ref[keys, cols[hh]])
                if b:
                    grad = grad + dot_bt(dn, low_ref[2 * p + hh, b - 1])
                e_ref[0, rows, :] = (grad * pq_ref[rows, cols[hh]].astype(F32)).astype(BF)
            tick((hh * blocks + b) * 2)
            for i in range(BLOCK // TILE):
                rows = slice(base + i * TILE, base + (i + 1) * TILE)
                later = slice(base + i * TILE, base + BLOCK)
                pk = pk_ref[rows, cols[hh]]
                pql = pq_ref[later, cols[hh]]
                grad = dot_at(da_ref[i * TILE :, i * TILE : (i + 1) * TILE], pql)
                at = anticausal(dot_bt(pk, pql))
                dv = dot(at, dn_ref[hh, later, :LANES])
                if b < blocks - 1:
                    grad = grad + dot_bt(v2[rows], back[b])
                    dv = dv + dot(pk, back[b][:, :LANES])
                e_ref[1, rows, :] = (grad * pk.astype(F32)).astype(BF)
                put(dv, rows, 2)
            tick((hh * blocks + b) * 2 + 1)
        for at, src in ((0, q_ref), (1, k_ref)):
            res = dot(e_ref[at], fx)
            out = (res[:, :LANES] - src[:, lanes].astype(F32) * res[:, LANES:]) * factor
            put(out, slice(0, length), at)
    store(dot(ht_ref[...], dqkv_ref[:, tile_at(p, 3 * LANES)]).astype(BF))


def input_rows(t, x_ref, wq, prm_ref, dqkv_ref, dy_ref, out_ref, gprm_ref):
    rows = tile_at(t, FFN_TILE)
    dh = dot_bt(dqkv_ref[rows, : wq.shape[1]], wq)
    unit, inv = centred(x_ref[rows, :].astype(F32))
    gprm_ref[0:1, :] += jnp.sum(dh * unit, axis=0, keepdims=True)
    gprm_ref[1:2, :] += jnp.sum(dh, axis=0, keepdims=True)
    out_ref[rows, :] = (dy_ref[rows, :] + norm_back(dh, unit, inv, prm_ref[0:1, :])).astype(BF)


def flip_rows(h_ref, ht_ref):
    for t in range(h_ref.shape[0] // TILE):
        rows = slice(t * TILE, (t + 1) * TILE)
        ht_ref[:, rows] = h_ref[rows, :].T


def backward_kernel(
    factor, x_ref, h_ref, q_ref, k_ref, v_ref, pq_ref, pk_ref, att_ref, den_ref, datt_ref, dy_ref,
    wq_ref, fx_ref, prm_ref, gin_ref, low_ref,
    out_ref, gq_ref, gprm_ref,
    ht_ref, dqkv_ref, dn_ref, e_ref, da_ref,
):
    gprm_ref[...] = gin_ref[...]
    flip_rows(h_ref, ht_ref)

    def pair(p, carry):
        def store(value):
            gq_ref[:, tile_at(p, 3 * LANES)] = value

        back_pair(
            p, factor, q_ref, k_ref, v_ref, pq_ref, pk_ref, att_ref, den_ref, datt_ref, fx_ref, low_ref,
            ht_ref, dqkv_ref, dn_ref, e_ref, da_ref, lambda j: None, store,
        )
        return carry

    lax.fori_loop(0, x_ref.shape[1] // LANES, pair, 0)

    def rows(t, carry):
        input_rows(t, x_ref, wq_ref[...], prm_ref, dqkv_ref, dy_ref, out_ref, gprm_ref)
        return carry

    lax.fori_loop(0, x_ref.shape[0] // FFN_TILE, rows, 0)


def sequence_weight(small, seq_ref):
    nf = 4
    me = lax.axis_index("dp") * nf + lax.axis_index("fsdp")
    row = lax.broadcasted_iota(jnp.int32, small.shape, 0)
    lane = lane_ids(small.shape[0]).astype(F32)
    peer = lax.div(row, 16)
    ids = small[:, 5:6].astype(F32)
    hit = (lane == ids) & (lax.rem(row, 16) == 0)
    counts = jnp.sum(
        jnp.where(hit & (lax.rem(peer, nf) == lax.axis_index("fsdp")), 1.0, 0.0),
        axis=0, keepdims=True,
    )
    mine = jnp.sum(jnp.where(hit & (peer == me), 1.0, 0.0), axis=0, keepdims=True)
    size = jnp.sum(counts * mine, axis=1, keepdims=True)
    groups = jnp.sum(jnp.where(counts > 0.5, 1.0, 0.0), axis=1, keepdims=True)
    members = lax.axis_size("dp")
    seq_ref[...] = jnp.broadcast_to(members / (groups * size), seq_ref.shape)


class Columns:
    def __init__(self, ref, start, size):
        self.ref, self.start, self.size = ref, start, size

    def where(self, index):
        n, *rest = index if isinstance(index, tuple) else (index,)
        rows, cols = [*rest, slice(None), slice(None)][:2]
        base = self.start + n * self.size
        low, high = cols.start or 0, self.size if cols.stop is None else cols.stop
        return rows, slice(base + low, base + high)

    def __getitem__(self, index):
        return self.ref[self.where(index)]

    def __setitem__(self, index, value):
        self.ref[self.where(index)] = value


class Total:
    def __init__(self, place, ref, part, near, far, sems):
        self.place, self.ref, self.part, self.near, self.far = place, ref, part, near, far
        self.send, self.recv = sems

    def copies(self, stage):
        peers = self.place.far() if stage else self.place.near()
        src, dst = (self.part, self.far) if stage else (self.ref, self.near)
        for k, peer in enumerate(peers):
            yield remote(src, dst.at[k], self.send.at[stage, k], self.recv.at[stage, k], peer)

    def start(self):
        for copy in self.copies(0):
            copy.start()

    def turn(self):
        for copy in self.copies(0):
            copy.wait_recv()
        self.part[...] = self.ref[...] + sum(self.near[k] for k in range(self.near.shape[0]))
        for copy in self.copies(1):
            copy.start()

    def result(self):
        for copy in self.copies(1):
            copy.wait_recv()
        return self.part[...] + sum(self.far[k] for k in range(self.far.shape[0]))

    def drain(self):
        for stage in range(2):
            for copy in self.copies(stage):
                copy.wait_send()


def layer_kernel(
    nz, factor, x_ref, cot_in, wqs_ref, wos_ref, wis_ref, wfs_ref, fm_ref, id_ref,
    g1_ref, s1_ref, g2_ref, s2_ref, bo_ref, bi_ref,
    act_out, grad_out, partq_ref, gf_ref, gi_ref, go_ref, rest_out, first_out,
    h_ref, q_ref, k_ref, v_ref, pq_ref, pk_ref, attr_ref, den_ref, low_ref,
    wqt_ref, wq_ref, wo_ref, wi_ref, wf_ref, sp_ref, cot_ref, fx_ref, vec_ref, col_ref, prm_ref,
    act_ref, dy_ref, y_ref, g_ref, gprm_ref, hid_ref, du_ref, h2_ref, gr_ref, dor_ref,
    bin_ref, seq_ref, lhs_ref, gq_ref,
    b0, b1, b2, b3, c0, c1, c2, c3,
    rest_ref, rest_part, rest_near, rest_far, first_ref, first_part, first_near, first_far,
    send, recv, own, big_send, big_recv, q_send, q_recv, rest_send, rest_recv, first_send, first_recv,
    local_sem, tile_sem,
):
    length, width = x_ref.shape
    hidden = hid_ref.shape[1]
    place = Place(nz)
    every = slice(None)
    sems = (send, recv, own)
    pairs, tiles, parts = width // LANES, length // TILE, hidden // width
    slabs = length // FFN_TILE

    def gather(name, shard, whole, view, m, plane=None, base=None):
        return Gather(place, shard, whole, view, sems, m, name in Y_FIRST, plane, base)

    both = (every, every)
    sp = gather("s", col_ref, sp_ref, (slice(0, 16), every), 0)
    o = gather("o", wos_ref, wo_ref, both, 1)
    f = gather("f", wfs_ref, wf_ref, both, 2)
    wq = [gather(f"q{p}", wqt_ref.at[p], wq_ref.at[p], both, 3 + p) for p in range(pairs)]
    wi = [
        gather(f"i{c}", wis_ref, wi_ref, (every, slice(c * width, (c + 1) * width)), 3 + pairs + c)
        for c in range(parts)
    ]
    wf = [
        gather(f"f{c}", wfs_ref, wf_ref, both, 3 + pairs + parts + c, c, f) for c in range(parts)
    ]
    named = {"s": sp, "o": o}
    for n in range(pairs):
        named[f"q{n}"] = wq[n]
    for n in range(parts):
        named[f"i{n}"] = wi[n]
        named[f"f{n}"] = wf[n]

    def write(c, value):
        if c < 4:
            gf_ref[c] = value
        elif c < 4 + parts:
            gi_ref[:, (c - 4) * width : (c - 3) * width] = value
        else:
            go_ref[...] = value

    def write_q(c, value):
        for at in range(3):
            where = pl.ds(pl.multiple_of(c * LANES + at * width, LANES), LANES)
            partq_ref[:, where] = value[:, at * LANES : (at + 1) * LANES]

    grid = (nz, 2, 2, 2)
    big = Reduce(place, g_ref, (b0, b1, b2, b3), (big_send, big_recv), write)
    mine = Reduce(place, gq_ref, (c0, c1, c2, c3), (q_send, q_recv), write_q)
    rest = Total(place, rest_ref, rest_part, rest_near, rest_far, (rest_send, rest_recv))
    first = Total(place, first_ref, first_part, first_near, first_far, (first_send, first_recv))
    cot_copy = pltpu.make_async_copy(cot_in, cot_ref, local_sem)

    def slab_out(t, src, dst, n):
        rows = tile_at(t, FFN_TILE)
        return pltpu.make_async_copy(src.at[rows], dst.at[rows], tile_sem.at[n, t])

    def at_site(name):
        for who, stage in PLAN.get(name, ()):
            named[who].step(stage)
        for c, stage in SUMS.get(name, ()):
            big.step(stage, c, c % 2 == 0)
        for c, stage in OWN_SUMS.get(name, ()):
            mine.step(stage, c)

    def sites(p, prefix):
        def site(j):
            for n in range(pairs):
                name = f"{prefix}{n}:{j}"
                if name in PLAN or name in SUMS or name in OWN_SUMS:
                    pl.when(p == n)(functools.partial(at_site, name))

        return site

    vec_ref[...] = jnp.zeros_like(vec_ref)
    for n, ref in enumerate((g1_ref, s1_ref, g2_ref, s2_ref, bo_ref)):
        vec_ref[n : n + 1, : ref.shape[1]] = ref[...].astype(F32)
    vec_ref[5:6, :] = jnp.full((1, LANES), id_ref[0], jnp.int32).astype(F32)
    for n in range(4):
        vec_ref[8 + n : 9 + n, :16] = bi_ref[:, n * 16 : (n + 1) * 16].astype(F32)
    col_ref[...] = dot_at(vec_ref[...].astype(BF), unit_rows(16)).astype(BF)
    for p in range(pairs):
        for n in range(3):
            at = n * width + p * LANES
            wqt_ref[p, :, n * LANES : (n + 1) * LANES] = wqs_ref[:, at : at + LANES]
    place.barrier()
    for g in (sp, *wq, o, wi[0], f, *wi[1:]):
        g.start()
    cot_copy.start()
    head_size, feats = fm_ref.shape[1:]
    for n in range(fm_ref.shape[0]):
        row = lax.broadcasted_iota(jnp.int32, (head_size, LANES), 0)
        place_at = jnp.where(lane_ids(head_size) == row + (n % 2) * head_size, 1.0, 0.0).astype(BF)
        fx_ref[n, :, :LANES] = dot_at(fm_ref[n], place_at).astype(BF)
        fx_ref[n, :, LANES:] = jnp.ones((feats, LANES), BF)
    at_site("start")
    sp.arrive(3)
    small = sp_ref[...].reshape(width, LANES)
    prm = dot_bt(unit_rows(16), small)
    prm_ref[...] = prm[:8]
    sequence_weight(small, seq_ref)
    for c in range(parts):
        for n in range(4):
            lhs_ref[n, c : c + 1, :] = prm[8 + n : 9 + n, c * LANES : (c + 1) * LANES]
    row = lax.broadcasted_iota(jnp.int32, (LANES, width), 0)
    col = lax.broadcasted_iota(jnp.int32, (LANES, width), 1)
    bias = jnp.zeros((8, width), F32)
    for n in range(4):
        spread = (lax.div(row, 16) == lax.div(col, 64)) & (
            lax.rem(row, 16) + n * 16 == lax.rem(col, 64)
        )
        bias = bias + dot(lhs_ref[n].astype(BF), jnp.where(spread, 1.0, 0.0).astype(BF))
    bin_ref[...] = bias
    gprm_ref[...] = jnp.zeros_like(gprm_ref)

    def rows(i):
        rows = tile_at(i)
        unit, _ = centred(x_ref[rows, :].astype(F32))
        h_ref[rows, :] = (unit * prm_ref[0:1, :] + prm_ref[1:2, :]).astype(BF)

    loop(0, tiles, rows)

    def pair(p):
        site = sites(p, "")
        for n in range(pairs):
            pl.when(p == n)(functools.partial(wq[n].arrive, 3))
        lanes = tile_at(p, LANES)
        for t in range(tiles):
            rows = slice(t * TILE, (t + 1) * TILE)
            qkv = dot(h_ref[rows, :], wq_ref[p].reshape(width, 3 * LANES))
            q_ref[rows, lanes] = (qkv[:, :LANES] * factor).astype(BF)
            k_ref[rows, lanes] = (qkv[:, LANES : 2 * LANES] * factor).astype(BF)
            v_ref[rows, lanes] = qkv[:, 2 * LANES :].astype(BF)
            site(t)
        attend_pair(
            p, q_ref, k_ref, v_ref, fx_ref, pq_ref, pk_ref, attr_ref, den_ref, low_ref,
            lambda j: site(tiles + j),
        )

    loop(0, pairs, pair)
    o.arrive(3)
    cot_copy.wait()

    def norm(t):
        wo = wo_ref[...].reshape(width, width)
        ffn_norm(t, x_ref, attr_ref, cot_ref, wo, prm_ref, seq_ref, y_ref, h2_ref, gr_ref)

    loop(0, slabs, norm)
    at_site("norm")
    for c in range(parts):
        wi[c].arrive(3)
        wf[c].arrive(3)
        cs = slice(c * width, (c + 1) * width)

        def chunk(t, c=c, cs=cs):
            w_in, w_out = wi_ref[..., cs].reshape(width, width), wf_ref[c].reshape(width, width)
            bias = bin_ref[c : c + 1, :]
            ffn_chunk(t, c, w_in, w_out, bias, h2_ref, gr_ref, hid_ref, du_ref, gprm_ref)

        loop(0, slabs, chunk)
        at_site(f"chunk{c}")
        loop(2 * c, 2 * c + 2, lambda n: grads_out(n, hid_ref, gr_ref, g_ref))

        def grad(n, c=c, cs=cs):
            value = dot_at(h2_ref[:, tile_at(n)], du_ref[:, cs]).astype(BF)
            g_ref[4 + c, pl.ds(n * 2, 2)] = value.reshape(2, 2, 2, 2, 16, width)

        loop(0, width // TILE, grad)
        at_site(f"grad{c}")

    def final(t):
        ffn_final(
            t, cot_ref, wo_ref[...].reshape(width, width), wi_ref[...].reshape(width, hidden),
            wf_ref[...].reshape(hidden, width), prm_ref, seq_ref, y_ref, hid_ref, du_ref,
            act_ref, dy_ref, dor_ref, y_ref, gprm_ref,
        )
        slab_out(t, act_ref, act_out, 0).start()

    loop(0, slabs, final)
    at_site("final")

    def grad_o(n):
        value = dot_at(attr_ref[:, tile_at(n)], dor_ref[...]).astype(BF)
        g_ref[4 + parts, pl.ds(n * 2, 2)] = value.reshape(2, 2, 2, 2, 16, width)

    loop(0, width // TILE, grad_o)
    at_site("grad_o")
    for n in range(3 + parts):
        for c in range(pairs):
            rest_ref[n * pairs + c : n * pairs + c + 1, :] = gprm_ref[2 + n : 3 + n, c * LANES : (c + 1) * LANES]
    for n in range((3 + parts) * pairs, rest_ref.shape[0]):
        rest_ref[n : n + 1, :] = jnp.zeros((1, LANES), F32)
    rest.start()

    ht_ref = du_ref.at[0:width, 0:length]
    da_ref = du_ref.at[width : 2 * width, 0:BLOCK]
    dn_ref = Columns(du_ref, length, 2 * LANES)
    e_ref = Columns(du_ref, length + 4 * LANES, 2 * LANES)
    dqkv_ref = hid_ref
    out_ref = h2_ref
    flip_rows(h_ref, ht_ref)

    def back(p):
        def store(value):
            gq_ref[p] = value.reshape(*grid, 16, 3 * LANES)

        back_pair(
            p, factor, q_ref, k_ref, v_ref, pq_ref, pk_ref, attr_ref, den_ref, y_ref, fx_ref,
            low_ref, ht_ref, dqkv_ref, dn_ref, e_ref, da_ref, sites(p, "b"), store,
        )
        mine.step(0, p)

        @pl.when(p == 0)
        def _():
            rest.turn()

    loop(0, pairs, back)
    last = pairs - 1

    def rows_back(t):
        weights = [wq_ref[p].reshape(width, 3 * LANES) for p in range(pairs)]
        input_rows(
            t, x_ref, jnp.concatenate(weights, axis=1), prm_ref, dqkv_ref, dy_ref, out_ref, gprm_ref
        )
        slab_out(t, out_ref, grad_out, 1).start()

    mine.step(2, last - 1)
    loop(0, slabs // 2, rows_back)
    mine.step(1, last)
    mine.step(4, last - 2)
    loop(slabs // 2, slabs, rows_back)
    for n in range(2):
        for c in range(pairs):
            first_ref[n * pairs + c : n * pairs + c + 1, :] = gprm_ref[n : n + 1, c * LANES : (c + 1) * LANES]
    first.start()
    mine.step(3, last - 1)
    mine.step(2, last)
    first.turn()
    rest_out[...] = rest.result()
    mine.step(3, last)
    first_out[...] = first.result()
    mine.step(4, last - 1)
    mine.step(4, last)
    for t in range(slabs):
        slab_out(t, act_ref, act_out, 0).wait()
        slab_out(t, out_ref, grad_out, 1).wait()
    for g in (sp, o, *wq, *wi):
        g.drain()
    f.drain((0,))
    for g in wf:
        g.drain((1, 2, 3))
    for c in range(g_ref.shape[0]):
        big.drain(c, c % 2 == 0)
    loop(0, pairs, mine.drain)
    rest.drain()
    first.drain()


def finish_kernel(
    act_in, grad_in, gq_in, gf_in, gi_in, go_in, rest_in, first_in,
    act_ref, grad_ref, gq_ref, go_ref, gi_ref, gf_ref,
    g1_ref, s1_ref, g2_ref, s2_ref, bi_ref, bo_ref,
    hold_ref, in_sem, out_sem,
):
    moves = []
    for n, (src, dst) in enumerate(((act_in, act_ref), (grad_in, grad_ref))):
        for t in range(src.shape[0] // TILE):
            rows = pl.ds(t * TILE, TILE)
            hold = hold_ref.at[n, rows]
            moves.append((
                pltpu.make_async_copy(src.at[rows], hold, in_sem.at[n, t]),
                pltpu.make_async_copy(hold, dst.at[rows], out_sem.at[n, t]),
            ))
    for come, _ in moves:
        come.start()
    gq_ref[...] = gq_in[...]
    go_ref[...] = go_in[...]
    gi_ref[...] = gi_in[...]
    gf_ref[...] = gf_in[...].reshape(gf_ref.shape)
    me = lax.axis_index("dp") * 4 + lax.axis_index("fsdp")
    row = lax.broadcasted_iota(jnp.int32, (LANES, LANES), 0)
    lane = lane_ids(LANES)

    def cut(value, start):
        pick = jnp.where(row == lane + start, 1.0, 0.0)
        return lax.dot_general(
            value, pick, (((1,), (0,)), ((), ())), precision=lax.Precision.HIGHEST,
            preferred_element_type=F32,
        )

    def only(value, base, count, which):
        part = value[base : base + count]
        at = lax.broadcasted_iota(jnp.int32, part.shape, 0)
        return jnp.sum(jnp.where(at == which, part, 0.0), axis=0, keepdims=True)

    for come, go in moves:
        come.wait()
        go.start()
    pairs = first_in.shape[0] // 2
    spot = lax.rem(me, 8) * 16
    first, rest = cut(first_in[...], spot), cut(rest_in[...], spot)
    which = lax.div(me, 8)
    for n, ref in enumerate((g1_ref, s1_ref)):
        ref[...] = only(first, n * pairs, pairs, which)[:, :16]
    for n, ref in enumerate((g2_ref, s2_ref, bo_ref)):
        ref[...] = only(rest, n * pairs, pairs, which)[:, :16]
    wide = cut(rest_in[...], lax.rem(me, 2) * 64)
    each = pairs * pairs
    bi_ref[...] = only(wide, 3 * pairs, each, lax.div(me, 2))[:, :64]
    for _, go in moves:
        go.wait()


ANY = pl.BlockSpec(memory_space=pl.ANY)
VM = pl.BlockSpec(memory_space=pltpu.VMEM)


def call(kernel, outs, scratch, name, ins=None, out_specs=None, collective=None):
    extra = {} if ins is None else {"in_specs": ins, "out_specs": out_specs}
    params = {} if collective is None else {"collective_id": collective, "has_side_effects": True}
    return pl.pallas_call(
        kernel,
        out_shape=[jax.ShapeDtypeStruct(s, d) for s, d in outs],
        scratch_shapes=[pltpu.SemaphoreType.DMA(s) if d is None else pltpu.VMEM(s, d) for s, d in scratch],
        compiler_params=pltpu.CompilerParams(vmem_limit_bytes=60 * 2**20, **params),
        name=name,
        **extra,
    )


def padded_features(fm):
    heads, feats, _ = fm.shape
    zero = jnp.zeros_like(fm)
    even = (jnp.arange(heads) % 2 == 0)[:, None, None]
    return jnp.concatenate(
        [jnp.where(even, fm, zero), jnp.where(even, zero, fm), jnp.ones((heads, feats, LANES), BF)],
        axis=-1,
    )


def by_pair(columns, outer):
    rows, count = columns.shape
    split = columns.reshape(rows, outer, count // (outer * LANES), LANES)
    return split.swapaxes(1, 2).reshape(rows, count)


def middle(tokens, attr, cotangent, wo, wi, wf, prm, seq_weight):
    length, width = tokens.shape
    hidden = wi.shape[1]
    big, deep = (length, width), (length, hidden)
    chunks = 5 + hidden // width
    return call(
        middle_kernel,
        [(big, BF), (big, F32), (big, F32), ((16, width), F32), ((chunks, width // 64, 4, 16, width), BF)],
        [(deep, BF), (deep, BF), (big, BF), (big, BF), (big, BF), ((8, hidden), F32)],
        "middle",
    )(tokens, attr, cotangent, wo, wi, wf, prm, seq_weight)


def forward_outs(length, width, heads, feats):
    big = (length, width)
    deep = (length, heads * feats)
    low = (heads, length // BLOCK - 1, feats, 2 * LANES)
    return [(big, BF)] * 4 + [(deep, BF)] * 2 + [(big, BF), (big, F32), (low, BF)]


def backward_scratch(length, width):
    return [
        ((width, length), BF), ((length, 3 * width), BF),
        ((2, length, 2 * LANES), BF), ((2, length, 2 * LANES), BF), ((BLOCK, BLOCK), BF),
    ]


def plain_body(
    tokens, cotangent, group_id, w_qkv, w_out, w_ffn_in, w_ffn_out,
    gain_one, shift_one, gain_two, shift_two, bias_in, bias_out, feature_matrix,
):
    gather = functools.partial(lax.all_gather, axis_name=AXES, axis=0, tiled=True)
    scatter = functools.partial(
        lax.psum_scatter, axis_name=AXES, scatter_dimension=0, tiled=True
    )
    length, width = tokens.shape
    heads, feats, head_size = feature_matrix.shape
    hidden = w_ffn_in.shape[1]
    factor = head_size ** (-0.25)
    wq, wo, wi, wf = gather(w_qkv), gather(w_out), gather(w_ffn_in), gather(w_ffn_out)
    prm = gather(jnp.stack([gain_one, shift_one, gain_two, shift_two, bias_out], axis=1))
    prm = jnp.pad(prm.T.astype(F32), ((0, 3), (0, 0)))
    wf = jnp.concatenate([wf, jnp.pad(gather(bias_in)[:, None], ((0, 0), (0, LANES - 1)))], axis=1)

    slice_seqs = lax.axis_size("dp") * group_id.shape[0]
    labels = jnp.arange(slice_seqs // 2, dtype=jnp.int32)
    onehot = (group_id[:, None] == labels[None, :]).astype(F32)
    counts = lax.psum(jnp.sum(onehot, axis=0), "dp")
    group_size = jnp.sum(onehot * counts[None, :], axis=-1)
    groups = jnp.sum((counts > 0.5).astype(F32))
    seq_weight = jnp.broadcast_to((slice_seqs / (groups * group_size))[:, None], (8, LANES))

    fx = padded_features(feature_matrix)
    h1, q, k, v, pq, pk, attr, den, low = call(
        functools.partial(forward_kernel, factor),
        forward_outs(length, width, heads, feats), [], "forward",
    )(tokens, wq, prm, fx)
    act, dy, datt, gprm, grads = middle(tokens, attr, cotangent, wo, wi, wf, prm, seq_weight)
    input_grad, gq, gprm = call(
        functools.partial(backward_kernel, factor),
        [((length, width), BF), ((width, 3 * width), BF), ((16, width), F32)],
        backward_scratch(length, width), "backward",
    )(tokens, h1, q, k, v, pq, pk, attr, den, datt, dy, by_pair(wq, 3), fx, prm, gprm, low)
    gq = by_pair(gq, width // LANES)
    grads = grads.reshape(-1, width // 16, 16, width)
    gf = grads[:4].transpose(1, 0, 2, 3).reshape(hidden, width)
    gi = grads[4:-1].transpose(1, 2, 0, 3).reshape(width, hidden)
    go = grads[-1].reshape(width, width)
    small = scatter(gprm[:8].T)
    gbin = scatter(gprm[5 : 5 + hidden // width].reshape(hidden))
    part = [scatter(t).astype(F32) for t in (gq, go, gi, gf)]
    return (act, input_grad, *part, *(small[:, i] for i in range(4)), gbin, small[:, 4])


def ring_body(
    tokens, cotangent, group_id, w_qkv, w_out, w_ffn_in, w_ffn_out,
    gain_one, shift_one, gain_two, shift_two, bias_in, bias_out, feature_matrix,
):
    length, width = tokens.shape
    heads, feats, head_size = feature_matrix.shape
    hidden = w_ffn_in.shape[1]
    factor = head_size ** (-0.25)
    nz = lax.axis_size("dp") // 2
    grid = (nz, 2, 2, 2)
    wide = 3 * width
    pairs = width // LANES
    parts = hidden // width
    chunks, many = 5 + parts, 3 + pairs + 2 * parts
    wqs = (pairs, *grid, 16, 3 * LANES)
    big, deep, tall = (length, width), (length, heads * feats), (length, hidden)
    half = (-(-(3 + parts) * pairs // 8) * 8, LANES)
    pair_rows = (2 * pairs, LANES)
    near, far = 3, 2 * nz - 1
    act, input_grad, gq, gf, gi, go, rest, first = call(
        functools.partial(layer_kernel, nz, factor),
        [
            (big, BF), (big, BF), ((16, wide), F32), ((4, 16, width), F32), ((16, hidden), F32),
            ((16, width), F32), (half, F32), (pair_rows, F32),
        ],
        [
            *[(big, BF)] * 4, *[(deep, BF)] * 2, (big, BF), (big, F32),
            ((heads, length // BLOCK - 1, feats, 2 * LANES), BF),
            ((pairs, 16, 3 * LANES), BF), (wqs, BF), ((*grid, 16, width), BF),
            ((*grid, 16, hidden), BF), ((*grid, 64, width), BF), ((*grid, 16, LANES), BF), (big, BF),
            ((heads, feats, 2 * LANES), BF), ((16, LANES), F32), ((LANES, LANES), BF),
            ((8, width), F32),
            (big, BF), (big, F32), (big, F32), ((chunks, *grid, 16, width), BF), ((16, width), F32),
            (tall, BF), (tall, BF), (big, BF), (big, BF), (big, BF),
            ((8, width), F32), ((8, LANES), F32), ((4, 8, LANES), F32),
            ((pairs, *grid, 16, 3 * LANES), BF),
            *Reduce.shapes(chunks, nz, 16, width),
            *Reduce.shapes(pairs, nz, 16, 3 * LANES),
            (half, F32), (half, F32), ((near, *half), F32), ((far, *half), F32),
            (pair_rows, F32), (pair_rows, F32), ((near, *pair_rows), F32), ((far, *pair_rows), F32),
            ((many, 4, nz - 1), None), ((many, 4, nz - 1), None), ((many,), None),
            ((chunks, 4, nz - 1), None), ((chunks, 4, nz - 1), None),
            ((pairs, 4, nz - 1), None), ((pairs, 4, nz - 1), None),
            ((2, far), None), ((2, far), None), ((2, far), None), ((2, far), None),
            ((), None), ((2, length // FFN_TILE), None),
        ],
        "layer",
        [VM, ANY, VM, ANY, ANY, ANY, VM, pl.BlockSpec(memory_space=pltpu.SMEM), *[VM] * 6],
        [ANY, ANY, *[VM] * 6],
        0,
    )(
        tokens, cotangent, w_qkv, w_out, w_ffn_in, w_ffn_out, feature_matrix.swapaxes(1, 2),
        group_id, *(t[None] for t in (gain_one, shift_one, gain_two, shift_two, bias_out, bias_in)),
    )
    act, input_grad, gq, go, gi, gf, *vecs = call(
        finish_kernel,
        [
            (big, BF), (big, BF), ((16, wide), F32), ((16, width), F32), ((16, hidden), F32),
            ((64, width), F32), *[((1, 16), F32)] * 4, ((1, 64), F32), ((1, 16), F32),
        ],
        [((2, length, width), BF), ((2, length // TILE), None), ((2, length // TILE), None)],
        "finish",
        [ANY, ANY, *[VM] * 6],
        [ANY, ANY, *[VM] * 10],
    )(act, input_grad, gq, gf, gi, go, rest, first)
    return (act, input_grad, gq, go, gi, gf, *(t[0] for t in vecs))


def solution(mesh):
    rows, vec = P(AXES, None), P(AXES)
    devices = mesh.shape["dp"] * mesh.shape["fsdp"]

    def body(*args):
        width = args[0].shape[1]
        ring = mesh.shape["fsdp"] == 4 and mesh.shape["dp"] % 2 == 0 and width == 16 * devices
        return (ring_body if ring else plain_body)(*args)

    return jax.shard_map(
        body,
        mesh=mesh,
        in_specs=(rows, rows, vec, *[rows] * 4, *[vec] * 6, P()),
        out_specs=(*[rows] * 6, *[vec] * 6),
        check_vma=False,
    )
```

time: 152 us -> 133 us (0.88)
  Pallas kernels: 151 us -> 132 us
    pallas_call x2 -> x1, Pallas kernels: 146 us -> 127 us  [ring_body(): call(functools.partial(layer_kernel, nz, factor), [(big, BF), (big, BF),...]
where the time goes in v4:
time: 133 us
  Pallas kernels  132 us (99%)
  between operations  1.46 us (1%)
    pallas_call x1, Pallas kernels, ring_body(): call(functools.partial(layer_kernel, nz, factor), [(big, BF), (big, BF),...  127 us
    pallas_call x1, Pallas kernels, ring_body(): call(finish_kernel, [(big, BF), (big, BF), ((16, wide), F32), ((16, width...  4.21 us

profile of v4, /device:TPU:0, one launch (start us, length us, event | category | flops | bytes accessed | tf_op | source)
XLA Modules:
  0.0 133.0 jit_solution(4317008315019416709)
XLA Ops:
  1.3 127.4 %layer.1 = (bf16[1024,512]{1,0:T(8,128)(2,1)}, bf16[1024,512]{1,0:T(8,128)(2,1)}, f32[16,1536]{1,0:T(8,128)}, f32[4,16,512]{2,1,0:T(8,128)}, f32[16,2048]{1,0:T(...) custom-call(bf16[1024,512]{1,0:T(8,128)(2,1)} %x_ref.1, bf16[1024,512]{1,0:T(8,128)(2,1)} %cot_in.1, ...), custom_call_target="tpu_custom_call" | custom-call | tf_op jit(solution)/shard_map/layer/pallas_call | solution.py:1209
  128.7 4.2 %finish.1 = (bf16[1024,512]{1,0:T(8,128)(2,1)}, bf16[1024,512]{1,0:T(8,128)(2,1)}, f32[16,1536]{1,0:T(8,128)}, f32[16,512]{1,0:T(8,128)}, f32[16,2048]{1,0:T(8,1...) custom-call(bf16[1024,512]{1,0:T(8,128)(2,1)} %get-tuple-element.32., ...), custom_call_target="tpu_custom_call" | custom-call | tf_op jit(solution)/shard_map/finish/pallas_call | solution.py:1244

commit v5 on v4

--- a/solution.py
+++ b/solution.py
@@ -85,58 +85,40 @@
     "grad2": ((6, 0),),
     "chunk3": ((6, 1), (5, 2), (4, 3)),
     "grad3": ((7, 0), (0, 0), (1, 0), (2, 0), (3, 0)),
-    "final": ((7, 1), (0, 1), (6, 2), (5, 3), (4, 4)),
+    "final": ((7, 1), (0, 1), (1, 1), (6, 2), (5, 3), (4, 4)),
     "grad_o": ((8, 0),),
-    "b0:1": ((1, 1),),
-    "b0:2": ((7, 2), (6, 3)),
-    "b0:3": ((2, 1),),
-    "b0:4": ((0, 2), (5, 4)),
-    "b0:5": ((3, 1),),
-    "b0:7": ((8, 1), (1, 2), (7, 3)),
-    "b1:1": ((2, 2), (6, 4)),
-    "b1:2": ((0, 3),),
-    "b1:3": ((3, 2), (1, 3)),
-    "b1:5": ((8, 2), (7, 4)),
-    "b1:6": ((2, 3), (0, 4)),
-    "b1:7": ((3, 3),),
-    "b2:0": ((1, 4), (8, 3)),
-    "b2:3": ((2, 4),),
-    "b2:4": ((3, 4),),
-    "b2:5": ((8, 4),),
+    "b0:0": ((2, 1), (3, 1), (8, 1)),
+    "b0:1": ((7, 2), (0, 2), (1, 2), (6, 3), (5, 4)),
+    "b1:0": ((2, 2), (3, 2), (8, 2)),
+    "b1:1": ((7, 3), (0, 3), (1, 3), (6, 4)),
+    "b2:0": ((2, 3), (3, 3), (8, 3)),
+    "b2:1": ((7, 4), (0, 4), (1, 4)),
+    "b3:0": ((2, 4), (3, 4), (8, 4)),
 }
 OWN_SUMS = {
-    "b1:2": ((0, 1),),
-    "b2:1": ((0, 2),),
-    "b2:2": ((1, 1),),
-    "b2:6": ((0, 3),),
-    "b3:1": ((1, 2),),
-    "b3:2": ((2, 1),),
-    "b3:4": ((0, 4),),
-    "b3:6": ((1, 3),),
+    "b1:0": ((0, 1),),
+    "b2:0": ((0, 2), (1, 1)),
+    "b3:0": ((0, 3), (1, 2), (2, 1)),
 }
 PLAN = {
-    "start": (("s", 1), ("q0", 1), ("q1", 1), ("q2", 1), ("s", 2), ("q3", 1), ("q0", 2), ("o", 1), ("q1", 2), ("i0", 1), ("q2", 2), ("s", 3), ("q3", 2), ("o", 2), ("q0", 3), ("i0", 2), ("q1", 3),),
-    "0:0": (("f0", 1), ("f1", 1), ("i1", 1), ("f2", 1),),
-    "0:1": (("q2", 3), ("f3", 1),),
-    "0:4": (("i2", 1),),
-    "0:8": (("q3", 3),),
-    "0:9": (("i3", 1),),
-    "1:3": (("i0", 3),),
-    "1:6": (("o", 3),),
-    "1:8": (("f1", 2),),
-    "1:11": (("f0", 2),),
-    "2:0": (("f3", 2),),
-    "2:4": (("i1", 2),),
-    "2:5": (("i2", 2),),
-    "2:8": (("f2", 2),),
-    "2:10": (("i3", 2),),
-    "3:7": (("f1", 3),),
-    "3:9": (("f0", 3),),
-    "chunk0": (("i1", 3), ("i2", 3), ("f3", 3),),
-    "grad0": (("f2", 3),),
-    "chunk1": (("i3", 3),),
+    "start": (("s", 1), ("q0", 1), ("q1", 1), ("q2", 1), ("s", 2), ("q3", 1), ("q0", 2), ("o", 1), ("q1", 2), ("i0", 1), ("s", 3), ("q2", 2), ("q3", 2), ("o", 2), ("q0", 3), ("i0", 2),),
+    "params": (("q1", 3), ("f0", 1), ("f1", 1), ("f2", 1), ("f3", 1),),
+    "0:0": (("q2", 3), ("q3", 3), ("i1", 1),),
+    "0:1": (("i2", 1),),
+    "0:2": (("o", 3), ("i3", 1),),
+    "1:0": (("i0", 3), ("f0", 2),),
+    "1:1": (("f1", 2),),
+    "1:2": (("i1", 2), ("f2", 2),),
+    "2:0": (("i2", 2),),
+    "2:1": (("i3", 2), ("f3", 2),),
+    "3:0": (("f0", 3),),
+    "3:1": (("f1", 3),),
+    "norm": (("i1", 3), ("f2", 3),),
+    "chunk0": (("i2", 3), ("f3", 3),),
+    "grad0": (("i3", 3),),
 }
-Y_FIRST = {"s", "q0", "q2", "q3", "o", "i2", "i3", "f1", "f3"}
+Y_FIRST = {"s", "q1", "q2", "i0", "i1", "i2", "i3", "f0"}
+LEAVE = ("s", "q0", "q1", "q2", "q3", "o", "i0", "F", "i1", "i2", "i3")
 
 
 class Place:
@@ -157,14 +139,17 @@
     def down(self, k):
         return lax.rem(self.z + self.nz - k, self.nz)
 
+    def around(self):
+        for k in range(1, 4 * self.nz):
+            y = 1 - self.y if k // 2 % 2 else self.y
+            x = 1 - self.x if k % 2 else self.x
+            yield (self.up(k // 4), y, x), (self.down(k // 4), y, x)
+
     def peers(self):
         yield self.device(c=1 - self.c)
-        yield self.device(x=1 - self.x)
-        yield self.device(y=1 - self.y)
         yield self.device(x=1 - self.x, c=1 - self.c)
-        for k in range(1, self.nz):
-            yield self.device(z=self.up(k))
-            yield self.device(z=self.up(k), y=1 - self.y)
+        for (z, y, x), _ in self.around():
+            yield self.device(z, y, x)
 
     def near(self):
         yield self.device(c=1 - self.c)
@@ -181,7 +166,7 @@
         sem = pltpu.get_barrier_semaphore()
         for peer in self.peers():
             pl.semaphore_signal(sem, inc=1, device_id=peer, device_id_type=MESH_ID)
-        pl.semaphore_wait(sem, 2 + 2 * self.nz)
+        pl.semaphore_wait(sem, 1 + 4 * self.nz)
 
 
 def remote(src, dst, send, recv, peer):
@@ -336,10 +321,30 @@
         for copy in self.copies(stage, c, x_first):
             copy.start()
 
-    def drain(self, c, x_first=False):
-        for stage in range(4):
+    def drain(self, c, x_first=False, stages=range(4)):
+        for stage in stages:
             for copy in self.copies(stage, c, x_first):
                 copy.wait_send()
+
+    def short(self, c, land, sems):
+        p = self.place
+        for k, (to, _) in enumerate(p.around()):
+            yield remote(self.r0.at[(c, *to)], land.at[k], sems[0].at[k], sems[1].at[k], p.device(*to))
+
+    def short_start(self, c, land, sems):
+        for copy in self.copies(0, c, False):
+            copy.wait_recv()
+        self.r0[c] = self.source[c, :, :, :, self.place.c] + self.r0[c]
+        for copy in self.short(c, land, sems):
+            copy.start()
+
+    def short_end(self, c, land, sems):
+        p = self.place
+        total = self.r0[c, p.z, p.y, p.x].astype(F32)
+        for k, copy in enumerate(self.short(c, land, sems)):
+            copy.wait_recv()
+            total = total + land[k].astype(F32)
+        self.write(c, total)
 
     @staticmethod
     def shapes(n, nz, rows, cols):
@@ -382,7 +387,7 @@
                 square = jnp.sum(wide * wide, axis=-1, keepdims=True)
                 feat = jnp.exp2(scores * LOG2E - (square * (0.5 * LOG2E) + shift))
                 dst[rows, cols[hh]] = feat.astype(BF)
-            site(2 * hh + int(src is k_ref))
+    site(1)
     ones = jnp.ones((length, LANES), BF)
     vx = jnp.concatenate([v_ref[:, lanes], ones], axis=1)
     states = [None, None]
@@ -404,7 +409,6 @@
             den = jnp.where(first, got[0][:, LANES:], got[1][:, LANES:])
             attr_ref[rows, lanes] = (num / den).astype(BF)
             den_ref[rows, lanes] = den
-            site(4 + b * (BLOCK // TILE) + i)
         if base + BLOCK < length:
             block = slice(base, base + BLOCK)
             for hh in range(2):
@@ -622,7 +626,6 @@
                 if b:
                     grad = grad + dot_bt(dn, low_ref[2 * p + hh, b - 1])
                 e_ref[0, rows, :] = (grad * pq_ref[rows, cols[hh]].astype(F32)).astype(BF)
-            tick((hh * blocks + b) * 2)
             for i in range(BLOCK // TILE):
                 rows = slice(base + i * TILE, base + (i + 1) * TILE)
                 later = slice(base + i * TILE, base + BLOCK)
@@ -636,11 +639,12 @@
                     dv = dv + dot(pk, back[b][:, :LANES])
                 e_ref[1, rows, :] = (grad * pk.astype(F32)).astype(BF)
                 put(dv, rows, 2)
-            tick((hh * blocks + b) * 2 + 1)
         for at, src in ((0, q_ref), (1, k_ref)):
             res = dot(e_ref[at], fx)
             out = (res[:, :LANES] - src[:, lanes].astype(F32) * res[:, LANES:]) * factor
             put(out, slice(0, length), at)
+        if hh == 0:
+            tick(0)
     store(dot(ht_ref[...], dqkv_ref[:, tile_at(p, 3 * LANES)]).astype(BF))
 
 
@@ -767,8 +771,9 @@
     bin_ref, seq_ref, lhs_ref, gq_ref,
     b0, b1, b2, b3, c0, c1, c2, c3,
     rest_ref, rest_part, rest_near, rest_far, first_ref, first_part, first_near, first_far,
+    land_ref,
     send, recv, own, big_send, big_recv, q_send, q_recv, rest_send, rest_recv, first_send, first_recv,
-    local_sem, tile_sem,
+    short_send, short_recv, local_sem, tile_sem,
 ):
     length, width = x_ref.shape
     hidden = hid_ref.shape[1]
@@ -793,7 +798,7 @@
     wf = [
         gather(f"f{c}", wfs_ref, wf_ref, both, 3 + pairs + parts + c, c, f) for c in range(parts)
     ]
-    named = {"s": sp, "o": o}
+    named = {"s": sp, "o": o, "F": f}
     for n in range(pairs):
         named[f"q{n}"] = wq[n]
     for n in range(parts):
@@ -818,6 +823,7 @@
     mine = Reduce(place, gq_ref, (c0, c1, c2, c3), (q_send, q_recv), write_q)
     rest = Total(place, rest_ref, rest_part, rest_near, rest_far, (rest_send, rest_recv))
     first = Total(place, first_ref, first_part, first_near, first_far, (first_send, first_recv))
+    short_sems = (short_send, short_recv)
     cot_copy = pltpu.make_async_copy(cot_in, cot_ref, local_sem)
 
     def slab_out(t, src, dst, n):
@@ -853,8 +859,8 @@
             at = n * width + p * LANES
             wqt_ref[p, :, n * LANES : (n + 1) * LANES] = wqs_ref[:, at : at + LANES]
     place.barrier()
-    for g in (sp, *wq, o, wi[0], f, *wi[1:]):
-        g.start()
+    for who in LEAVE:
+        named[who].start()
     cot_copy.start()
     head_size, feats = fm_ref.shape[1:]
     for n in range(fm_ref.shape[0]):
@@ -867,6 +873,7 @@
     small = sp_ref[...].reshape(width, LANES)
     prm = dot_bt(unit_rows(16), small)
     prm_ref[...] = prm[:8]
+    at_site("params")
     sequence_weight(small, seq_ref)
     for c in range(parts):
         for n in range(4):
@@ -888,6 +895,7 @@
         h_ref[rows, :] = (unit * prm_ref[0:1, :] + prm_ref[1:2, :]).astype(BF)
 
     loop(0, tiles, rows)
+    at_site("rows")
 
     def pair(p):
         site = sites(p, "")
@@ -900,11 +908,12 @@
             q_ref[rows, lanes] = (qkv[:, :LANES] * factor).astype(BF)
             k_ref[rows, lanes] = (qkv[:, LANES : 2 * LANES] * factor).astype(BF)
             v_ref[rows, lanes] = qkv[:, 2 * LANES :].astype(BF)
-            site(t)
+        site(0)
         attend_pair(
             p, q_ref, k_ref, v_ref, fx_ref, pq_ref, pk_ref, attr_ref, den_ref, low_ref,
-            lambda j: site(tiles + j),
+            site,
         )
+        site(2)
 
     loop(0, pairs, pair)
     o.arrive(3)
@@ -978,6 +987,7 @@
             low_ref, ht_ref, dqkv_ref, dn_ref, e_ref, da_ref, sites(p, "b"), store,
         )
         mine.step(0, p)
+        sites(p, "b")(1)
 
         @pl.when(p == 0)
         def _():
@@ -993,23 +1003,23 @@
         )
         slab_out(t, out_ref, grad_out, 1).start()
 
+    mine.step(3, last - 2)
     mine.step(2, last - 1)
     loop(0, slabs // 2, rows_back)
-    mine.step(1, last)
-    mine.step(4, last - 2)
+    mine.short_start(last, land_ref, short_sems)
     loop(slabs // 2, slabs, rows_back)
     for n in range(2):
         for c in range(pairs):
             first_ref[n * pairs + c : n * pairs + c + 1, :] = gprm_ref[n : n + 1, c * LANES : (c + 1) * LANES]
     first.start()
     mine.step(3, last - 1)
-    mine.step(2, last)
     first.turn()
     rest_out[...] = rest.result()
-    mine.step(3, last)
+    mine.step(4, last - 3)
+    mine.step(4, last - 2)
+    mine.step(4, last - 1)
     first_out[...] = first.result()
-    mine.step(4, last - 1)
-    mine.step(4, last)
+    mine.short_end(last, land_ref, short_sems)
     for t in range(slabs):
         slab_out(t, act_ref, act_out, 0).wait()
         slab_out(t, out_ref, grad_out, 1).wait()
@@ -1020,7 +1030,10 @@
         g.drain((1, 2, 3))
     for c in range(g_ref.shape[0]):
         big.drain(c, c % 2 == 0)
-    loop(0, pairs, mine.drain)
+    loop(0, last, mine.drain)
+    mine.drain(last, stages=(0,))
+    for copy in mine.short(last, land_ref, short_sems):
+        copy.wait_send()
     rest.drain()
     first.drain()
 
@@ -1227,10 +1240,12 @@
             *Reduce.shapes(pairs, nz, 16, 3 * LANES),
             (half, F32), (half, F32), ((near, *half), F32), ((far, *half), F32),
             (pair_rows, F32), (pair_rows, F32), ((near, *pair_rows), F32), ((far, *pair_rows), F32),
+            ((4 * nz - 1, 16, 3 * LANES), BF),
             ((many, 4, nz - 1), None), ((many, 4, nz - 1), None), ((many,), None),
             ((chunks, 4, nz - 1), None), ((chunks, 4, nz - 1), None),
             ((pairs, 4, nz - 1), None), ((pairs, 4, nz - 1), None),
             ((2, far), None), ((2, far), None), ((2, far), None), ((2, far), None),
+            ((4 * nz - 1,), None), ((4 * nz - 1,), None),
             ((), None), ((2, length // FFN_TILE), None),
         ],
         "layer",

time: 133 us -> 120 us (0.902)
  Pallas kernels: 132 us -> 118 us
    pallas_call x1, Pallas kernels: 127 us -> 114 us  [ring_body(): call(functools.partial(layer_kernel, nz, factor), [(big, BF), (big, BF),...]
where the time goes in v5:
time: 120 us
  Pallas kernels  118 us (98%)
  between operations  1.46 us (1%)
    pallas_call x1, Pallas kernels, ring_body(): call(functools.partial(layer_kernel, nz, factor), [(big, BF), (big, BF),...  114 us
    pallas_call x1, Pallas kernels, ring_body(): call(finish_kernel, [(big, BF), (big, BF), ((16, wide), F32), ((16, width...  4.21 us

profile of v5, /device:TPU:0, one launch (start us, length us, event | category | flops | bytes accessed | tf_op | source)
XLA Modules:
  0.0 119.6 jit_solution(10767189893492289312)
XLA Ops:
  1.3 113.9 %layer.1 = (bf16[1024,512]{1,0:T(8,128)(2,1)}, bf16[1024,512]{1,0:T(8,128)(2,1)}, f32[16,1536]{1,0:T(8,128)}, f32[4,16,512]{2,1,0:T(8,128)}, f32[16,2048]{1,0:T(...) custom-call(bf16[1024,512]{1,0:T(8,128)(2,1)} %x_ref.1, bf16[1024,512]{1,0:T(8,128)(2,1)} %cot_in.1, ...), custom_call_target="tpu_custom_call" | custom-call | tf_op jit(solution)/shard_map/layer/pallas_call | solution.py:1222
  115.2 4.2 %finish.1 = (bf16[1024,512]{1,0:T(8,128)(2,1)}, bf16[1024,512]{1,0:T(8,128)(2,1)}, f32[16,1536]{1,0:T(8,128)}, f32[16,512]{1,0:T(8,128)}, f32[16,2048]{1,0:T(8,1...) custom-call(bf16[1024,512]{1,0:T(8,128)(2,1)} %get-tuple-element.32., ...), custom_call_target="tpu_custom_call" | custom-call | tf_op jit(solution)/shard_map/finish/pallas_call | solution.py:1259

commit v6 on v5

--- a/solution.py
+++ b/solution.py
@@ -85,15 +85,14 @@
     "grad2": ((6, 0),),
     "chunk3": ((6, 1), (5, 2), (4, 3)),
     "grad3": ((7, 0), (0, 0), (1, 0), (2, 0), (3, 0)),
-    "final": ((7, 1), (0, 1), (1, 1), (6, 2), (5, 3), (4, 4)),
+    "final": ((7, 1), (0, 1), (1, 1), (6, 2), (5, 3)),
     "grad_o": ((8, 0),),
     "b0:0": ((2, 1), (3, 1), (8, 1)),
-    "b0:1": ((7, 2), (0, 2), (1, 2), (6, 3), (5, 4)),
+    "b0:1": ((7, 2), (0, 2), (1, 2), (6, 3)),
     "b1:0": ((2, 2), (3, 2), (8, 2)),
-    "b1:1": ((7, 3), (0, 3), (1, 3), (6, 4)),
+    "b1:1": ((7, 3), (0, 3), (1, 3)),
     "b2:0": ((2, 3), (3, 3), (8, 3)),
-    "b2:1": ((7, 4), (0, 4), (1, 4)),
-    "b3:0": ((2, 4), (3, 4), (8, 4)),
+    "tail": ((4, 4), (5, 4), (6, 4), (7, 4), (0, 4), (1, 4), (2, 4), (3, 4), (8, 4)),
 }
 OWN_SUMS = {
     "b1:0": ((0, 1),),
@@ -275,55 +274,57 @@
         self.send, self.recv = sems
         self.write = write
 
-    def hops(self, stage, c, x_first):
+    def hops(self, stage, cs, x_first):
         p = self.place
         every = slice(None)
+        r0, r1, r2, r3 = (ref.at[cs] for ref in (self.r0, self.r1, self.r2, self.r3))
         if stage == 0:
-            yield self.source.at[c, every, every, every, 1 - p.c], self.r0.at[c], p.device(c=1 - p.c)
+            yield self.source.at[cs, every, every, every, 1 - p.c], r0, p.device(c=1 - p.c)
         elif stage == 1:
             if x_first:
-                yield self.r0.at[c, every, every, 1 - p.x], self.r1.at[c], p.device(x=1 - p.x)
+                yield r0.at[every, every, every, 1 - p.x], r1, p.device(x=1 - p.x)
             else:
-                yield self.r0.at[c, every, 1 - p.y], self.r1.at[c], p.device(y=1 - p.y)
+                yield r0.at[every, every, 1 - p.y], r1, p.device(y=1 - p.y)
         elif stage == 2:
             if x_first:
-                yield self.r1.at[c, every, 1 - p.y], self.r2.at[c], p.device(y=1 - p.y)
+                yield r1.at[every, every, 1 - p.y], r2, p.device(y=1 - p.y)
             else:
-                yield self.r1.at[c, every, 1 - p.x], self.r2.at[c], p.device(x=1 - p.x)
+                yield r1.at[every, every, 1 - p.x], r2, p.device(x=1 - p.x)
         else:
             for k in range(1, p.nz):
-                yield self.r2.at[c, p.up(k)], self.r3.at[c, k - 1], p.device(z=p.up(k))
-
-    def copies(self, stage, c, x_first):
-        for k, (src, dst, peer) in enumerate(self.hops(stage, c, x_first)):
+                yield r2.at[every, p.up(k)], r3.at[every, k - 1], p.device(z=p.up(k))
+
+    def copies(self, stage, c, x_first, count=1):
+        for k, (src, dst, peer) in enumerate(self.hops(stage, pl.ds(c, count), x_first)):
             yield remote(src, dst, self.send.at[c, stage, k], self.recv.at[c, stage, k], peer)
 
-    def step(self, stage, c, x_first=False):
+    def step(self, stage, c, x_first=False, count=1):
         p = self.place
+        cs = pl.ds(c, count)
         if stage:
-            for copy in self.copies(stage - 1, c, x_first):
+            for copy in self.copies(stage - 1, c, x_first, count):
                 copy.wait_recv()
         if stage == 1:
-            mine = self.source[c, :, :, :, p.c]
-            self.r0[c] = mine + self.r0[c]
+            self.r0[cs] = self.source[cs, :, :, :, p.c] + self.r0[cs]
         elif stage == 2:
-            mine = self.r0[c, :, :, p.x] if x_first else self.r0[c, :, p.y]
-            self.r1[c] = mine + self.r1[c]
+            mine = self.r0[cs, :, :, p.x] if x_first else self.r0[cs, :, p.y]
+            self.r1[cs] = mine + self.r1[cs]
         elif stage == 3:
-            mine = self.r1[c, :, p.y] if x_first else self.r1[c, :, p.x]
-            self.r2[c] = mine + self.r2[c]
+            mine = self.r1[cs, :, p.y] if x_first else self.r1[cs, :, p.x]
+            self.r2[cs] = mine + self.r2[cs]
         elif stage == 4:
-            total = self.r2[c, p.z].astype(F32)
-            for k in range(p.nz - 1):
-                total = total + self.r3[c, k].astype(F32)
-            self.write(c, total)
+            for n in range(count):
+                total = self.r2[c + n, p.z].astype(F32)
+                for k in range(p.nz - 1):
+                    total = total + self.r3[c + n, k].astype(F32)
+                self.write(c + n, total)
             return
-        for copy in self.copies(stage, c, x_first):
+        for copy in self.copies(stage, c, x_first, count):
             copy.start()
 
-    def drain(self, c, x_first=False, stages=range(4)):
+    def drain(self, c, x_first=False, count=1, stages=range(4)):
         for stage in stages:
-            for copy in self.copies(stage, c, x_first):
+            for copy in self.copies(stage, c, x_first, count):
                 copy.wait_send()
 
     def short(self, c, land, sems):
@@ -499,12 +500,10 @@
 
 
 def ffn_final(
-    t, cot_ref, wo, wi, wf, prm_ref, seq_ref, y_ref, hid_ref, du_ref,
-    act_ref, dy_ref, dor_ref, datt_ref, gprm_ref,
+    t, cot_ref, wo, wi, prm_ref, seq_ref, y_ref, du_ref, dy_ref, dor_ref, datt_ref, gprm_ref
 ):
     rows = tile_at(t, FFN_TILE)
     y = y_ref[rows, :]
-    act_ref[rows, :] = (y + dot(hid_ref[rows, :], wf) + prm_ref[4:5, :]).astype(BF)
     dh = dot_bt(du_ref[rows, :], wi)
     unit, inv = centred(y)
     g = cot_ref[rows, :].astype(F32) * seq_ref[0:1, 0:1]
@@ -572,7 +571,7 @@
 
 def back_pair(
     p, factor, q_ref, k_ref, v_ref, pq_ref, pk_ref, att_ref, den_ref, datt_ref, fx_ref, low_ref,
-    ht_ref, dqkv_ref, dn_ref, e_ref, da_ref, tick, store,
+    ht_ref, dqkv_refs, dn_ref, e_ref, da_ref, tick, store,
 ):
     length = q_ref.shape[0]
     feats = fx_ref.shape[1]
@@ -608,11 +607,11 @@
             back[b - 1] = jnp.concatenate([total[:, :LANES], extra], axis=1).astype(BF)
 
         def put(value, rows, at, hh=hh):
-            where = pl.ds(pl.multiple_of((3 * p + at) * LANES, LANES), LANES)
+            ref = dqkv_refs[at]
             if hh:
                 mine = lane_ids(value.shape[0]) >= 64
-                value = jnp.where(mine, value, dqkv_ref[rows, where].astype(F32))
-            dqkv_ref[rows, where] = value.astype(BF)
+                value = jnp.where(mine, value, ref[rows, lanes].astype(F32))
+            ref[rows, lanes] = value.astype(BF)
 
         for b in range(blocks):
             base = b * BLOCK
@@ -645,12 +644,12 @@
             put(out, slice(0, length), at)
         if hh == 0:
             tick(0)
-    store(dot(ht_ref[...], dqkv_ref[:, tile_at(p, 3 * LANES)]).astype(BF))
-
-
-def input_rows(t, x_ref, wq, prm_ref, dqkv_ref, dy_ref, out_ref, gprm_ref):
+    store(dot(ht_ref[...], jnp.concatenate([ref[:, lanes] for ref in dqkv_refs], axis=1)).astype(BF))
+
+
+def input_rows(t, x_ref, wq, prm_ref, dqkv_refs, dy_ref, out_ref, gprm_ref):
     rows = tile_at(t, FFN_TILE)
-    dh = dot_bt(dqkv_ref[rows, : wq.shape[1]], wq)
+    dh = dot_bt(jnp.concatenate([ref[rows, :] for ref in dqkv_refs], axis=1), wq)
     unit, inv = centred(x_ref[rows, :].astype(F32))
     gprm_ref[0:1, :] += jnp.sum(dh * unit, axis=0, keepdims=True)
     gprm_ref[1:2, :] += jnp.sum(dh, axis=0, keepdims=True)
@@ -670,6 +669,8 @@
     ht_ref, dqkv_ref, dn_ref, e_ref, da_ref,
 ):
     gprm_ref[...] = gin_ref[...]
+    width = x_ref.shape[1]
+    dqkv_refs = [dqkv_ref.at[:, n * width : (n + 1) * width] for n in range(3)]
     flip_rows(h_ref, ht_ref)
 
     def pair(p, carry):
@@ -678,14 +679,14 @@
 
         back_pair(
             p, factor, q_ref, k_ref, v_ref, pq_ref, pk_ref, att_ref, den_ref, datt_ref, fx_ref, low_ref,
-            ht_ref, dqkv_ref, dn_ref, e_ref, da_ref, lambda j: None, store,
+            ht_ref, dqkv_refs, dn_ref, e_ref, da_ref, lambda j: None, store,
         )
         return carry
 
     lax.fori_loop(0, x_ref.shape[1] // LANES, pair, 0)
 
     def rows(t, carry):
-        input_rows(t, x_ref, wq_ref[...], prm_ref, dqkv_ref, dy_ref, out_ref, gprm_ref)
+        input_rows(t, x_ref, wq_ref[...], prm_ref, dqkv_refs, dy_ref, out_ref, gprm_ref)
         return carry
 
     lax.fori_loop(0, x_ref.shape[0] // FFN_TILE, rows, 0)
@@ -949,10 +950,8 @@
     def final(t):
         ffn_final(
             t, cot_ref, wo_ref[...].reshape(width, width), wi_ref[...].reshape(width, hidden),
-            wf_ref[...].reshape(hidden, width), prm_ref, seq_ref, y_ref, hid_ref, du_ref,
-            act_ref, dy_ref, dor_ref, y_ref, gprm_ref,
+            prm_ref, seq_ref, y_ref, du_ref, dy_ref, dor_ref, y_ref, gprm_ref,
         )
-        slab_out(t, act_ref, act_out, 0).start()
 
     loop(0, slabs, final)
     at_site("final")
@@ -974,7 +973,7 @@
     da_ref = du_ref.at[width : 2 * width, 0:BLOCK]
     dn_ref = Columns(du_ref, length, 2 * LANES)
     e_ref = Columns(du_ref, length + 4 * LANES, 2 * LANES)
-    dqkv_ref = hid_ref
+    dqkv_refs = (cot_ref, gr_ref, dor_ref)
     out_ref = h2_ref
     flip_rows(h_ref, ht_ref)
 
@@ -984,7 +983,7 @@
 
         back_pair(
             p, factor, q_ref, k_ref, v_ref, pq_ref, pk_ref, attr_ref, den_ref, y_ref, fx_ref,
-            low_ref, ht_ref, dqkv_ref, dn_ref, e_ref, da_ref, sites(p, "b"), store,
+            low_ref, ht_ref, dqkv_refs, dn_ref, e_ref, da_ref, sites(p, "b"), store,
         )
         mine.step(0, p)
         sites(p, "b")(1)
@@ -993,15 +992,30 @@
         def _():
             rest.turn()
 
+        @pl.when(p == 2)
+        def _():
+            rest_out[...] = rest.result()
+
     loop(0, pairs, back)
     last = pairs - 1
 
     def rows_back(t):
-        weights = [wq_ref[p].reshape(width, 3 * LANES) for p in range(pairs)]
+        weights = [
+            wq_ref[p, ..., n * LANES : (n + 1) * LANES].reshape(width, LANES)
+            for n in range(3)
+            for p in range(pairs)
+        ]
         input_rows(
-            t, x_ref, jnp.concatenate(weights, axis=1), prm_ref, dqkv_ref, dy_ref, out_ref, gprm_ref
+            t, x_ref, jnp.concatenate(weights, axis=1), prm_ref, dqkv_refs, dy_ref, out_ref, gprm_ref
         )
         slab_out(t, out_ref, grad_out, 1).start()
+
+    def output(t):
+        rows = tile_at(t, FFN_TILE)
+        out = x_ref[rows, :].astype(F32) + dot(attr_ref[rows, :], wo_ref[...].reshape(width, width))
+        out = out + dot(hid_ref[rows, :], wf_ref[...].reshape(hidden, width)) + prm_ref[4:5, :]
+        act_ref[rows, :] = out.astype(BF)
+        slab_out(t, act_ref, act_out, 0).start()
 
     mine.step(3, last - 2)
     mine.step(2, last - 1)
@@ -1013,8 +1027,10 @@
             first_ref[n * pairs + c : n * pairs + c + 1, :] = gprm_ref[n : n + 1, c * LANES : (c + 1) * LANES]
     first.start()
     mine.step(3, last - 1)
+    loop(0, slabs // 2, output)
     first.turn()
-    rest_out[...] = rest.result()
+    loop(slabs // 2, slabs, output)
+    at_site("tail")
     mine.step(4, last - 3)
     mine.step(4, last - 2)
     mine.step(4, last - 1)
@@ -1042,23 +1058,27 @@
     act_in, grad_in, gq_in, gf_in, gi_in, go_in, rest_in, first_in,
     act_ref, grad_ref, gq_ref, go_ref, gi_ref, gf_ref,
     g1_ref, s1_ref, g2_ref, s2_ref, bi_ref, bo_ref,
-    hold_ref, in_sem, out_sem,
+    hold_ref, holdq_ref, holdf_ref, holdi_ref, holdo_ref, in_sem, out_sem,
 ):
     moves = []
+
+    def move(src, hold, dst):
+        n = len(moves)
+        moves.append((
+            pltpu.make_async_copy(src, hold, in_sem.at[n]),
+            pltpu.make_async_copy(hold, dst, out_sem.at[n]),
+        ))
+        moves[n][0].start()
+
     for n, (src, dst) in enumerate(((act_in, act_ref), (grad_in, grad_ref))):
         for t in range(src.shape[0] // TILE):
             rows = pl.ds(t * TILE, TILE)
-            hold = hold_ref.at[n, rows]
-            moves.append((
-                pltpu.make_async_copy(src.at[rows], hold, in_sem.at[n, t]),
-                pltpu.make_async_copy(hold, dst.at[rows], out_sem.at[n, t]),
-            ))
-    for come, _ in moves:
-        come.start()
-    gq_ref[...] = gq_in[...]
-    go_ref[...] = go_in[...]
-    gi_ref[...] = gi_in[...]
-    gf_ref[...] = gf_in[...].reshape(gf_ref.shape)
+            move(src.at[rows], hold_ref.at[n, rows], dst.at[rows])
+    move(gq_in, holdq_ref, gq_ref)
+    move(gi_in, holdi_ref, gi_ref)
+    move(go_in, holdo_ref, go_ref)
+    for n in range(4):
+        move(gf_in.at[n], holdf_ref.at[n], gf_ref.at[pl.ds(16 * n, 16)])
     me = lax.axis_index("dp") * 4 + lax.axis_index("fsdp")
     row = lax.broadcasted_iota(jnp.int32, (LANES, LANES), 0)
     lane = lane_ids(LANES)
@@ -1188,7 +1208,7 @@
         functools.partial(backward_kernel, factor),
         [((length, width), BF), ((width, 3 * width), BF), ((16, width), F32)],
         backward_scratch(length, width), "backward",
-    )(tokens, h1, q, k, v, pq, pk, attr, den, datt, dy, by_pair(wq, 3), fx, prm, gprm, low)
+    )(tokens, h1, q, k, v, pq, pk, attr, den, datt, dy, wq, fx, prm, gprm, low)
     gq = by_pair(gq, width // LANES)
     grads = grads.reshape(-1, width // 16, 16, width)
     gf = grads[:4].transpose(1, 0, 2, 3).reshape(hidden, width)
@@ -1262,10 +1282,13 @@
             (big, BF), (big, BF), ((16, wide), F32), ((16, width), F32), ((16, hidden), F32),
             ((64, width), F32), *[((1, 16), F32)] * 4, ((1, 64), F32), ((1, 16), F32),
         ],
-        [((2, length, width), BF), ((2, length // TILE), None), ((2, length // TILE), None)],
+        [
+            ((2, length, width), BF), ((16, wide), F32), ((4, 16, width), F32), ((16, hidden), F32),
+            ((16, width), F32), ((2 * length // TILE + 7,), None), ((2 * length // TILE + 7,), None),
+        ],
         "finish",
-        [ANY, ANY, *[VM] * 6],
-        [ANY, ANY, *[VM] * 10],
+        [*[ANY] * 6, VM, VM],
+        [*[ANY] * 6, *[VM] * 6],
     )(act, input_grad, gq, gf, gi, go, rest, first)
     return (act, input_grad, gq, go, gi, gf, *(t[0] for t in vecs))
 

time: 120 us -> 115 us (0.958)
  Pallas kernels: 118 us -> 113 us
    pallas_call x1, Pallas kernels: 114 us -> 109 us  [ring_body(): call(functools.partial(layer_kernel, nz, factor), [(big, BF), (big, BF),...]
where the time goes in v6:
time: 115 us
  Pallas kernels  113 us (98%)
  between operations  1.46 us (1%)
    pallas_call x1, Pallas kernels, ring_body(): call(functools.partial(layer_kernel, nz, factor), [(big, BF), (big, BF),...  109 us
    pallas_call x1, Pallas kernels, ring_body(): call(finish_kernel, [(big, BF), (big, BF), ((16, wide), F32), ((16, width...  3.9 us

profile of v6, /device:TPU:0, one launch (start us, length us, event | category | flops | bytes accessed | tf_op | source)
XLA Modules:
  0.0 114.7 jit_solution(15839346615401988917)
XLA Ops:
  1.3 109.4 %layer.1 = (bf16[1024,512]{1,0:T(8,128)(2,1)}, bf16[1024,512]{1,0:T(8,128)(2,1)}, f32[16,1536]{1,0:T(8,128)}, f32[4,16,512]{2,1,0:T(8,128)}, f32[16,2048]{1,0:T(...) custom-call(bf16[1024,512]{1,0:T(8,128)(2,1)} %x_ref.1, bf16[1024,512]{1,0:T(8,128)(2,1)} %cot_in.1, ...), custom_call_target="tpu_custom_call" | custom-call | tf_op jit(solution)/shard_map/layer/pallas_call | solution.py:1242
  110.7 3.9 %finish.1 = (bf16[1024,512]{1,0:T(8,128)(2,1)}, bf16[1024,512]{1,0:T(8,128)(2,1)}, f32[16,1536]{1,0:T(8,128)}, f32[16,512]{1,0:T(8,128)}, f32[16,2048]{1,0:T(8,1...) custom-call(bf16[1024,512]{1,0:T(8,128)(2,1)} %get-tuple-element.32., ...), custom_call_target="tpu_custom_call" | custom-call | tf_op jit(solution)/shard_map/finish/pallas_call | solution.py:1279

commit v7 on v6

--- a/solution.py
+++ b/solution.py
@@ -85,9 +85,9 @@
     "grad2": ((6, 0),),
     "chunk3": ((6, 1), (5, 2), (4, 3)),
     "grad3": ((7, 0), (0, 0), (1, 0), (2, 0), (3, 0)),
-    "final": ((7, 1), (0, 1), (1, 1), (6, 2), (5, 3)),
-    "grad_o": ((8, 0),),
-    "b0:0": ((2, 1), (3, 1), (8, 1)),
+    "final": ((7, 1), (0, 1), (6, 2), (5, 3)),
+    "grad_o": ((8, 0), (1, 1), (2, 1)),
+    "b0:0": ((3, 1), (8, 1)),
     "b0:1": ((7, 2), (0, 2), (1, 2), (6, 3)),
     "b1:0": ((2, 2), (3, 2), (8, 2)),
     "b1:1": ((7, 3), (0, 3), (1, 3)),
@@ -100,23 +100,23 @@
     "b3:0": ((0, 3), (1, 2), (2, 1)),
 }
 PLAN = {
-    "start": (("s", 1), ("q0", 1), ("q1", 1), ("q2", 1), ("s", 2), ("q3", 1), ("q0", 2), ("o", 1), ("q1", 2), ("i0", 1), ("s", 3), ("q2", 2), ("q3", 2), ("o", 2), ("q0", 3), ("i0", 2),),
-    "params": (("q1", 3), ("f0", 1), ("f1", 1), ("f2", 1), ("f3", 1),),
-    "0:0": (("q2", 3), ("q3", 3), ("i1", 1),),
-    "0:1": (("i2", 1),),
-    "0:2": (("o", 3), ("i3", 1),),
-    "1:0": (("i0", 3), ("f0", 2),),
-    "1:1": (("f1", 2),),
-    "1:2": (("i1", 2), ("f2", 2),),
-    "2:0": (("i2", 2),),
-    "2:1": (("i3", 2), ("f3", 2),),
-    "3:0": (("f0", 3),),
-    "3:1": (("f1", 3),),
-    "norm": (("i1", 3), ("f2", 3),),
-    "chunk0": (("i2", 3), ("f3", 3),),
-    "grad0": (("i3", 3),),
+    "start": (("s", 1), ("q0", 1), ("q1", 1), ("q2", 1), ("s", 2), ("q3", 1), ("q0", 2), ("o", 1), ("q1", 2), ("s", 3), ("i0", 1), ("q2", 2), ("q3", 2), ("q0", 3), ("q1", 3), ("o", 2),),
+    "rows": (("f3", 1), ("i0", 2), ("f0", 1), ("f1", 1), ("f2", 1),),
+    "0:0": (("q2", 3), ("i1", 1),),
+    "0:2": (("q3", 3), ("i2", 1),),
+    "1:0": (("f3", 2), ("o", 3), ("i3", 1),),
+    "1:1": (("f0", 2),),
+    "1:2": (("i0", 3), ("f1", 2),),
+    "2:1": (("i1", 2), ("f2", 2),),
+    "2:2": (("i2", 2),),
+    "3:1": (("f0", 3),),
+    "3:2": (("f3", 3),),
+    "norm": (("f1", 3), ("i3", 2),),
+    "chunk0": (("i1", 3), ("f2", 3),),
+    "grad0": (("i2", 3),),
+    "chunk1": (("i3", 3),),
 }
-Y_FIRST = {"s", "q1", "q2", "i0", "i1", "i2", "i3", "f0"}
+Y_FIRST = {"q1", "o", "f2", "f3"}
 LEAVE = ("s", "q0", "q1", "q2", "q3", "o", "i0", "F", "i1", "i2", "i3")
 
 
@@ -161,11 +161,14 @@
             yield self.device(z=self.up(k))
             yield self.device(z=self.up(k), y=1 - self.y)
 
-    def barrier(self):
-        sem = pltpu.get_barrier_semaphore()
+    def greet(self):
         for peer in self.peers():
-            pl.semaphore_signal(sem, inc=1, device_id=peer, device_id_type=MESH_ID)
-        pl.semaphore_wait(sem, 1 + 4 * self.nz)
+            pl.semaphore_signal(
+                pltpu.get_barrier_semaphore(), inc=1, device_id=peer, device_id_type=MESH_ID
+            )
+
+    def all_here(self):
+        pl.semaphore_wait(pltpu.get_barrier_semaphore(), 1 + 4 * self.nz)
 
 
 def remote(src, dst, send, recv, peer):
@@ -517,19 +520,12 @@
     datt_ref[rows, :] = dot_bt(dor, wo)
 
 
-def put_rows(g_ref, chunk, c, value):
-    if len(g_ref.shape) == 5:
-        g_ref[chunk, c] = value
-    else:
-        g_ref[chunk, lax.div(c, 2), lax.rem(c, 2)] = value.reshape(2, 2, *value.shape[1:])
-
-
 def grads_out(c, hid_ref, gr_ref, g_ref):
     width = gr_ref.shape[1]
     grad = dot_at(hid_ref[:, tile_at(c)], gr_ref[...]).astype(BF)
     grad = grad.reshape(4, 4, 16, width)
     for q in range(4):
-        put_rows(g_ref, q, c, grad[:, q])
+        g_ref[q, c] = grad[:, q]
 
 
 def grads_in(c, h_ref, du_ref, attr_ref, dor_ref, g_ref):
@@ -848,6 +844,7 @@
 
         return site
 
+    place.greet()
     vec_ref[...] = jnp.zeros_like(vec_ref)
     for n, ref in enumerate((g1_ref, s1_ref, g2_ref, s2_ref, bo_ref)):
         vec_ref[n : n + 1, : ref.shape[1]] = ref[...].astype(F32)
@@ -859,7 +856,7 @@
         for n in range(3):
             at = n * width + p * LANES
             wqt_ref[p, :, n * LANES : (n + 1) * LANES] = wqs_ref[:, at : at + LANES]
-    place.barrier()
+    place.all_here()
     for who in LEAVE:
         named[who].start()
     cot_copy.start()
@@ -938,13 +935,11 @@
 
         loop(0, slabs, chunk)
         at_site(f"chunk{c}")
-        loop(2 * c, 2 * c + 2, lambda n: grads_out(n, hid_ref, gr_ref, g_ref))
-
-        def grad(n, c=c, cs=cs):
-            value = dot_at(h2_ref[:, tile_at(n)], du_ref[:, cs]).astype(BF)
-            g_ref[4 + c, pl.ds(n * 2, 2)] = value.reshape(2, 2, 2, 2, 16, width)
-
-        loop(0, width // TILE, grad)
+        value = dot_at(hid_ref[:, cs], gr_ref[...]).astype(BF).reshape(8, 4, 16, width)
+        for q in range(4):
+            g_ref[q, c] = value[:, q].reshape(2, 2, 2, 16, width)
+        value = dot_at(h2_ref[...], du_ref[:, cs]).astype(BF)
+        g_ref[4 + c] = value.reshape(*grid, 16, width)
         at_site(f"grad{c}")
 
     def final(t):
@@ -956,11 +951,8 @@
     loop(0, slabs, final)
     at_site("final")
 
-    def grad_o(n):
-        value = dot_at(attr_ref[:, tile_at(n)], dor_ref[...]).astype(BF)
-        g_ref[4 + parts, pl.ds(n * 2, 2)] = value.reshape(2, 2, 2, 2, 16, width)
-
-    loop(0, width // TILE, grad_o)
+    value = dot_at(attr_ref[...], dor_ref[...]).astype(BF)
+    g_ref[4 + parts] = value.reshape(*grid, 16, width)
     at_site("grad_o")
     for n in range(3 + parts):
         for c in range(pairs):

time: 115 us -> 112 us (0.974)
  Pallas kernels: 113 us -> 110 us
    pallas_call x1, Pallas kernels: 109 us -> 107 us  [ring_body(): call(functools.partial(layer_kernel, nz, factor), [(big, BF), (big, BF),...]
where the time goes in v7:
time: 112 us
  Pallas kernels  110 us (98%)
  between operations  1.46 us (1%)
    pallas_call x1, Pallas kernels, ring_body(): call(functools.partial(layer_kernel, nz, factor), [(big, BF), (big, BF),...  107 us
    pallas_call x1, Pallas kernels, ring_body(): call(finish_kernel, [(big, BF), (big, BF), ((16, wide), F32), ((16, width...  3.9 us

profile of v7, /device:TPU:0, one launch (start us, length us, event | category | flops | bytes accessed | tf_op | source)
XLA Modules:
  0.0 111.9 jit_solution(12423067188911272665)
XLA Ops:
  1.3 106.6 %layer.1 = (bf16[1024,512]{1,0:T(8,128)(2,1)}, bf16[1024,512]{1,0:T(8,128)(2,1)}, f32[16,1536]{1,0:T(8,128)}, f32[4,16,512]{2,1,0:T(8,128)}, f32[16,2048]{1,0:T(...) custom-call(bf16[1024,512]{1,0:T(8,128)(2,1)} %x_ref.1, bf16[1024,512]{1,0:T(8,128)(2,1)} %cot_in.1, ...), custom_call_target="tpu_custom_call" | custom-call | tf_op jit(solution)/shard_map/layer/pallas_call | solution.py:1234
  107.9 3.9 %finish.1 = (bf16[1024,512]{1,0:T(8,128)(2,1)}, bf16[1024,512]{1,0:T(8,128)(2,1)}, f32[16,1536]{1,0:T(8,128)}, f32[16,512]{1,0:T(8,128)}, f32[16,2048]{1,0:T(8,1...) custom-call(bf16[1024,512]{1,0:T(8,128)(2,1)} %get-tuple-element.32., ...), custom_call_target="tpu_custom_call" | custom-call | tf_op jit(solution)/shard_map/finish/pallas_call | solution.py:1271

commit v8 on v7

--- a/solution.py
+++ b/solution.py
@@ -1009,8 +1009,6 @@
         act_ref[rows, :] = out.astype(BF)
         slab_out(t, act_ref, act_out, 0).start()
 
-    mine.step(3, last - 2)
-    mine.step(2, last - 1)
     loop(0, slabs // 2, rows_back)
     mine.short_start(last, land_ref, short_sems)
     loop(slabs // 2, slabs, rows_back)
@@ -1018,9 +1016,11 @@
         for c in range(pairs):
             first_ref[n * pairs + c : n * pairs + c + 1, :] = gprm_ref[n : n + 1, c * LANES : (c + 1) * LANES]
     first.start()
-    mine.step(3, last - 1)
+    mine.step(3, last - 2)
+    mine.step(2, last - 1)
     loop(0, slabs // 2, output)
     first.turn()
+    mine.step(3, last - 1)
     loop(slabs // 2, slabs, output)
     at_site("tail")
     mine.step(4, last - 3)

time: 112 us -> 112 us (level)
  no operation moved by 1% of the time
where the time goes in v8:
time: 112 us; the launch traced here: 111 us
  Pallas kernels  110 us (98%)
  between operations  1.46 us (1%)
    pallas_call x1, Pallas kernels, ring_body(): call(functools.partial(layer_kernel, nz, factor), [(big, BF), (big, BF),...  106 us
    pallas_call x1, Pallas kernels, ring_body(): call(finish_kernel, [(big, BF), (big, BF), ((16, wide), F32), ((16, width...  3.9 us

profile of v8, /device:TPU:0, one launch (start us, length us, event | category | flops | bytes accessed | tf_op | source)
XLA Modules:
  0.0 111.4 jit_solution(18016347870974125459)
XLA Ops:
  1.3 106.0 %layer.1 = (bf16[1024,512]{1,0:T(8,128)(2,1)}, bf16[1024,512]{1,0:T(8,128)(2,1)}, f32[16,1536]{1,0:T(8,128)}, f32[4,16,512]{2,1,0:T(8,128)}, f32[16,2048]{1,0:T(...) custom-call(bf16[1024,512]{1,0:T(8,128)(2,1)} %x_ref.1, bf16[1024,512]{1,0:T(8,128)(2,1)} %cot_in.1, ...), custom_call_target="tpu_custom_call" | custom-call | tf_op jit(solution)/shard_map/layer/pallas_call | solution.py:1234
  107.3 3.9 %finish.1 = (bf16[1024,512]{1,0:T(8,128)(2,1)}, bf16[1024,512]{1,0:T(8,128)(2,1)}, f32[16,1536]{1,0:T(8,128)}, f32[16,512]{1,0:T(8,128)}, f32[16,2048]{1,0:T(8,1...) custom-call(bf16[1024,512]{1,0:T(8,128)(2,1)} %get-tuple-element.32., ...), custom_call_target="tpu_custom_call" | custom-call | tf_op jit(solution)/shard_map/finish/pallas_call | solution.py:1271
